TPU v7x, 32 devices: a whole 2x2x4 slice. The times are simulated.
32 devices in a mesh: rep: 4 (over y, x), shard: 8 (over z, core).
Axes of the slice: x: 2, y: 2, z: 4, core: 2. Of those that a mesh axis runs over, the one named last changes fastest.
Arguments:
- tokens: bfloat16 [20480, 768], P(('rep', 'shard')), may hold values from -6 to 6
- ln1_gain: bfloat16 [768], P('shard'), may hold values from 0.5 to 1.5
- ln1_bias: bfloat16 [768], P('shard'), may hold values from -1.5 to 1.5
- w_qkv: bfloat16 [768, 2304], P('shard'), may hold values from -0.21875 to 0.21875
- qv_bias: bfloat16 [1536], P('shard'), may hold values from -1.5 to 1.5
- w_out: bfloat16 [768, 768], P('shard'), may hold values from -1.75 to 1.75
- out_bias: bfloat16 [768], P('shard'), may hold values from -1.5 to 1.5
- ln2_gain: bfloat16 [768], P('shard'), may hold values from 0.5 to 1.5
- ln2_bias: bfloat16 [768], P('shard'), may hold values from -1.5 to 1.5
- w_fc: bfloat16 [768, 3072], P('shard'), may hold values from -0.21875 to 0.21875
- fc_bias: bfloat16 [3072], P('shard'), may hold values from -1.5 to 1.5
- w_proj: bfloat16 [3072, 768], P('shard'), may hold values from -0.109375 to 0.109375
- proj_bias: bfloat16 [768], P('shard'), may hold values from -1.5 to 1.5
- teacher: bfloat16 [20480, 768], P(('rep', 'shard')), may hold values from -6 to 6
- cotangent: bfloat16 [20480, 768], P(('rep', 'shard')), may hold values from -12 to 12
- valid_mask: int32 [20480], P(('rep', 'shard')), may hold values from 0 to 1, as said below
Outputs:
- block_out: bfloat16 [20480, 768], P(('rep', 'shard'))
- input_grad: float32 [20480, 768], P(('rep', 'shard'))
- grad_ln1_gain: float32 [768], P('shard')
- grad_ln1_bias: float32 [768], P('shard')
- grad_w_qkv: float32 [768, 2304], P('shard')
- grad_qv_bias: float32 [1536], P('shard')
- grad_w_out: float32 [768, 768], P('shard')
- grad_out_bias: float32 [768], P('shard')
- grad_ln2_gain: float32 [768], P('shard')
- grad_ln2_bias: float32 [768], P('shard')
- grad_w_fc: float32 [768, 3072], P('shard')
- grad_fc_bias: float32 [3072], P('shard')
- grad_w_proj: float32 [3072, 768], P('shard')
- grad_proj_bias: float32 [768], P('shard')
Inputs may be any that keep to these rules, and one draw needn't show every extreme that they name: `valid_mask`: the first of each device's 640 rows is 1.
All inputs are finite; a program needn't handle non-finite values.
Results may differ from a plain program's by a relative error of at most 0.012.
Values may be sent and summed in bfloat16 or wider, within the bound.
No kernel may reach another device: no remote copies, remote signals or barrier semaphores. Data moves between devices by JAX's collectives and lax.ppermute only.
A program may use at most 256 MiB of HBM per device.

v0:
```python
import jax
import jax.numpy as jnp
from jax import lax
from jax.sharding import PartitionSpec as P

HEAD = 64
PR_DEV = 128


def layer_norm(values, gain_vec, bias_vec):
    centered = values - jnp.mean(values, axis=-1, keepdims=True)
    variance = jnp.mean(centered * centered, axis=-1, keepdims=True)
    return centered * lax.rsqrt(variance + 1e-05) * gain_vec + bias_vec


def gelu_tanh(values):
    return (
        0.5
        * values
        * (1.0 + jnp.tanh(0.7978845608028654 * (values + 0.044715 * values * values * values)))
    )


def column_sums(matrix):
    return jnp.sum(matrix.astype(jnp.float32), axis=0)


def local(
    tokens,
    ln1_gain,
    ln1_bias,
    w_qkv,
    qv_bias,
    w_out,
    out_bias,
    ln2_gain,
    ln2_bias,
    w_fc,
    fc_bias,
    w_proj,
    proj_bias,
    teacher,
    cotangent,
    valid_mask,
):
    gathered = (
        lax.all_gather(ln1_gain, "shard", axis=0, tiled=True),
        lax.all_gather(ln1_bias, "shard", axis=0, tiled=True),
        lax.all_gather(w_qkv, "shard", axis=0, tiled=True),
        lax.all_gather(qv_bias, "shard", axis=0, tiled=True),
        lax.all_gather(w_out, "shard", axis=0, tiled=True),
        lax.all_gather(out_bias, "shard", axis=0, tiled=True),
        lax.all_gather(ln2_gain, "shard", axis=0, tiled=True),
        lax.all_gather(ln2_bias, "shard", axis=0, tiled=True),
        lax.all_gather(w_fc, "shard", axis=0, tiled=True),
        lax.all_gather(fc_bias, "shard", axis=0, tiled=True),
        lax.all_gather(w_proj, "shard", axis=0, tiled=True),
        lax.all_gather(proj_bias, "shard", axis=0, tiled=True),
    )
    (
        gain_one,
        bias_one,
        full_qkv,
        full_qv,
        full_out,
        full_ob,
        gain_two,
        bias_two,
        full_fc,
        full_fb,
        full_proj,
        full_pb,
    ) = gathered
    mask_f = valid_mask.astype(jnp.float32)
    token_total = lax.psum(jnp.sum(mask_f), ("rep", "shard"))
    tok_rows = tokens.shape[0]
    feat_width = tokens.shape[1]
    inputs = tokens.astype(jnp.float32)
    normed_one, norm_one_back = jax.vjp(
        layer_norm, inputs, gain_one.astype(jnp.float32), bias_one.astype(jnp.float32)
    )
    act_one = normed_one.astype(jnp.bfloat16)
    qv_float = full_qv.astype(jnp.float32)
    bias_row = jnp.concatenate(
        [qv_float[:feat_width], jnp.zeros((feat_width,), jnp.float32), qv_float[feat_width:]]
    )
    proj_qkv = (jnp.dot(act_one, full_qkv, preferred_element_type=jnp.float32) + bias_row).astype(
        jnp.bfloat16
    )
    queries = proj_qkv[:, :feat_width]
    keys_local = proj_qkv[:, feat_width : 2 * feat_width]
    values_local = proj_qkv[:, 2 * feat_width :]
    prompt_keys, prompt_values = (
        lax.all_gather(keys_local[:PR_DEV], "shard", axis=0, tiled=True),
        lax.all_gather(values_local[:PR_DEV], "shard", axis=0, tiled=True),
    )
    prompt_len = prompt_keys.shape[0]
    all_keys = jnp.concatenate([prompt_keys, keys_local[PR_DEV:]], axis=0)
    all_values = jnp.concatenate([prompt_values, values_local[PR_DEV:]], axis=0)
    key_count = all_keys.shape[0]
    shard_pos = lax.axis_index("shard")
    row_ids = jnp.arange(tok_rows, dtype=jnp.int32)[:, None]
    key_ids = jnp.arange(key_count, dtype=jnp.int32)[None, :]
    in_prompt = key_ids < prompt_len
    prompt_ok = in_prompt & (key_ids <= shard_pos * PR_DEV + row_ids)
    cont_ok = in_prompt | (key_ids - prompt_len <= row_ids - PR_DEV)
    allowed = jnp.where(row_ids < PR_DEV, prompt_ok, cont_ok)
    span = 2 * HEAD
    pair_count = feat_width // span

    def columns(matrix, index):
        return lax.dynamic_slice_in_dim(matrix, index * span, span, 1)

    def pair_scores(query_cols, key_cols):
        query_three = query_cols.reshape(tok_rows, 2, HEAD)
        key_three = key_cols.reshape(key_count, 2, HEAD)
        raw_scores = (
            jnp.einsum("qhd,khd->hqk", query_three, key_three, preferred_element_type=jnp.float32)
            * 0.125
        )
        return jnp.where(allowed[None], raw_scores, jnp.float32(-1e30))

    def attend_pair(index):
        scores = pair_scores(columns(queries, index), columns(all_keys, index))
        row_max = jnp.max(scores, axis=-1, keepdims=True)
        expo = jnp.exp(scores - row_max)
        row_total = jnp.sum(expo, axis=-1, keepdims=True)
        probs = expo / row_total
        log_total = row_max[..., 0] + jnp.log(row_total[..., 0])
        value_three = columns(all_values, index).reshape(key_count, 2, HEAD)
        mixed = jnp.einsum(
            "hqk,khd->qhd",
            probs.astype(jnp.bfloat16),
            value_three,
            preferred_element_type=jnp.float32,
        )
        return (mixed.reshape(tok_rows, span).astype(jnp.bfloat16), log_total)

    pair_out, pair_lse = lax.map(attend_pair, jnp.arange(pair_count, dtype=jnp.int32))
    attn_mix = jnp.transpose(pair_out, (1, 0, 2)).reshape(tok_rows, feat_width)
    resid_one = (
        inputs
        + jnp.dot(attn_mix, full_out, preferred_element_type=jnp.float32)
        + full_ob.astype(jnp.float32)
    )
    normed_two, norm_two_back = jax.vjp(
        layer_norm, resid_one, gain_two.astype(jnp.float32), bias_two.astype(jnp.float32)
    )
    act_two = normed_two.astype(jnp.bfloat16)
    hidden_pre = jnp.dot(act_two, full_fc, preferred_element_type=jnp.float32) + full_fb.astype(
        jnp.float32
    )
    hidden_act, gelu_back = jax.vjp(gelu_tanh, hidden_pre)
    hidden_low = hidden_act.astype(jnp.bfloat16)
    output = (
        resid_one
        + jnp.dot(hidden_low, full_proj, preferred_element_type=jnp.float32)
        + full_pb.astype(jnp.float32)
    )
    device_count = lax.axis_size("rep") * lax.axis_size("shard")
    factor = tok_rows * device_count / token_total
    grad_output = cotangent.astype(jnp.float32) + factor * mask_f[:, None] * (
        output - teacher.astype(jnp.float32)
    )
    grad_branch = grad_output.astype(jnp.bfloat16)
    grad_pb = column_sums(grad_branch)
    grad_proj = jnp.einsum("tf,td->fd", hidden_low, grad_branch, preferred_element_type=jnp.float32)
    grad_hidden = jnp.einsum(
        "td,fd->tf", grad_branch, full_proj, preferred_element_type=jnp.float32
    )
    (grad_pre,) = gelu_back(grad_hidden)
    grad_pre_low = grad_pre.astype(jnp.bfloat16)
    grad_fb = column_sums(grad_pre_low)
    grad_fc = jnp.einsum("td,tf->df", act_two, grad_pre_low, preferred_element_type=jnp.float32)
    grad_act_two = jnp.einsum(
        "tf,df->td", grad_pre_low, full_fc, preferred_element_type=jnp.float32
    )
    grad_resid_part, grad_gain_two, grad_bias_two = norm_two_back(grad_act_two)
    grad_resid = grad_output + grad_resid_part
    grad_attn = grad_resid.astype(jnp.bfloat16)
    grad_ob = column_sums(grad_attn)
    grad_wo = jnp.einsum("te,td->ed", attn_mix, grad_attn, preferred_element_type=jnp.float32)
    grad_mix = jnp.einsum(
        "td,ed->te", grad_attn, full_out, preferred_element_type=jnp.float32
    ).astype(jnp.bfloat16)

    def pair_back(operands):
        index, log_total = operands
        query_cols = columns(queries, index)
        key_cols = columns(all_keys, index)
        scores = pair_scores(query_cols, key_cols)
        probs = jnp.exp(scores - log_total[:, :, None])
        grad_three = columns(grad_mix, index).reshape(tok_rows, 2, HEAD)
        value_three = columns(all_values, index).reshape(key_count, 2, HEAD)
        grad_probs = jnp.einsum(
            "qhd,khd->hqk", grad_three, value_three, preferred_element_type=jnp.float32
        )
        row_dot = jnp.sum(probs * grad_probs, axis=-1, keepdims=True)
        grad_scores = (probs * (grad_probs - row_dot)).astype(jnp.bfloat16)
        grad_query = (
            jnp.einsum(
                "hqk,khd->qhd",
                grad_scores,
                key_cols.reshape(key_count, 2, HEAD),
                preferred_element_type=jnp.float32,
            )
            * 0.125
        )
        grad_key = (
            jnp.einsum(
                "hqk,qhd->khd",
                grad_scores,
                query_cols.reshape(tok_rows, 2, HEAD),
                preferred_element_type=jnp.float32,
            )
            * 0.125
        )
        grad_value = jnp.einsum(
            "hqk,qhd->khd",
            probs.astype(jnp.bfloat16),
            grad_three,
            preferred_element_type=jnp.float32,
        )
        return (
            grad_query.reshape(tok_rows, span),
            grad_key.reshape(key_count, span),
            grad_value.reshape(key_count, span),
        )

    pair_gq, pair_gk, pair_gv = lax.map(
        pair_back, (jnp.arange(pair_count, dtype=jnp.int32), pair_lse)
    )
    grad_queries = jnp.transpose(pair_gq, (1, 0, 2)).reshape(tok_rows, feat_width)
    grad_keys_all = jnp.transpose(pair_gk, (1, 0, 2)).reshape(key_count, feat_width)
    grad_values_all = jnp.transpose(pair_gv, (1, 0, 2)).reshape(key_count, feat_width)
    grad_prompt_keys, grad_prompt_values = (
        lax.psum_scatter(grad_keys_all[:prompt_len], "shard", scatter_dimension=0, tiled=True),
        lax.psum_scatter(grad_values_all[:prompt_len], "shard", scatter_dimension=0, tiled=True),
    )
    grad_keys = jnp.concatenate([grad_prompt_keys, grad_keys_all[prompt_len:]], axis=0)
    grad_values = jnp.concatenate([grad_prompt_values, grad_values_all[prompt_len:]], axis=0)
    grad_qkv = jnp.concatenate([grad_queries, grad_keys, grad_values], axis=1).astype(jnp.bfloat16)
    grad_qv = jnp.concatenate(
        [column_sums(grad_qkv[:, :feat_width]), column_sums(grad_qkv[:, 2 * feat_width :])]
    )
    grad_wqkv = jnp.einsum("td,te->de", act_one, grad_qkv, preferred_element_type=jnp.float32)
    grad_act_one = jnp.einsum("te,de->td", grad_qkv, full_qkv, preferred_element_type=jnp.float32)
    grad_input_part, grad_gain_one, grad_bias_one = norm_one_back(grad_act_one)
    input_grad = grad_resid + grad_input_part
    owned = (
        lax.psum_scatter(
            grad_gain_one.astype(jnp.bfloat16), "shard", scatter_dimension=0, tiled=True
        ).astype(jnp.float32),
        lax.psum_scatter(
            grad_bias_one.astype(jnp.bfloat16), "shard", scatter_dimension=0, tiled=True
        ).astype(jnp.float32),
        lax.psum_scatter(
            grad_wqkv.astype(jnp.bfloat16), "shard", scatter_dimension=0, tiled=True
        ).astype(jnp.float32),
        lax.psum_scatter(
            grad_qv.astype(jnp.bfloat16), "shard", scatter_dimension=0, tiled=True
        ).astype(jnp.float32),
        lax.psum_scatter(
            grad_wo.astype(jnp.bfloat16), "shard", scatter_dimension=0, tiled=True
        ).astype(jnp.float32),
        lax.psum_scatter(
            grad_ob.astype(jnp.bfloat16), "shard", scatter_dimension=0, tiled=True
        ).astype(jnp.float32),
        lax.psum_scatter(
            grad_gain_two.astype(jnp.bfloat16), "shard", scatter_dimension=0, tiled=True
        ).astype(jnp.float32),
        lax.psum_scatter(
            grad_bias_two.astype(jnp.bfloat16), "shard", scatter_dimension=0, tiled=True
        ).astype(jnp.float32),
        lax.psum_scatter(
            grad_fc.astype(jnp.bfloat16), "shard", scatter_dimension=0, tiled=True
        ).astype(jnp.float32),
        lax.psum_scatter(
            grad_fb.astype(jnp.bfloat16), "shard", scatter_dimension=0, tiled=True
        ).astype(jnp.float32),
        lax.psum_scatter(
            grad_proj.astype(jnp.bfloat16), "shard", scatter_dimension=0, tiled=True
        ).astype(jnp.float32),
        lax.psum_scatter(
            grad_pb.astype(jnp.bfloat16), "shard", scatter_dimension=0, tiled=True
        ).astype(jnp.float32),
    )
    summed = (
        lax.psum(owned[0].astype(jnp.bfloat16), "rep").astype(jnp.float32),
        lax.psum(owned[1].astype(jnp.bfloat16), "rep").astype(jnp.float32),
        lax.psum(owned[2].astype(jnp.bfloat16), "rep").astype(jnp.float32),
        lax.psum(owned[3].astype(jnp.bfloat16), "rep").astype(jnp.float32),
        lax.psum(owned[4].astype(jnp.bfloat16), "rep").astype(jnp.float32),
        lax.psum(owned[5].astype(jnp.bfloat16), "rep").astype(jnp.float32),
        lax.psum(owned[6].astype(jnp.bfloat16), "rep").astype(jnp.float32),
        lax.psum(owned[7].astype(jnp.bfloat16), "rep").astype(jnp.float32),
        lax.psum(owned[8].astype(jnp.bfloat16), "rep").astype(jnp.float32),
        lax.psum(owned[9].astype(jnp.bfloat16), "rep").astype(jnp.float32),
        lax.psum(owned[10].astype(jnp.bfloat16), "rep").astype(jnp.float32),
        lax.psum(owned[11].astype(jnp.bfloat16), "rep").astype(jnp.float32),
    )
    return (
        output.astype(jnp.bfloat16),
        input_grad,
        summed[0],
        summed[1],
        summed[2],
        summed[3],
        summed[4],
        summed[5],
        summed[6],
        summed[7],
        summed[8],
        summed[9],
        summed[10],
        summed[11],
    )


def solution(mesh):
    return jax.shard_map(
        local,
        mesh=mesh,
        in_specs=(
            P(("rep", "shard"), None),
            P("shard"),
            P("shard"),
            P("shard", None),
            P("shard"),
            P("shard", None),
            P("shard"),
            P("shard"),
            P("shard"),
            P("shard", None),
            P("shard"),
            P("shard", None),
            P("shard"),
            P(("rep", "shard"), None),
            P(("rep", "shard"), None),
            P(("rep", "shard")),
        ),
        out_specs=(
            P(("rep", "shard"), None),
            P(("rep", "shard"), None),
            P("shard"),
            P("shard"),
            P("shard", None),
            P("shard"),
            P("shard", None),
            P("shard"),
            P("shard"),
            P("shard"),
            P("shard", None),
            P("shard"),
            P("shard", None),
            P("shard"),
        ),
        check_vma=False,
    )
```

profile of v0, /device:TPU:16, one launch (start us, length us, event | category | flops | bytes accessed | tf_op | source)
XLA Modules:
  0.0 803.7 jit_solution(6407339874634745417)
XLA Ops:
  16.5 26.6 %all-reduce.16 = (bf16[1536]{0:T(1024)(128)(2,1)S(1)}, bf16[768]{0:T(1024)(128)(2,1)S(1)}, bf16[768]{0:T(1024)(128)(2,1)S(1)}, bf16[768]{0:T(1024)(128)(2,1)S(1)...) all-reduce(bf16[1536]{0:T(1024)(128)(2,1)S(1)} %dynamic-update-slic, ...), channel_id=1, replica_groups=mesh['rep'=4,'shard'=8] {'shard'}, use_global_device_ids=true, to_apply=%add.2 | all-reduce | flops 6144 | bytes 24576
  46.8 4.8 all-gather.8.cloned.1.call-done
  51.6 5.0 add_convert_fusion
  62.2 39.9 %psum.91 = f32[]{:T(128)} all-reduce(f32[]{:T(128)} %convert_reduce_fusion.1), channel_id=1, replica_groups=mesh['rep'=4,'shard'=8] {'rep','shard'}, use_global_device_ids=true, to_apply=%region_9.10 | all-reduce | flops 1 | bytes 8 | tf_op jit(solution)/shard_map/psum | solution.py:75
  102.8 12.8 %all-gather = bf16[8,1,384]{2,1,0:T(2,128)(2,1)S(1)} all-gather(bf16[1,1,384]{2,1,0:T(2,128)(2,1)S(1)} %reshape.231), channel_id=1, replica_groups=mesh['rep'=4,'shard'=8] {'shard'}, dimensions={0}, use_global_device_ids=true | all-gather | bytes 6912 | tf_op jit(solution)/shard_map/all_gather | solution.py:56
  128.6 4.3 copy.37
  132.9 77.5 %while.28 = (s32[]{:T(128)}, bf16[6,640,128]{1,2,0:T(8,128)(2,1)}, f32[6,2,640]{2,1,0:T(2,128)}, s32[6]{0:T(128)S(1)}, bf16[1536,768]{0,1:T(8,128)(2,1)}, /*inde...) while((s32[]{:T(128)}, bf16[6,640,128]{1,2,0:T(8,128)(2,1)}, ...), condition=%wide.region_5.6_spmd.clone, body=%wide.region_2.5_spmd.clone.sunk | while | flops 531905280 | bytes 30922088 | solution.py:139
  214.8 9.3 %fusion.46 = f32[640,3072]{1,0:T(8,128)} fusion(bf16[768,3072]{1,0:T(8,128)(2,1)} %all-gather.16.cloned.1.call-done, f32[640,768]{1,0:T(8,128)} %copy-done.11, f32[768]{0:T(1024)S(1)} %convert_element_type.194, f32[768]{0:T(1024)S(1)} %convert_element_type.193, f32[640]{0:T(1024)S(1)} %fusion.36, f32[640]{0:T(1024)S(1)} %broadcast_multiply_fusion), kind=kOutput, calls=%fused_computation.112 | convolution fusion | flops 3022356480 | bytes 14560256 | tf_op jit(solution)/shard_map/dot_general | solution.py:150
  224.1 13.3 %all-gather.18.cloned.1.call-done = bf16[3072,768]{1,0:T(8,128)(2,1)} async-done(((bf16[384,768]{1,0:T(8,128)(2,1)}), bf16[3072,768]{1,0:T(8,128)(2,1)}) %all-gather.18.cloned.1.call-update) | async-done | bytes 4718608 | tf_op jit(solution)/shard_map/all_gather | solution.py:57
  237.5 11.2 %fusion.58 = (bf16[640,768]{1,0:T(8,128)(2,1)}, f32[640,768]{1,0:T(8,128)S(1)}) fusion(f32[768]{0:T(1024)S(1)} %convert_element_type.198, f32[640,768]{1,0:T(8,128)} %copy-done.11, bf16[3072,768]{1,0:T(8,128)(2,1)} %all-gather.18.cloned.1.call-done, f32[640,3072]{1,0:T(8,128)} %fusion.46, f32[3072]{0:T(1024)S(1)} %bitcast.151), kind=kOutput, calls=%fused_computation.123 | convolution fusion | flops 3041034240 | bytes 17513472 | tf_op jit(solution)/shard_map/dot_general | solution.py:157
  251.7 10.2 %fusion.59 = (bf16[3072]{0:T(1024)(128)(2,1)}, bf16[640,3072]{1,0:T(8,128)(2,1)S(1)}) fusion(bf16[3072,768]{1,0:T(8,128)(2,1)S(1)} %copy-done.41, f32[640,768]{1,0:T(8,128)S(1)} %get-tuple-element.332, f32[640,3072]{1,0:T(8,128)S(1)} %copy-done.45, f32[3072]{0:T(1024)S(1)} %bitcast.152), kind=kOutput, calls=%fused_computation.124 | convolution fusion | flops 3071505408 | bytes 18499584 | tf_op jit(solution)/shard_map/td,fd->tf/dot_general | solution.py:168
  262.0 4.2 multiply_reduce_fusion.1
  271.0 175.9 %while.29 = (s32[]{:T(128)}, bf16[6,640,128]{1,2,0:T(8,128)(2,1)}, f32[6,1536,128]{1,2,0:T(8,128)}, f32[6,1536,128]{1,2,0:T(8,128)}, s32[6]{0:T(128)S(1)}, /*ind...) while((s32[]{:T(128)}, bf16[6,640,128]{1,2,0:T(8,128)(2,1)}, ...), condition=%wide.region_14.15_spmd.clone, body=%wide.region_12.14_spmd.clone.sunk | while | flops 1281260288 | bytes 106502936 | solution.py:230
  280.6 5.0 multiply_reduce_fusion.5
  285.6 6.1 multiply_convert_fusion.5
  291.8 4.3 fusion.126
  309.9 5.0 multiply_reduce_fusion.5
  315.0 6.1 multiply_convert_fusion.5
  321.1 4.3 fusion.126
  339.2 5.0 multiply_reduce_fusion.5
  344.2 6.1 multiply_convert_fusion.5
  350.4 4.3 fusion.126
  368.6 5.0 multiply_reduce_fusion.5
  373.6 6.1 multiply_convert_fusion.5
  379.7 4.3 fusion.126
  397.9 5.0 multiply_reduce_fusion.5
  402.9 6.1 multiply_convert_fusion.5
  409.0 4.3 fusion.126
  427.2 5.0 multiply_reduce_fusion.5
  432.2 6.1 multiply_convert_fusion.5
  438.3 4.3 fusion.126
  446.9 3.9 slice.77
  450.9 4.0 slice.79
  455.1 3.4 convolution_convert_fusion.3
  458.6 8.3 %convolution_convert_fusion.1 = bf16[768,3072]{1,0:T(8,128)(2,1)} fusion(bf16[640,3072]{1,0:T(8,128)(2,1)} %copy-done.46, f32[640,768]{1,0:T(8,128)S(1)} %copy-done.13, f32[768]{0:T(1024)S(1)} %copy-done.37, f32[768]{0:T(1024)S(1)} %convert_element_type.193, f32[640]{0:T(1024)S(1)} %fusion.36, f32[640]{0:T(1024)S(1)} %broadcast_multiply_fusion), kind=kOutput, calls=%fused_computation.50 | convolution fusion | flops 3024715776 | bytes 10628096 | tf_op jit(solution)/shard_map/td,tf->df/dot_general | solution.py:174
  468.5 10.8 %convolution_convert_fusion = bf16[3072,768]{1,0:T(8,128)(2,1)} fusion(f32[640,768]{1,0:T(8,128)S(1)} %copy-done.4, f32[640,3072]{1,0:T(8,128)} %fusion.46, f32[3072]{0:T(1024)S(1)} %bitcast.153), kind=kOutput, calls=%fused_computation.49 | convolution fusion | flops 3042410496 | bytes 14561280 | tf_op jit(solution)/shard_map/tf,td->fd/dot_general | solution.py:167
  484.3 4.0 reduce-scatter.7.cloned.1.call-done
  489.3 41.0 %reduce-scatter.9.cloned.1.call-done = f32[128,768]{0,1:T(8,128)} async-done(((f32[1024,768]{0,1:T(8,128)}), f32[128,768]{0,1:T(8,128)}) %reduce-scatter.9.cloned.1.call-update) | async-done | bytes 393232 | tf_op jit(solution)/shard_map/reduce_scatter | solution.py:238
  531.5 6.7 convolution_convert_fusion.2
  541.9 20.2 %reduce-scatter.13.cloned.1.call-done = bf16[96,768]{1,0:T(8,128)(2,1)} async-done(((bf16[768,768]{1,0:T(8,128)(2,1)}), bf16[96,768]{1,0:T(8,128)(2,1)}) %reduce-scatter.13.cloned.1.call-update) | async-done | bytes 147472 | tf_op jit(solution)/shard_map/reduce_scatter | solution.py:263
  562.0 59.3 %reduce-scatter.15.cloned.1.call-done = bf16[96,3072]{1,0:T(8,128)(2,1)} async-done(((bf16[768,3072]{1,0:T(8,128)(2,1)}), bf16[96,3072]{1,0:T(8,128)(2,1)}) %reduce-scatter.15.cloned.1.call-update) | async-done | bytes 589840 | tf_op jit(solution)/shard_map/reduce_scatter | solution.py:275
  621.3 55.7 %reduce-scatter.17.cloned.1.call-done = bf16[384,768]{1,0:T(8,128)(2,1)} async-done(((bf16[3072,768]{1,0:T(8,128)(2,1)}), bf16[384,768]{1,0:T(8,128)(2,1)}) %reduce-scatter.17.cloned.1.call-update) | async-done | bytes 589840 | tf_op jit(solution)/shard_map/reduce_scatter | solution.py:281
  677.0 44.2 %reduce-scatter.11.cloned.1.call-done = bf16[96,2304]{1,0:T(8,128)(2,1)} async-done(((bf16[768,2304]{1,0:T(8,128)(2,1)}), bf16[96,2304]{1,0:T(8,128)(2,1)}) %reduce-scatter.11.cloned.1.call-update) | async-done | bytes 442384 | tf_op jit(solution)/shard_map/reduce_scatter | solution.py:257
  721.3 5.7 fusion.47
  729.3 22.3 %all-reduce.15 = (bf16[768]{0:T(1024)(128)(2,1)S(1)}, bf16[768]{0:T(1024)(128)(2,1)S(1)}, bf16[1536]{0:T(1024)(128)(2,1)S(1)}, bf16[768]{0:T(1024)(128)(2,1)S(1)...) all-reduce(bf16[768]{0:T(1024)(128)(2,1)S(1)} %get-tuple-element.24, ...), channel_id=4, replica_groups=mesh['rep'=4,'shard'=8] {'shard'}, use_global_device_ids=true, to_apply=%region_20.21.clone | all-reduce | flops 9216 | bytes 36864
  752.2 9.9 %all-reduce.17 = (bf16[96]{0:T(256)(128)(2,1)S(1)}, bf16[96]{0:T(256)(128)(2,1)S(1)}, bf16[192]{0:T(256)(128)(2,1)S(1)}, bf16[96]{0:T(256)(128)(2,1)S(1)}, bf16[...) all-reduce(bf16[96]{0:T(256)(128)(2,1)S(1)} %dynamic-slice.8, ...), channel_id=1, replica_groups=mesh['rep'=4,'shard'=8] {'rep'}, use_global_device_ids=true, to_apply=%region_21.22 | all-reduce | flops 1152 | bytes 4608 | tf_op jit(solution)/shard_map/psum | solution.py:289
  766.4 3.5 add_add_fusion.2
  769.9 20.1 %all-reduce.21.cloned.1.call-done = (bf16[96,2304]{1,0:T(8,128)(2,1)}, bf16[96,768]{1,0:T(8,128)(2,1)}, bf16[96,3072]{1,0:T(8,128)(2,1)}, bf16[384,768]{1,0:T(8,128)(2,1)}) async-done(((bf16[96,2304]{1,0:T(8,128)(2,1)}, bf16[96,768]{1,0:T(8,128)(2,1)}, bf16[96,3072]{1,0:T(8,128)(2,1)}, bf16[384,768]{1,0:T(8,128)(2,1)}), (bf16[96,2304]{1,0:T(8,128)(2,1)}, bf16[96,768]{1,0:T(8,128)(2,1)}, ...) | async-done | bytes 1769488 | tf_op jit(solution)/shard_map/psum | solution.py:291
  (421 shorter events, 218.7 us)
Async XLA Ops:
  7.2 44.4 %all-gather.8.cloned.1.call-start = ((), (), s32[]{:S(2)}) async-start(), calls=%async_computation.6 | async-start | bytes 3981312 | tf_op jit(solution)/shard_map/all_gather | solution.py:49
  7.9 111.8 %all-gather.12.cloned.1.call-start = ((), (), s32[]{:S(2)}) async-start(), calls=%async_computation.8 | async-start | bytes 1769472 | tf_op jit(solution)/shard_map/all_gather | solution.py:94
  43.1 13.4 %copy-start.22 = (f32[768]{0:T(1024)}, f32[768]{0:T(1024)S(1)}, u32[]{:S(2)}) copy-start(f32[768]{0:T(1024)S(1)} %convert_element_type.187) | copy-start | bytes 9220
  43.1 13.5 %copy-start.34 = (f32[768]{0:T(1024)}, f32[768]{0:T(1024)S(1)}, u32[]{:S(2)}) copy-start(f32[768]{0:T(1024)S(1)} %convert_element_type.188) | copy-start | bytes 9220
  44.6 12.0 %copy-start.20 = (f32[640]{0:T(1024)}, f32[640]{0:T(1024)S(1)}, u32[]{:S(2)}) copy-start(f32[640]{0:T(1024)S(1)} %broadcast_multiply_fusion.1) | copy-start | bytes 7684
  46.8 9.8 %copy-start.24 = (f32[640]{0:T(1024)}, f32[640]{0:T(1024)S(1)}, u32[]{:S(2)}) copy-start(f32[640]{0:T(1024)S(1)} %fusion.35) | copy-start | bytes 7684
  46.8 14.8 %copy-start.28 = (s32[640]{0:T(1024)S(1)}, s32[640]{0:T(1024)}, u32[]{:S(2)}) copy-start(s32[640]{0:T(1024)} %param.35) | copy-start | bytes 7684
  46.8 55.2 %copy-start.40 = (bf16[384]{0:T(512)(128)(2,1)S(1)}, bf16[384]{0:T(512)(128)(2,1)}, u32[]{:S(2)}) copy-start(bf16[384]{0:T(512)(128)(2,1)} %param.30) | copy-start | bytes 2308
  59.0 66.6 %all-gather.10.cloned.1.call-start = ((), (), s32[]{:S(2)}) async-start(), calls=%async_computation.7 | async-start | bytes 1769472 | tf_op jit(solution)/shard_map/all_gather | solution.py:95
  59.7 150.7 %all-gather.14.cloned.1.call-start = ((), (), s32[]{:S(2)}) async-start(), calls=%async_computation.9 | async-start | bytes 1327104 | tf_op jit(solution)/shard_map/all_gather | solution.py:51
  60.3 154.5 %all-gather.16.cloned.1.call-start = ((), (), s32[]{:S(2)}) async-start(), calls=%async_computation.10 | async-start | bytes 5308416 | tf_op jit(solution)/shard_map/all_gather | solution.py:55
  60.9 176.6 %all-gather.18.cloned.1.call-start = ((), (), s32[]{:S(2)}) async-start(), calls=%async_computation.11 | async-start | bytes 5308416 | tf_op jit(solution)/shard_map/all_gather | solution.py:57
  61.5 426.8 %reduce-scatter.7.cloned.1.call-start = ((), (), s32[]{:S(2)}) async-start(), calls=%async_computation.12 | async-start | bytes 3538944 | tf_op jit(solution)/shard_map/reduce_scatter | solution.py:237
  102.8 112.0 %copy-start.36 = (f32[768]{0:T(1024)}, f32[768]{0:T(1024)S(1)}, u32[]{:S(2)}) copy-start(f32[768]{0:T(1024)S(1)} %convert_element_type.194) | copy-start | bytes 9220
  115.6 134.1 %copy-start.29 = (f32[8,1,384]{2,1,0:T(1,128)}, f32[8,1,384]{2,1,0:T(1,128)S(1)}, u32[]{:S(2)}) copy-start(f32[8,1,384]{2,1,0:T(1,128)S(1)} %convert_element_type.229) | copy-start | bytes 36868
  132.9 77.5 %copy-start.8 = (bf16[640,768]{1,0:T(8,128)(2,1)S(1)}, bf16[640,768]{1,0:T(8,128)(2,1)}, u32[]{:S(2)}) copy-start(bf16[640,768]{1,0:T(8,128)(2,1)} %param.20) | copy-start | bytes 2949124
  237.5 11.2 %copy-start.15 = (bf16[640,768]{1,0:T(8,128)(2,1)S(1)}, bf16[640,768]{1,0:T(8,128)(2,1)}, u32[]{:S(2)}) copy-start(bf16[640,768]{1,0:T(8,128)(2,1)} %param.33) | copy-start | bytes 2949124
  237.5 11.2 %copy-start.16 = (bf16[640,768]{1,0:T(8,128)(2,1)S(1)}, bf16[640,768]{1,0:T(8,128)(2,1)}, u32[]{:S(2)}) copy-start(bf16[640,768]{1,0:T(8,128)(2,1)} %param.34) | copy-start | bytes 2949124
  237.5 12.2 %copy-start.45 = (f32[640,3072]{1,0:T(8,128)S(1)}, f32[640,3072]{1,0:T(8,128)}, u32[]{:S(2)}) copy-start(f32[640,3072]{1,0:T(8,128)} %fusion.46) | copy-start | bytes 23592964
  248.7 13.3 %slice-start = ((s8[4718592]{0:T(1024)(128)(4,1)}), s8[4194304]{0:T(1024)(128)(4,1)S(1)}, s32[]{:S(2)}) async-start(s8[4718592]{0:T(1024)(128)(4,1)} %bitcast.155), calls=%async_computation.19 | async-start | bytes 8388608
  249.7 17.3 %copy-start.3 = (f32[640,768]{1,0:T(8,128)}, f32[640,768]{1,0:T(8,128)S(1)}, u32[]{:S(2)}) copy-start(f32[640,768]{1,0:T(8,128)S(1)} %get-tuple-element.332) | copy-start | bytes 5898244
  251.7 10.3 %copy-start.12 = (f32[640,768]{1,0:T(8,128)S(1)}, f32[640,768]{1,0:T(8,128)}, u32[]{:S(2)}) copy-start(f32[640,768]{1,0:T(8,128)} %copy-done.11) | copy-start | bytes 5898244
  251.7 10.3 %slice-start.1 = ((s8[4718592]{0:T(1024)(128)(4,1)}), s8[524288]{0:T(1024)(128)(4,1)S(1)}, s32[]{:S(2)}) async-start(s8[4718592]{0:T(1024)(128)(4,1)} %bitcast.155), calls=%async_computation.20 | async-start | bytes 1048576
  271.0 7.4 copy-start.43
  300.3 5.9 copy-start.6
  300.3 7.4 copy-start.43
  329.6 5.9 copy-start.6
  329.6 7.4 copy-start.43
  359.0 5.9 copy-start.6
  359.0 7.4 copy-start.43
  388.3 7.4 copy-start.43
  417.6 7.4 copy-start.43
  450.9 79.4 %reduce-scatter.9.cloned.1.call-start = ((), (), s32[]{:S(2)}) async-start(), calls=%async_computation.13 | async-start | bytes 3538944 | tf_op jit(solution)/shard_map/reduce_scatter | solution.py:238
  455.0 107.0 %reduce-scatter.13.cloned.1.call-start = ((), (), s32[]{:S(2)}) async-start(), calls=%async_computation.15 | async-start | bytes 1327104 | tf_op jit(solution)/shard_map/reduce_scatter | solution.py:263
  458.5 162.8 %reduce-scatter.15.cloned.1.call-start = ((), (), s32[]{:S(2)}) async-start(), calls=%async_computation.16 | async-start | bytes 5308416 | tf_op jit(solution)/shard_map/reduce_scatter | solution.py:275
  467.0 210.0 %reduce-scatter.17.cloned.1.call-start = ((), (), s32[]{:S(2)}) async-start(), calls=%async_computation.17 | async-start | bytes 5308416 | tf_op jit(solution)/shard_map/reduce_scatter | solution.py:281
  479.3 52.2 %copy-start.9 = (bf16[640,768]{1,0:T(8,128)(2,1)S(1)}, bf16[640,768]{1,0:T(8,128)(2,1)}, u32[]{:S(2)}) copy-start(bf16[640,768]{1,0:T(8,128)(2,1)} %param.20) | copy-start | bytes 2949124
  479.3 52.2 %copy-start.21 = (f32[640]{0:T(1024)S(1)}, f32[640]{0:T(1024)}, u32[]{:S(2)}) copy-start(f32[640]{0:T(1024)} %copy-done.20) | copy-start | bytes 7684
  479.3 52.2 %copy-start.23 = (f32[768]{0:T(1024)S(1)}, f32[768]{0:T(1024)}, u32[]{:S(2)}) copy-start(f32[768]{0:T(1024)} %copy-done.22) | copy-start | bytes 9220
  479.3 52.2 %copy-start.25 = (f32[640]{0:T(1024)S(1)}, f32[640]{0:T(1024)}, u32[]{:S(2)}) copy-start(f32[640]{0:T(1024)} %copy-done.24) | copy-start | bytes 7684
  479.3 52.2 %copy-start.35 = (f32[768]{0:T(1024)S(1)}, f32[768]{0:T(1024)}, u32[]{:S(2)}) copy-start(f32[768]{0:T(1024)} %copy-done.34) | copy-start | bytes 9220
  479.4 241.9 %reduce-scatter.11.cloned.1.call-start = ((), (), s32[]{:S(2)}) async-start(), calls=%async_computation.14 | async-start | bytes 3981312 | tf_op jit(solution)/shard_map/reduce_scatter | solution.py:257
  538.3 251.7 %all-reduce.21.cloned.1.call-start = ((), (), s32[]{:S(2)}) async-start(), calls=%async_computation.18 | async-start | bytes 3538944 | tf_op jit(solution)/shard_map/psum | solution.py:291
  721.3 8.0 copy-start.31
  721.3 8.0 copy-start.32
  721.3 8.0 copy-start.33
  721.3 8.0 copy-start.38
  721.3 8.0 copy-start.39
  (49 other events, 162.4 us)
Sparse Core Ops, SparseCore 0:
  9.6 41.9 all-gather.7
  59.1 24.6 all-gather.11
  86.1 24.3 all-gather.9
  111.9 22.3 all-gather.13
  135.8 50.1 all-gather.15
  187.5 49.9 all-gather.17
  451.0 37.2 reduce-scatter.6
  490.6 39.6 reduce-scatter.8
  533.2 28.8 reduce-scatter.12
  564.2 57.0 reduce-scatter.14
  623.6 53.3 reduce-scatter.16
  679.2 42.0 reduce-scatter.10
  724.7 65.2 all-reduce.20
where the time goes:
time: 813 us; the launch traced here: 804 us
  waiting for transfers between devices  266 us (33%)
  matrix products  188 us (23%)
  blocking collectives  112 us (14%)
  other arithmetic  106 us (13%)
  local copies, waits for them, and re-layouts  103 us (13%)
  between operations  18.7 us (2%)
  loops' own time  9.07 us (1%)
    reduce_scatter x1, waiting for transfers between devices, local(): lax.psum_scatter(grad_fc.astype(jnp.bfloat16), 'shard', scatter_dimension...  59.3 us
    reduce_scatter x1, waiting for transfers between devices, local(): lax.psum_scatter(grad_proj.astype(jnp.bfloat16), 'shard', scatter_dimensi...  55.7 us
    unnamed x2, blocking collectives  49 us
    reduce_scatter x1, waiting for transfers between devices, local(): lax.psum_scatter(grad_wqkv.astype(jnp.bfloat16), 'shard', scatter_dimensi...  44.2 us
    dot_general x12, matrix products, pair_scores(): jnp.einsum('qhd,khd->hqk', query_three, key_three, preferred_element_type...  41.7 us
    reduce_scatter x1, waiting for transfers between devices, local(): lax.psum_scatter(grad_values_all[:prompt_len], 'shard', scatter_dimension...  41 us
    psum x1, blocking collectives, local(): token_total = lax.psum(jnp.sum(mask_f), ('rep', 'shard'))  39.9 us
    convert_element_type x6, other arithmetic, pair_back(): grad_scores = (probs * (grad_probs - row_dot)).astype(jnp.bfloat16)  36.8 us
  transfers between devices with their start and end apart: 13, of which 9 were waited for; matrix products, arithmetic and copies ran while one was open for 21% of the time, Pallas kernels for 0%

commit v1 on v0

v1 whole, which is shorter than its diff:
```python
import jax
import jax.numpy as jnp
from jax import lax
from jax.experimental import pallas as pl
from jax.experimental.pallas import tpu as pltpu
from jax.sharding import PartitionSpec as P

F32 = jnp.float32
BF = jnp.bfloat16
HEAD = 64
PR_DEV = 128
PAIR = 2 * HEAD
SCALE = 0.125
EPS = 1e-05
NEG = -1e30
VMEM_LIMIT = 60 * 1024 * 1024


def dot_nt(a, b):
    return lax.dot_general(a, b, (((1,), (1,)), ((), ())), preferred_element_type=F32)


def dot_nn(a, b):
    return lax.dot_general(a, b, (((1,), (0,)), ((), ())), preferred_element_type=F32)


def dot_tn(a, b):
    return lax.dot_general(a, b, (((0,), (0,)), ((), ())), preferred_element_type=F32)


def normalize(values):
    centered = values - jnp.mean(values, axis=-1, keepdims=True)
    inv = lax.rsqrt(jnp.mean(centered * centered, axis=-1, keepdims=True) + EPS)
    return centered * inv, inv


def norm_back(e, z, inv):
    return inv * (
        e - jnp.mean(e, axis=-1, keepdims=True) - z * jnp.mean(e * z, axis=-1, keepdims=True)
    )


def layer_norm(values, gain_vec, bias_vec):
    return normalize(values)[0] * gain_vec + bias_vec


def gelu_tanh(values):
    return (
        0.5
        * values
        * (1.0 + jnp.tanh(0.7978845608028654 * (values + 0.044715 * values * values * values)))
    )


def column_sums(matrix):
    return jnp.sum(matrix.astype(F32), axis=0)


def cost(flops, nbytes, trans=0):
    return pl.CostEstimate(flops=int(flops), bytes_accessed=int(nbytes), transcendentals=int(trans))


def qkv_call(bundle, tokens, vecs, shard):
    ns, _, width = bundle.shape
    tok = tokens.shape[0]
    cont = tok - PR_DEV
    plen = ns * PR_DEV
    keys = plen + cont
    dsh = width // ns

    def kern(sh_ref, g_ref, t_ref, vec_ref, h_ref, q_ref, k_ref, v_ref):
        gain, bias, bq, bv = vec_ref[0:1], vec_ref[1:2], vec_ref[2:3], vec_ref[3:4]
        wq, wk, wv = (
            g_ref[:, j * dsh : (j + 1) * dsh, :].reshape(width, width) for j in range(3)
        )
        step = 4

        def chunk(x, r0):
            h = (normalize(x.astype(F32))[0] * gain + bias).astype(BF)
            rows = pl.ds(r0, h.shape[0])
            h_ref[rows, :] = h
            k_ref[rows, :] = dot_nn(h, wk).astype(BF)
            v_ref[rows, :] = (dot_nn(h, wv) + bv).astype(BF)

        def to_q(h):
            return ((dot_nn(h, wq) + bq).astype(BF).astype(F32) * SCALE).astype(BF)

        for b in range(0, ns, step):
            x = g_ref[b : b + step, 3 * dsh : 3 * dsh + PR_DEV, :]
            chunk(x.reshape(x.shape[0] * PR_DEV, width), b * PR_DEV)
        chunk(t_ref[PR_DEV:, :], plen)
        own = pl.multiple_of(sh_ref[0] * PR_DEV, PR_DEV)
        q_ref[:PR_DEV, :] = to_q(h_ref[pl.ds(own, PR_DEV), :])
        q_ref[PR_DEV:, :] = to_q(h_ref[plen:, :])

    shape = lambda r: jax.ShapeDtypeStruct((r, width), BF)
    vm = pl.BlockSpec(memory_space=pltpu.VMEM)
    return pl.pallas_call(
        kern,
        in_specs=[pl.BlockSpec(memory_space=pltpu.SMEM), vm, vm, vm],
        out_specs=[vm] * 4,
        out_shape=[shape(keys), shape(tok), shape(keys), shape(keys)],
        compiler_params=pltpu.CompilerParams(vmem_limit_bytes=VMEM_LIMIT),
        cost_estimate=cost(2 * width * width * (2 * keys + tok), 2 * width * (6 * keys)),
        name="qkv",
    )(shard, bundle, tokens, vecs)


def attn_fwd(q, k, v, shard, rb):
    tok, width = q.shape
    keys = k.shape[0]
    cont = tok - PR_DEV
    plen = keys - cont
    npair = width // PAIR

    def kern(sh_ref, q_ref, k_ref, v_ref, o_ref, lse_ref):
        sh = sh_ref[0]
        first = lax.broadcasted_iota(jnp.int32, (1, PAIR), 1) < HEAD

        def block(r0, rows, n, offset, masked):
            outs, lses = [], []
            for h in range(2):
                mine = first if h == 0 else jnp.logical_not(first)
                qq = jnp.where(mine, q_ref[pl.ds(r0, rows), :], 0).astype(BF)
                s = dot_nt(qq, k_ref[pl.ds(0, n), :])
                tail = s[:, n - masked :]
                row = lax.broadcasted_iota(jnp.int32, tail.shape, 0)
                col = lax.broadcasted_iota(jnp.int32, tail.shape, 1)
                tail = jnp.where(col <= row + offset, tail, NEG)
                s = tail if masked == n else jnp.concatenate([s[:, : n - masked], tail], axis=1)
                top = jnp.max(s, axis=1, keepdims=True)
                p = jnp.exp(s - top)
                total = jnp.sum(p, axis=1, keepdims=True)
                outs.append(dot_nn(p.astype(BF), v_ref[pl.ds(0, n), :]) * (1.0 / total))
                lses.append(top + jnp.log(total))
            o_ref[pl.ds(r0, rows), :] = jnp.where(first, outs[0], outs[1]).astype(BF)
            turned = jnp.transpose(jnp.where(first, lses[0], lses[1]))
            lse_ref[0, 0:1, pl.ds(r0, rows)] = turned[0:1]
            lse_ref[0, 1:2, pl.ds(r0, rows)] = turned[HEAD : HEAD + 1]

        block(0, PR_DEV, plen, sh * PR_DEV, plen)
        for i in range(cont // rb):
            block(PR_DEV + i * rb, rb, plen + (i + 1) * rb, 0, rb)

    spq = pl.BlockSpec((tok, PAIR), lambda i: (0, i))
    spk = pl.BlockSpec((keys, PAIR), lambda i: (0, i))
    return pl.pallas_call(
        kern,
        grid=(npair,),
        in_specs=[pl.BlockSpec(memory_space=pltpu.SMEM), spq, spk, spk],
        out_specs=[spq, pl.BlockSpec((1, 2, tok), lambda i: (i, 0, 0))],
        out_shape=[
            jax.ShapeDtypeStruct((tok, width), BF),
            jax.ShapeDtypeStruct((npair, 2, tok), F32),
        ],
        compiler_params=pltpu.CompilerParams(vmem_limit_bytes=VMEM_LIMIT),
        cost_estimate=cost(16 * width * tok * keys, 4 * width * (tok + keys)),
        name="attn_fwd",
    )(shard, q, k, v)


def attn_bwd(q, k, v, o, do, lse, shard, rb):
    tok, width = q.shape
    keys = k.shape[0]
    cont = tok - PR_DEV
    plen = keys - cont
    npair = width // PAIR

    def kern(sh_ref, q_ref, k_ref, v_ref, o_ref, do_ref, lse_ref, dq_ref, dk_ref, dv_ref, ka, va):
        sh = sh_ref[0]
        first = lax.broadcasted_iota(jnp.int32, (1, PAIR), 1) < HEAD
        ka[...] = jnp.zeros_like(ka)
        va[...] = jnp.zeros_like(va)
        hr = lax.broadcasted_iota(jnp.int32, (8, PAIR), 0)
        hc = lax.broadcasted_iota(jnp.int32, (8, PAIR), 1)
        pick = jnp.where(hc // HEAD == hr, 1.0, 0.0).astype(F32)

        def block(r0, rows, n, offset, masked):
            prod = o_ref[pl.ds(r0, rows), :].astype(F32) * do_ref[pl.ds(r0, rows), :].astype(F32)
            row_dot = lax.dot_general(
                pick,
                prod,
                (((1,), (1,)), ((), ())),
                precision=lax.Precision.HIGHEST,
                preferred_element_type=F32,
            )
            dqs = []
            for h in range(2):
                mine = first if h == 0 else jnp.logical_not(first)
                qq = jnp.where(mine, q_ref[pl.ds(r0, rows), :], 0).astype(BF)
                gg = jnp.where(mine, do_ref[pl.ds(r0, rows), :], 0).astype(BF)
                kk = k_ref[pl.ds(0, n), :]
                s = dot_nt(kk, qq)
                tail = s[n - masked :]
                col = lax.broadcasted_iota(jnp.int32, tail.shape, 0)
                row = lax.broadcasted_iota(jnp.int32, tail.shape, 1)
                tail = jnp.where(col <= row + offset, tail, NEG)
                s = tail if masked == n else jnp.concatenate([s[: n - masked], tail], axis=0)
                p = jnp.exp(s - lse_ref[0, h : h + 1, pl.ds(r0, rows)])
                dp = dot_nt(v_ref[pl.ds(0, n), :], gg)
                ds = (p * (dp - row_dot[h : h + 1, :])).astype(BF)
                va[pl.ds(0, n), :] += dot_nn(p.astype(BF), gg)
                ka[pl.ds(0, n), :] += dot_nn(ds, qq)
                dqs.append(dot_tn(ds, kk))
            dq_ref[pl.ds(r0, rows), :] = (jnp.where(first, dqs[0], dqs[1]) * SCALE).astype(BF)

        block(0, PR_DEV, plen, sh * PR_DEV, plen)
        for i in range(cont // rb):
            block(PR_DEV + i * rb, rb, plen + (i + 1) * rb, 0, rb)
        dk_ref[...] = ka[...].astype(BF)
        dv_ref[...] = va[...].astype(BF)

    spq = pl.BlockSpec((tok, PAIR), lambda i: (0, i))
    spk = pl.BlockSpec((keys, PAIR), lambda i: (0, i))
    return pl.pallas_call(
        kern,
        grid=(npair,),
        in_specs=[
            pl.BlockSpec(memory_space=pltpu.SMEM),
            spq,
            spk,
            spk,
            spq,
            spq,
            pl.BlockSpec((1, 2, tok), lambda i: (i, 0, 0)),
        ],
        out_specs=[spq, spk, spk],
        out_shape=[
            jax.ShapeDtypeStruct((tok, width), BF),
            jax.ShapeDtypeStruct((keys, width), BF),
            jax.ShapeDtypeStruct((keys, width), BF),
        ],
        scratch_shapes=[pltpu.VMEM((keys, PAIR), F32), pltpu.VMEM((keys, PAIR), F32)],
        compiler_params=pltpu.CompilerParams(vmem_limit_bytes=VMEM_LIMIT),
        cost_estimate=cost(40 * width * tok * keys, 8 * width * (tok + keys)),
        name="attn_bwd",
    )(shard, q, k, v, o, do, lse)


def dh1_call(bundle, tokens, vecs, dq, dk, dv, dx1, shard):
    ns, _, width = bundle.shape
    tok = tokens.shape[0]
    cont = tok - PR_DEV
    plen = ns * PR_DEV
    dsh = width // ns

    def kern(sh_ref, g_ref, t_ref, vec_ref, dq_ref, dk_ref, dv_ref, dx_ref, pd_ref, ig_ref, sm_ref):
        gain = vec_ref[0:1]
        wq, wk, wv = (
            g_ref[:, j * dsh : (j + 1) * dsh, :].reshape(width, width) for j in range(3)
        )
        step = 4
        g_gain = jnp.zeros((1, width), F32)
        g_bias = jnp.zeros((1, width), F32)
        g_v = jnp.zeros((1, width), F32)
        total = lambda m: jnp.sum(m, axis=0, keepdims=True)
        for b in range(0, ns, step):
            x = g_ref[b : b + step, 3 * dsh : 3 * dsh + PR_DEV, :]
            rows = x.shape[0] * PR_DEV
            z, _ = normalize(x.reshape(rows, width).astype(F32))
            dvr = dv_ref[b * PR_DEV : b * PR_DEV + rows, :]
            dh = dot_nt(dk_ref[b * PR_DEV : b * PR_DEV + rows, :], wk) + dot_nt(dvr, wv)
            g_gain += total(dh * z)
            g_bias += total(dh)
            g_v += total(dvr.astype(F32))
            pd_ref[b * PR_DEV : b * PR_DEV + rows, :] = dh.astype(BF)
        z, inv = normalize(t_ref[PR_DEV:, :].astype(F32))
        dvr = dv_ref[plen:, :]
        dh = dot_nt(dk_ref[plen:, :], wk) + dot_nt(dvr, wv) + dot_nt(dq_ref[PR_DEV:, :], wq)
        g_gain += total(dh * z)
        g_bias += total(dh)
        g_v += total(dvr.astype(F32))
        ig_ref[PR_DEV:, :] = dx_ref[PR_DEV:, :] + norm_back(dh * gain, z, inv)
        ig_ref[:PR_DEV, :] = dx_ref[:PR_DEV, :]
        own = pl.ds(pl.multiple_of(sh_ref[0] * PR_DEV, PR_DEV), PR_DEV)
        z, _ = normalize(t_ref[:PR_DEV, :].astype(F32))
        part = dot_nt(dq_ref[:PR_DEV, :], wq)
        g_gain += total(part * z)
        g_bias += total(part)
        both = dot_nt(dk_ref[own, :], wk) + dot_nt(dv_ref[own, :], wv)
        pd_ref[own, :] = (both + part).astype(BF)
        sm_ref[0:1, :] = g_gain
        sm_ref[1:2, :] = g_bias
        sm_ref[2:3, :] = total(dq_ref[...].astype(F32))
        sm_ref[3:4, :] = g_v
        sm_ref[4:8, :] = jnp.zeros((4, width), F32)

    vm = pl.BlockSpec(memory_space=pltpu.VMEM)
    return pl.pallas_call(
        kern,
        in_specs=[pl.BlockSpec(memory_space=pltpu.SMEM)] + [vm] * 7,
        out_specs=[vm] * 3,
        out_shape=[
            jax.ShapeDtypeStruct((plen, width), BF),
            jax.ShapeDtypeStruct((tok, width), F32),
            jax.ShapeDtypeStruct((8, width), F32),
        ],
        compiler_params=pltpu.CompilerParams(vmem_limit_bytes=VMEM_LIMIT),
        cost_estimate=cost(
            2 * width * width * (2 * (plen + cont) + tok), 2 * width * (5 * plen + 8 * cont)
        ),
        name="dh1",
    )(shard, bundle, tokens, vecs, dq, dk, dv, dx1)


def grad_wqkv_call(h1, dq, dk, dv, small, shard, ns):
    keys, width = h1.shape
    tok = dq.shape[0]
    plen = ns * PR_DEV
    dsh = width // ns
    extra = small.shape[1]

    def kern(sh_ref, h_ref, dq_ref, dk_ref, dv_ref, s_ref, o_ref):
        own = pl.ds(pl.multiple_of(sh_ref[0] * PR_DEV, PR_DEV), PR_DEV)
        gq = dot_tn(h_ref[own, :], dq_ref[:PR_DEV, :]) + dot_tn(h_ref[plen:, :], dq_ref[PR_DEV:, :])
        o_ref[:, :dsh, :] = gq.astype(BF).reshape(ns, dsh, width)
        gk = dot_tn(h_ref[...], dk_ref[...])
        o_ref[:, dsh : 2 * dsh, :] = gk.astype(BF).reshape(ns, dsh, width)
        gv = dot_tn(h_ref[...], dv_ref[...])
        o_ref[:, 2 * dsh : 3 * dsh, :] = gv.astype(BF).reshape(ns, dsh, width)
        o_ref[:, 3 * dsh :, :] = s_ref[...]

    vm = pl.BlockSpec(memory_space=pltpu.VMEM)
    return pl.pallas_call(
        kern,
        in_specs=[pl.BlockSpec(memory_space=pltpu.SMEM)] + [vm] * 5,
        out_specs=vm,
        out_shape=jax.ShapeDtypeStruct((ns, 3 * dsh + extra, width), BF),
        compiler_params=pltpu.CompilerParams(vmem_limit_bytes=VMEM_LIMIT),
        cost_estimate=cost(2 * width * width * (2 * keys + tok), 2 * width * (4 * keys)),
        name="grad_wqkv",
    )(shard, h1, dq, dk, dv, small)


def finish_call(grad, summed, tokens, vecs):
    tok, width = grad.shape

    def kern(g_ref, s_ref, t_ref, vec_ref, o_ref):
        z, inv = normalize(t_ref[...].astype(F32))
        e = s_ref[...].astype(F32) * vec_ref[0:1]
        o_ref[...] = g_ref[...] + norm_back(e, z, inv)

    block = pl.BlockSpec((PR_DEV, width), lambda i: (0, 0))
    return pl.pallas_call(
        kern,
        grid=(1,),
        in_specs=[block, block, block, pl.BlockSpec(vecs.shape, lambda i: (0, 0))],
        out_specs=block,
        out_shape=jax.ShapeDtypeStruct((tok, width), F32),
        input_output_aliases={0: 0},
        cost_estimate=cost(20 * PR_DEV * width, 12 * PR_DEV * width),
        name="finish",
    )(grad, summed, tokens, vecs)


def rep_sum(values):
    n = lax.axis_size("rep")
    if n & (n - 1):
        return [lax.psum(v.astype(t), "rep").astype(F32) for v, t in values]
    out = [v for v, _ in values]
    bit = 1
    while bit < n:
        perm = [(i, i ^ bit) for i in range(n)]
        got = [lax.ppermute(v.astype(t), "rep", perm) for v, (_, t) in zip(out, values)]
        out = [v.astype(t).astype(F32) + g.astype(F32) for v, g, (_, t) in zip(out, got, values)]
        bit *= 2
    return out


def local(
    tokens,
    ln1_gain,
    ln1_bias,
    w_qkv,
    qv_bias,
    w_out,
    out_bias,
    ln2_gain,
    ln2_bias,
    w_fc,
    fc_bias,
    w_proj,
    proj_bias,
    teacher,
    cotangent,
    valid_mask,
):
    ns = lax.axis_size("shard")
    shard = lax.axis_index("shard").astype(jnp.int32).reshape(1)
    tok, width = tokens.shape
    hidden = w_fc.shape[1]
    plen = ns * PR_DEV
    dsh = width // ns
    rb = 256

    bundle = lax.all_gather(
        jnp.concatenate(
            [w_qkv[:, :width], w_qkv[:, width : 2 * width], w_qkv[:, 2 * width :], tokens[:PR_DEV]]
        ),
        "shard",
    )
    mask_f = valid_mask.astype(F32)
    counts = jnp.sum(mask_f.reshape(-1, PR_DEV), axis=1).astype(BF)
    sizes = [v.shape[0] for v in (ln1_gain, ln1_bias, qv_bias, out_bias, ln2_gain, ln2_bias, fc_bias, proj_bias)]
    offs = [0]
    for s in sizes:
        offs.append(offs[-1] + s)
    packed = jnp.concatenate(
        [ln1_gain, ln1_bias, qv_bias, out_bias, ln2_gain, ln2_bias, fc_bias, proj_bias, counts]
    )
    packed = jnp.pad(packed, (0, (-packed.shape[0]) % 128))
    params = lax.all_gather(packed.reshape(1, -1), "shard", axis=0, tiled=True).astype(F32)
    gain_one, bias_one, full_qv, full_ob, gain_two, bias_two, full_fb, full_pb = (
        params[:, offs[i] : offs[i + 1]].reshape(-1) for i in range(8)
    )
    count = jnp.sum(params[:, offs[8] : offs[8] + tok // PR_DEV])
    (token_total,) = rep_sum([(jnp.full((8, 128), count, F32), F32)])
    token_total = token_total[0, 0]
    vecs = jnp.stack([gain_one, bias_one, full_qv[:width], full_qv[width:]] + [gain_one] * 4)

    full_out = lax.all_gather(w_out, "shard", axis=0, tiled=True)
    full_fc = lax.all_gather(w_fc, "shard", axis=0, tiled=True)
    full_proj = lax.all_gather(w_proj, "shard", axis=0, tiled=True)

    h1, q, k, v = qkv_call(bundle, tokens, vecs, shard)
    mix, lse = attn_fwd(q, k, v, shard, rb)

    inputs = tokens.astype(F32)
    resid_one = inputs + dot_nn(mix, full_out) + full_ob
    normed_two, norm_two_back = jax.vjp(layer_norm, resid_one, gain_two, bias_two)
    act_two = normed_two.astype(BF)
    hidden_pre = dot_nn(act_two, full_fc) + full_fb
    hidden_act, gelu_back = jax.vjp(gelu_tanh, hidden_pre)
    hidden_low = hidden_act.astype(BF)
    output = resid_one + dot_nn(hidden_low, full_proj) + full_pb
    device_count = lax.axis_size("rep") * ns
    factor = tok * device_count / token_total
    grad_output = cotangent.astype(F32) + factor * mask_f[:, None] * (output - teacher.astype(F32))
    grad_branch = grad_output.astype(BF)
    grad_pb = column_sums(grad_branch)
    grad_proj = dot_tn(hidden_low, grad_branch)
    own_proj = lax.psum_scatter(grad_proj.astype(BF), "shard", scatter_dimension=0, tiled=True)
    grad_hidden = dot_nt(grad_branch, full_proj)
    (grad_pre,) = gelu_back(grad_hidden)
    grad_pre_low = grad_pre.astype(BF)
    grad_fb = column_sums(grad_pre_low)
    grad_fc = dot_tn(act_two, grad_pre_low)
    own_fc = lax.psum_scatter(grad_fc.astype(BF), "shard", scatter_dimension=0, tiled=True)
    grad_act_two = dot_nt(grad_pre_low, full_fc)
    grad_resid_part, grad_gain_two, grad_bias_two = norm_two_back(grad_act_two)
    grad_resid = grad_output + grad_resid_part
    grad_attn = grad_resid.astype(BF)
    grad_ob = column_sums(grad_attn)
    grad_wo = dot_tn(mix, grad_attn)
    own_wo = lax.psum_scatter(grad_wo.astype(BF), "shard", scatter_dimension=0, tiled=True)
    grad_mix = dot_nt(grad_attn, full_out).astype(BF)

    dq, dk, dv = attn_bwd(q, k, v, mix, grad_mix, lse, shard, rb)
    part, ig, small = dh1_call(bundle, tokens, vecs, dq, dk, dv, grad_resid, shard)
    own_dh = lax.psum_scatter(part, "shard", scatter_dimension=0, tiled=True)
    input_grad = finish_call(ig, own_dh, tokens, vecs)

    small_list = [
        small[0],
        small[1],
        jnp.concatenate([small[2], small[3]]),
        grad_ob,
        grad_gain_two,
        grad_bias_two,
        grad_fb,
        grad_pb,
    ]
    rows = jnp.concatenate([s.reshape(ns, -1) for s in small_list], axis=1).astype(BF)
    unit = 16 * width
    rows = jnp.pad(rows, ((0, 0), (0, (-rows.shape[1]) % unit))).reshape(ns, -1, width)
    grads = grad_wqkv_call(h1, dq, dk, dv, rows, shard, ns)
    own_qkv = lax.psum_scatter(
        grads.reshape(-1, width), "shard", scatter_dimension=0, tiled=True
    )
    sum_proj, sum_fc, sum_wo = rep_sum(
        [(own_proj.astype(F32), BF), (own_fc.astype(F32), BF), (own_wo.astype(F32), BF)]
    )
    (sum_qkv,) = rep_sum([(own_qkv.astype(F32), BF)])
    grad_qkv_own = jnp.concatenate(
        [sum_qkv[:dsh], sum_qkv[dsh : 2 * dsh], sum_qkv[2 * dsh : 3 * dsh]], axis=1
    )
    flat = sum_qkv[3 * dsh :].reshape(-1)
    vec = [flat[offs[i] : offs[i + 1]] for i in range(8)]
    return (
        output.astype(BF),
        input_grad,
        vec[0],
        vec[1],
        grad_qkv_own,
        vec[2],
        sum_wo,
        vec[3],
        vec[4],
        vec[5],
        sum_fc,
        vec[6],
        sum_proj,
        vec[7],
    )


def solution(mesh):
    rows = P(("rep", "shard"), None)
    mat = P("shard", None)
    vec = P("shard")
    return jax.shard_map(
        local,
        mesh=mesh,
        in_specs=(
            rows,
            vec,
            vec,
            mat,
            vec,
            mat,
            vec,
            vec,
            vec,
            mat,
            vec,
            mat,
            vec,
            rows,
            rows,
            P(("rep", "shard")),
        ),
        out_specs=(rows, rows, vec, vec, mat, vec, mat, vec, vec, vec, mat, vec, mat, vec),
        check_vma=False,
    )
```

time: 813 us -> 562 us (0.69)
  matrix products: 188 us -> 66 us
  blocking collectives: 112 us -> 12.3 us
  other arithmetic: 106 us -> 15.2 us
  local copies, waits for them, and re-layouts: 103 us -> 12.6 us
  Pallas kernels: 0 us -> 90.3 us
  waiting for transfers between devices: 266 us -> 327 us
  starting transfers between devices: 0.69 us -> 15.5 us
  loops' own time: 9.07 us -> 0 us
    dot_general x54 -> x9, matrix products: 188 us -> 66 us  [the longest x3 22.6 us: dot_nt(): lax.dot_general(a, b, (((1,), (1,)), ((), ())), preferred_element_type=F32)]
    all_gather x6 -> x4, waiting for transfers between devices: 18.2 us -> 112 us  [the longest x1 43.6 us: local(): full_proj = lax.all_gather(w_proj, 'shard', axis=0, tiled=True)]
    pallas_call x0 -> x6, Pallas kernels: none -> 90.3 us  [the longest x1 32.2 us: attn_bwd(): pl.pallas_call(kern, grid=(npair,), in_specs=[pl.BlockSpec(memory_space=p...]
    reduce_scatter x6 -> x5, waiting for transfers between devices: 224 us -> 173 us  [the longest x1 57.5 us: local(): lax.psum_scatter(grad_proj.astype(BF), 'shard', scatter_dimension=0, tile...]
    psum x2 -> x0, blocking collectives: 49.8 us -> none  [the longest x1 39.9 us: local(): token_total = lax.psum(jnp.sum(mask_f), ('rep', 'shard'))]
    unnamed x2 -> x0, blocking collectives: 49 us -> none
    convert_element_type x25 -> x4, other arithmetic: 48 us -> 2.39 us  [rep_sum(): v.astype(t).astype(F32) + g.astype(F32)]
    dynamic_slice x54 -> x0, local copies, waits for them, and re-layouts: 42.3 us -> none  [the longest x42 34.7 us: columns(): return lax.dynamic_slice_in_dim(matrix, index * span, span, 1)]
  transfers between devices with their start and end apart: 13 -> 19, of which waited for: 9 -> 15; matrix products, arithmetic and copies ran while one was open for 21% -> 8% of each run, Pallas kernels for 0% -> 6%
where the time goes in v1:
time: 562 us; the launch traced here: 554 us
  waiting for transfers between devices  327 us (58%)
  Pallas kernels  90.3 us (16%)
  matrix products  66 us (12%)
  starting transfers between devices  15.5 us (3%)
  between operations  15.3 us (3%)
  other arithmetic  15.2 us (3%)
  local copies, waits for them, and re-layouts  12.6 us (2%)
  blocking collectives  12.3 us (2%)
    reduce_scatter x1, waiting for transfers between devices, local(): lax.psum_scatter(grad_proj.astype(BF), 'shard', scatter_dimension=0, tile...  57.5 us
    reduce_scatter x1, waiting for transfers between devices, local(): lax.psum_scatter(grad_fc.astype(BF), 'shard', scatter_dimension=0, tiled=...  54.1 us
    all_gather x1, waiting for transfers between devices, local(): full_proj = lax.all_gather(w_proj, 'shard', axis=0, tiled=True)  43.6 us
    all_gather x1, waiting for transfers between devices, local(): full_fc = lax.all_gather(w_fc, 'shard', axis=0, tiled=True)  39.7 us
    ppermute x10, waiting for transfers between devices, rep_sum(): lax.ppermute(v.astype(t), 'rep', perm)  38.5 us
    pallas_call x1, Pallas kernels, attn_bwd(): pl.pallas_call(kern, grid=(npair,), in_specs=[pl.BlockSpec(memory_space=p...  32.2 us
    reduce_scatter x1, waiting for transfers between devices, local(): lax.psum_scatter(grad_wo.astype(BF), 'shard', scatter_dimension=0, tiled=...  29.4 us
    all_gather x1, waiting for transfers between devices, local(): lax.all_gather(jnp.concatenate([w_qkv[:, :width], w_qkv[:, width:2 * widt...  29.1 us
  transfers between devices with their start and end apart: 19, of which 15 were waited for; matrix products, arithmetic and copies ran while one was open for 8% of the time, Pallas kernels for 6%

profile of v1, /device:TPU:16, one launch (start us, length us, event | category | flops | bytes accessed | tf_op | source)
XLA Modules:
  0.0 554.4 jit_solution(17381340117087739133)
XLA Ops:
  8.3 1.1 fusion.17
  12.7 12.3 %all-gather.2 = bf16[8,1,1280]{2,1,0:T(2,128)(2,1)S(1)} all-gather(bf16[1,1,1280]{2,1,0:T(2,128)(2,1)S(1)} %reshape.133), channel_id=3, replica_groups=mesh['rep'=4,'shard'=8] {'shard'}, dimensions={0}, use_global_device_ids=true | all-gather | bytes 23040 | tf_op jit(solution)/shard_map/all_gather | solution.py:412
  26.3 1.6 collective-permute-start
  27.9 2.0 collective-permute-done
  30.6 1.6 collective-permute-start.1
  36.2 29.1 %all-gather.14.cloned.1.call-done = bf16[3328,768]{1,0:T(8,128)(2,1)} async-done(((bf16[416,768]{1,0:T(8,128)(2,1)}), bf16[3328,768]{1,0:T(8,128)(2,1)}) %all-gather.14.cloned.1.call-update) | async-done | bytes 5111824 | tf_op jit(solution)/shard_map/all_gather | solution.py:396
  65.3 10.0 %qkv.1 = (bf16[1536,768]{1,0:T(8,128)(2,1)}, bf16[640,768]{1,0:T(8,128)(2,1)}, bf16[1536,768]{1,0:T(8,128)(2,1)}, bf16[1536,768]{1,0:T(8,128)(2,1)}) custom-call(s32[1]{0:T(128)} %bitcast.sh_ref, bf16[8,416,768]{2,1,0:T(8,128)(2,1)} %bitcast.32, bf16[640,768]{1,0:T(8,128)(2,1)} %t_ref.5, f32[8,768]{1,0:T(8,128)} %stack.11.vec_ref), custom_call_target="tpu_custom_call" | custom-call | flops 4378853376 | bytes 14155776 | tf_op jit(solution)/shard_map/qkv/pallas_call | solution.py:98
  75.3 23.0 %attn_fwd.1 = (bf16[640,768]{1,0:T(8,128)(2,1)}, f32[6,2,640]{2,1,0:T(2,128)}) custom-call(s32[1]{0:T(128)} %bitcast.sh_ref, bf16[640,768]{1,0:T(8,128)(2,1)} %get-tuple-element.26.q_ref, bf16[1536,768]{1,0:T(8,128)(2,1)} %get-tuple-element.27.k_ref, bf16[1536,768]{1,0:T(8,128)(2,1)} %get-tuple-element.28.v_ref), custom_call_target="tpu_custom_call" | custom-call | flops 12079595520 | bytes 6684672 | tf_op jit(solution)/shard_map/attn_fwd/pallas_call | solution.py:147
  98.3 2.7 fusion.21
  101.4 39.7 %all-gather.10.cloned.1.call-done = bf16[768,3072]{1,0:T(8,128)(2,1)} async-done(((bf16[96,3072]{1,0:T(8,128)(2,1)}), bf16[768,3072]{1,0:T(8,128)(2,1)}) %all-gather.10.cloned.1.call-update) | async-done | bytes 4718608 | tf_op jit(solution)/shard_map/all_gather | solution.py:422
  141.1 7.9 %fusion.10 = f32[640,3072]{1,0:T(8,128)} fusion(bf16[768,3072]{1,0:T(8,128)(2,1)} %all-gather.10.cloned.1.call-done, f32[640,768]{1,0:T(8,128)S(1)} %get-tuple-element.74, f32[768]{0:T(1024)S(1)} %add.122, f32[768]{0:T(1024)S(1)} %mul.127, f32[640]{0:T(1024)S(1)} %fusion.7, f32[640]{0:T(1024)S(1)} %broadcast_multiply_fusion), kind=kOutput, calls=%fused_computation.54 | convolution fusion | flops 3022356480 | bytes 14560256 | tf_op jit(solution)/shard_map/dot_general | solution.py:24
  149.0 43.6 %all-gather.12.cloned.1.call-done = bf16[3072,768]{1,0:T(8,128)(2,1)} async-done(((bf16[384,768]{1,0:T(8,128)(2,1)}), bf16[3072,768]{1,0:T(8,128)(2,1)}) %all-gather.12.cloned.1.call-update) | async-done | bytes 4718608 | tf_op jit(solution)/shard_map/all_gather | solution.py:423
  192.6 10.6 %fusion.22 = (bf16[640,768]{1,0:T(8,128)(2,1)}, f32[640,768]{1,0:T(8,128)S(1)}) fusion(f32[768]{0:T(1024)S(1)} %add.131, f32[640,768]{1,0:T(8,128)S(1)} %get-tuple-element.74, bf16[3072,768]{1,0:T(8,128)(2,1)} %all-gather.12.cloned.1.call-done, f32[640,3072]{1,0:T(8,128)} %fusion.10, f32[3072]{0:T(1024)S(1)} %add.125), kind=kOutput, calls=%fused_computation.64 | convolution fusion | flops 3041034240 | bytes 17513472 | tf_op jit(solution)/shard_map/dot_general | solution.py:24
  204.4 2.1 copy-done.19
  206.5 10.5 %fusion.13 = (bf16[3072]{0:T(1024)(128)(2,1)S(1)}, bf16[640,3072]{1,0:T(8,128)(2,1)}) fusion(f32[640,3072]{1,0:T(8,128)S(1)} %copy-done.21, f32[3072]{0:T(1024)S(1)} %add.125, bf16[640,768]{1,0:T(8,128)(2,1)S(1)} %get-tuple-element.46, bf16[3072,768]{1,0:T(8,128)(2,1)S(1)} %copy-done.19), kind=kOutput, calls=%fused_computation.56 | convolution fusion | flops 3071013888 | bytes 17516544 | tf_op jit(solution)/shard_map/dot_general | solution.py:20
  217.1 8.3 %multiply_reduce_fusion = (bf16[768]{0:T(1024)(128)(2,1)S(1)}, f32[640]{0:T(1024)S(1)}, bf16[768]{0:T(1024)(128)(2,1)S(1)}, f32[640,768]{1,0:T(8,128)}) fusion(f32[640,768]{1,0:T(8,128)S(1)} %get-tuple-element.74, f32[640]{0:T(1024)S(1)} %fusion.7, f32[640]{0:T(1024)S(1)} %broadcast_multiply_fusion, f32[768]{0:T(1024)S(1)} %mul.127, ...), kind=kOutput, calls=%fused_computation.14 | convolution fusion | flops 3023828736 | bytes 12596736 | tf_op jit(solution)/shard_map/dot_general | solution.py:20
  225.5 2.4 fusion.15
  228.0 1.8 convert_reduce_fusion
  230.0 3.8 convolution_convert_fusion.3.do_ref
  233.8 32.2 %attn_bwd.1 = (bf16[640,768]{1,0:T(8,128)(2,1)}, bf16[1536,768]{1,0:T(8,128)(2,1)}, bf16[1536,768]{1,0:T(8,128)(2,1)}) custom-call(s32[1]{0:T(128)} %bitcast.sh_ref, bf16[640,768]{1,0:T(8,128)(2,1)} %get-tuple-element.26.q_ref, bf16[1536,768]{1,0:T(8,128)(2,1)} %get-tuple-element.27.k_ref, bf16[1536,768]{1,0:T(8,128)(2,1)} %get-tuple-element.28.v_ref, ...), custom_call_target="tpu_custom_call" | custom-call | flops 30198988800 | bytes 13369344 | tf_op jit(solution)/shard_map/attn_bwd/pallas_call | solution.py:215
  266.0 12.9 %dh1.1 = (bf16[1024,768]{1,0:T(8,128)(2,1)}, f32[640,768]{1,0:T(8,128)}, f32[8,768]{1,0:T(8,128)}) custom-call(s32[1]{0:T(128)} %bitcast.sh_ref, bf16[8,416,768]{2,1,0:T(8,128)(2,1)} %bitcast.33, bf16[640,768]{1,0:T(8,128)(2,1)} %t_ref.5, f32[8,768]{1,0:T(8,128)} %stack.11.vec_ref, bf16[640,768]{1,0:T(8,128)(2,1)} %get-tuple-element.31.dq_ref, ...), custom_call_target="tpu_custom_call" | custom-call | flops 4378853376 | bytes 14155776 | tf_op jit(solution)/shard_map/dh1/pallas_call | solution.py:289
  280.9 10.0 %grad_wqkv.1 = bf16[8,304,768]{2,1,0:T(8,128)(2,1)} custom-call(s32[1]{0:T(128)} %bitcast.sh_ref, bf16[1536,768]{1,0:T(8,128)(2,1)} %get-tuple-element.36.h_ref, bf16[640,768]{1,0:T(8,128)(2,1)} %get-tuple-element.31.dq_ref, bf16[1536,768]{1,0:T(8,128)(2,1)} %get-tuple-element.32.dk_ref, bf16[1536,768]{1,0:T(8,128)(2,1)} %get-tuple-element.33.dv_ref, ...), custom_call_target="tpu_custom_call" | custom-call | flops 4378853376 | bytes 9437184 | tf_op jit(solution)/shard_map/grad_wqkv/pallas_call | solution.py:324
  290.9 1.1 copy-done.20
  292.1 3.7 convolution_convert_fusion.2
  297.0 10.6 %convolution_convert_fusion = bf16[3072,768]{1,0:T(8,128)(2,1)} fusion(bf16[640,768]{1,0:T(8,128)(2,1)S(1)} %copy-done.7, f32[640,3072]{1,0:T(8,128)} %fusion.10, f32[3072]{0:T(1024)S(1)} %add.125), kind=kOutput, calls=%fused_computation.11 | convolution fusion | flops 3041918976 | bytes 13578240 | tf_op jit(solution)/shard_map/dot_general | solution.py:28
  307.6 7.9 %convolution_convert_fusion.1 = bf16[768,3072]{1,0:T(8,128)(2,1)} fusion(bf16[640,3072]{1,0:T(8,128)(2,1)} %get-tuple-element.48, f32[640,768]{1,0:T(8,128)S(1)} %get-tuple-element.74, f32[768]{0:T(1024)S(1)} %add.122, f32[768]{0:T(1024)S(1)} %mul.127, f32[640]{0:T(1024)S(1)} %fusion.7, f32[640]{0:T(1024)S(1)} %broadcast_multiply_fusion), kind=kOutput, calls=%fused_computation.12 | convolution fusion | flops 3024715776 | bytes 10628096 | tf_op jit(solution)/shard_map/dot_general | solution.py:28
  315.6 18.1 %reduce-scatter.8.cloned.1.call-done = bf16[304,768]{1,0:T(8,128)(2,1)} async-done(((bf16[2432,768]{1,0:T(8,128)(2,1)}), bf16[304,768]{1,0:T(8,128)(2,1)}) %reduce-scatter.8.cloned.1.call-update) | async-done | bytes 466960 | tf_op jit(solution)/shard_map/reduce_scatter | solution.py:477
  333.7 1.5 collective-permute-start.2
  335.2 29.4 %reduce-scatter.10.cloned.1.call-done = bf16[96,768]{1,0:T(8,128)(2,1)} async-done(((bf16[768,768]{1,0:T(8,128)(2,1)}), bf16[96,768]{1,0:T(8,128)(2,1)}) %reduce-scatter.10.cloned.1.call-update) | async-done | bytes 147472 | tf_op jit(solution)/shard_map/reduce_scatter | solution.py:455
  364.6 1.4 collective-permute-start.4
  365.9 1.2 add_convert_fusion.3
  367.1 1.6 collective-permute-start.3
  368.7 2.5 collective-permute-done.4
  372.1 1.4 collective-permute-start.5
  373.5 10.2 %collective-permute-done.5 = bf16[96,768]{1,0:T(8,128)(2,1)S(1)} collective-permute-done((bf16[96,768]{1,0:T(8,128)(2,1)S(1)}, bf16[96,768]{1,0:T(8,128)(2,1)S(1)}, u32[]{:S(2)}, u32[]{:S(2)}) %collective-permute-start.5) | collective-permute-done | bytes 147488 | tf_op jit(solution)/shard_map/ppermute | solution.py:364
  384.4 14.5 %reduce-scatter.6.cloned.1.call-done.s_ref = bf16[128,768]{1,0:T(8,128)(2,1)} async-done(((bf16[1024,768]{1,0:T(8,128)(2,1)}), bf16[128,768]{1,0:T(8,128)(2,1)}) %reduce-scatter.6.cloned.1.call-update) | async-done | bytes 196624 | tf_op jit(solution)/shard_map/reduce_scatter | solution.py:460
  398.9 2.2 finish.1
  401.1 57.5 %reduce-scatter.14.cloned.1.call-done = bf16[384,768]{1,0:T(8,128)(2,1)} async-done(((bf16[3072,768]{1,0:T(8,128)(2,1)}), bf16[384,768]{1,0:T(8,128)(2,1)}) %reduce-scatter.14.cloned.1.call-update) | async-done | bytes 589840 | tf_op jit(solution)/shard_map/reduce_scatter | solution.py:442
  458.6 1.5 collective-permute-start.8
  460.2 54.1 %reduce-scatter.12.cloned.1.call-done = bf16[96,3072]{1,0:T(8,128)(2,1)} async-done(((bf16[768,3072]{1,0:T(8,128)(2,1)}), bf16[96,3072]{1,0:T(8,128)(2,1)}) %reduce-scatter.12.cloned.1.call-update) | async-done | bytes 589840 | tf_op jit(solution)/shard_map/reduce_scatter | solution.py:448
  514.3 1.5 collective-permute-start.6
  517.8 1.5 collective-permute-start.9
  519.4 11.1 %collective-permute-done.6 = bf16[96,3072]{1,0:T(8,128)(2,1)S(1)} collective-permute-done((bf16[96,3072]{1,0:T(8,128)(2,1)}, bf16[96,3072]{1,0:T(8,128)(2,1)S(1)}, u32[]{:S(2)}, u32[]{:S(2)}) %collective-permute-start.6) | collective-permute-done | bytes 589856 | tf_op jit(solution)/shard_map/ppermute | solution.py:364
  530.6 1.5 collective-permute-start.7
  533.1 1.0 collective-permute-done.9
  534.1 1.1 convert_add_fusion
  535.2 11.0 %collective-permute-done.7 = bf16[96,3072]{1,0:T(8,128)(2,1)S(1)} collective-permute-done((bf16[96,3072]{1,0:T(8,128)(2,1)S(1)}, bf16[96,3072]{1,0:T(8,128)(2,1)S(1)}, u32[]{:S(2)}, u32[]{:S(2)}) %collective-permute-start.7) | collective-permute-done | bytes 589856 | tf_op jit(solution)/shard_map/ppermute | solution.py:364
  546.3 1.2 convert_add_fusion.1
  (124 shorter events, 19.8 us)
Async XLA Ops:
  7.2 58.1 %all-gather.14.cloned.1.call-start = ((), (), s32[]{:S(2)}) async-start(), calls=%async_computation.13 | async-start | bytes 5750784 | tf_op jit(solution)/shard_map/all_gather | solution.py:396
  8.2 4.2 copy-start.10
  8.2 4.4 copy-start.11
  8.2 4.3 copy-start.12
  8.2 4.3 copy-start.13
  8.2 4.3 copy-start.14
  8.2 4.3 copy-start.15
  8.2 4.3 copy-start.16
  8.3 4.3 copy-start.17
  8.3 4.3 copy-start.18
  10.3 88.0 %all-gather.8.cloned.1.call-start = ((), (), s32[]{:S(2)}) async-start(), calls=%async_computation.5 | async-start | bytes 1327104 | tf_op jit(solution)/shard_map/all_gather | solution.py:421
  11.1 130.0 %all-gather.10.cloned.1.call-start = ((), (), s32[]{:S(2)}) async-start(), calls=%async_computation.6 | async-start | bytes 5308416 | tf_op jit(solution)/shard_map/all_gather | solution.py:422
  11.8 180.8 %all-gather.12.cloned.1.call-start = ((), (), s32[]{:S(2)}) async-start(), calls=%async_computation.7 | async-start | bytes 5308416 | tf_op jit(solution)/shard_map/all_gather | solution.py:423
  12.4 321.4 %reduce-scatter.8.cloned.1.call-start = ((), (), s32[]{:S(2)}) async-start(), calls=%async_computation.9 | async-start | bytes 4202496 | tf_op jit(solution)/shard_map/reduce_scatter | solution.py:477
  26.3 3.7 collective-permute-start
  30.6 3.7 collective-permute-start.1
  75.3 23.0 %copy-start.5 = (bf16[640,768]{1,0:T(8,128)(2,1)S(1)}, bf16[640,768]{1,0:T(8,128)(2,1)}, u32[]{:S(2)}) copy-start(bf16[640,768]{1,0:T(8,128)(2,1)} %t_ref.5) | copy-start | bytes 2949124
  149.0 54.2 %copy-start.2 = (bf16[640,768]{1,0:T(8,128)(2,1)S(1)}, bf16[640,768]{1,0:T(8,128)(2,1)}, u32[]{:S(2)}) copy-start(bf16[640,768]{1,0:T(8,128)(2,1)} %param.29) | copy-start | bytes 2949124
  192.6 10.6 %copy-start.3 = (bf16[640,768]{1,0:T(8,128)(2,1)S(1)}, bf16[640,768]{1,0:T(8,128)(2,1)}, u32[]{:S(2)}) copy-start(bf16[640,768]{1,0:T(8,128)(2,1)} %param.30) | copy-start | bytes 2949124
  192.6 11.9 %copy-start.21 = (f32[640,3072]{1,0:T(8,128)S(1)}, f32[640,3072]{1,0:T(8,128)}, u32[]{:S(2)}) copy-start(f32[640,3072]{1,0:T(8,128)} %fusion.10) | copy-start | bytes 23592964
  203.1 1.3 copy-start
  203.1 3.4 copy-start.19
  204.4 12.6 %copy-start.6 = (bf16[640,768]{1,0:T(8,128)(2,1)}, bf16[640,768]{1,0:T(8,128)(2,1)S(1)}, u32[]{:S(2)}) copy-start(bf16[640,768]{1,0:T(8,128)(2,1)S(1)} %get-tuple-element.46) | copy-start | bytes 2949124
  225.5 2.4 copy-start.1
  225.5 2.4 copy-start.4
  290.9 1.2 copy-start.20
  290.9 73.7 %reduce-scatter.10.cloned.1.call-start = ((), (), s32[]{:S(2)}) async-start(), calls=%async_computation.10 | async-start | bytes 1327104 | tf_op jit(solution)/shard_map/reduce_scatter | solution.py:455
  295.8 1.2 copy-start.7
  295.8 103.1 %reduce-scatter.6.cloned.1.call-start = ((), (), s32[]{:S(2)}) async-start(), calls=%async_computation.8 | async-start | bytes 1769472 | tf_op jit(solution)/shard_map/reduce_scatter | solution.py:460
  296.5 162.1 %reduce-scatter.14.cloned.1.call-start = ((), (), s32[]{:S(2)}) async-start(), calls=%async_computation.12 | async-start | bytes 5308416 | tf_op jit(solution)/shard_map/reduce_scatter | solution.py:442
  307.6 206.7 %reduce-scatter.12.cloned.1.call-start = ((), (), s32[]{:S(2)}) async-start(), calls=%async_computation.11 | async-start | bytes 5308416 | tf_op jit(solution)/shard_map/reduce_scatter | solution.py:448
  333.7 32.2 %collective-permute-start.2 = (bf16[304,768]{1,0:T(8,128)(2,1)}, bf16[304,768]{1,0:T(8,128)(2,1)S(1)}, u32[]{:S(2)}, u32[]{:S(2)}) collective-permute-start(bf16[304,768]{1,0:T(8,128)(2,1)} %reduce-scatter.8.cloned.1.call-done), channel_id=1, source_target_pairs={{0,8},{8,0},{16,24},{24,16},{1,9},{9,1},{17,25},{25,17},{2,10},{10... | collective-permute-start | bytes 1400840 | tf_op jit(solution)/shard_map/ppermute | solution.py:364
  364.6 6.6 %collective-permute-start.4 = (bf16[96,768]{1,0:T(8,128)(2,1)}, bf16[96,768]{1,0:T(8,128)(2,1)S(1)}, u32[]{:S(2)}, u32[]{:S(2)}) collective-permute-start(bf16[96,768]{1,0:T(8,128)(2,1)} %reduce-scatter.10.cloned.1.call-done), channel_id=1, source_target_pairs={{0,8},{8,0},{16,24},{24,16},{1,9},{9,1},{17,25},{25,17},{2,10},{10... | collective-permute-start | bytes 442376 | tf_op jit(solution)/shard_map/ppermute | solution.py:364
  367.1 93.0 %collective-permute-start.3 = (bf16[304,768]{1,0:T(8,128)(2,1)S(1)}, bf16[304,768]{1,0:T(8,128)(2,1)S(1)}, u32[]{:S(2)}, u32[]{:S(2)}) collective-permute-start(bf16[304,768]{1,0:T(8,128)(2,1)S(1)} %add_convert_fusion.3), channel_id=1, source_target_pairs={{0,16},{8,24},{16,0},{24,8},{1,17},{9,25},{17,1},{25,9},{2,18},{10... | collective-permute-start | bytes 1400840 | tf_op jit(solution)/shard_map/ppermute | solution.py:364
  372.1 11.5 %collective-permute-start.5 = (bf16[96,768]{1,0:T(8,128)(2,1)S(1)}, bf16[96,768]{1,0:T(8,128)(2,1)S(1)}, u32[]{:S(2)}, u32[]{:S(2)}) collective-permute-start(bf16[96,768]{1,0:T(8,128)(2,1)S(1)} %add_convert_fusion.4), channel_id=1, source_target_pairs={{0,16},{8,24},{16,0},{24,8},{1,17},{9,25},{17,1},{25,9},{2,18},{10... | collective-permute-start | bytes 442376 | tf_op jit(solution)/shard_map/ppermute | solution.py:364
  458.6 59.1 %copy-start.8 = (bf16[384,768]{1,0:T(8,128)(2,1)S(1)}, bf16[384,768]{1,0:T(8,128)(2,1)}, u32[]{:S(2)}) copy-start(bf16[384,768]{1,0:T(8,128)(2,1)} %reduce-scatter.14.cloned.1.call-done) | copy-start | bytes 1769476
  458.6 59.1 %collective-permute-start.8 = (bf16[384,768]{1,0:T(8,128)(2,1)}, bf16[384,768]{1,0:T(8,128)(2,1)S(1)}, u32[]{:S(2)}, u32[]{:S(2)}) collective-permute-start(bf16[384,768]{1,0:T(8,128)(2,1)} %reduce-scatter.14.cloned.1.call-done), channel_id=1, source_target_pairs={{0,8},{8,0},{16,24},{24,16},{1,9},{9,1},{17,25},{25,17},{2,10},{10... | collective-permute-start | bytes 1769480 | tf_op jit(solution)/shard_map/ppermute | solution.py:364
  514.3 16.2 %copy-start.9 = (bf16[96,3072]{1,0:T(8,128)(2,1)S(1)}, bf16[96,3072]{1,0:T(8,128)(2,1)}, u32[]{:S(2)}) copy-start(bf16[96,3072]{1,0:T(8,128)(2,1)} %reduce-scatter.12.cloned.1.call-done) | copy-start | bytes 1769476
  514.3 16.2 %collective-permute-start.6 = (bf16[96,3072]{1,0:T(8,128)(2,1)}, bf16[96,3072]{1,0:T(8,128)(2,1)S(1)}, u32[]{:S(2)}, u32[]{:S(2)}) collective-permute-start(bf16[96,3072]{1,0:T(8,128)(2,1)} %reduce-scatter.12.cloned.1.call-done), channel_id=1, source_target_pairs={{0,8},{8,0},{16,24},{24,16},{1,9},{9,1},{17,25},{25,17},{2,10},{10... | collective-permute-start | bytes 1769480 | tf_op jit(solution)/shard_map/ppermute | solution.py:364
  517.8 16.3 %collective-permute-start.9 = (bf16[384,768]{1,0:T(8,128)(2,1)S(1)}, bf16[384,768]{1,0:T(8,128)(2,1)S(1)}, u32[]{:S(2)}, u32[]{:S(2)}) collective-permute-start(bf16[384,768]{1,0:T(8,128)(2,1)S(1)} %add_convert_fusion.1), channel_id=1, source_target_pairs={{0,16},{8,24},{16,0},{24,8},{1,17},{9,25},{17,1},{25,9},{2,18},{10... | collective-permute-start | bytes 1769480 | tf_op jit(solution)/shard_map/ppermute | solution.py:364
  530.6 15.7 %collective-permute-start.7 = (bf16[96,3072]{1,0:T(8,128)(2,1)S(1)}, bf16[96,3072]{1,0:T(8,128)(2,1)S(1)}, u32[]{:S(2)}, u32[]{:S(2)}) collective-permute-start(bf16[96,3072]{1,0:T(8,128)(2,1)S(1)} %add_convert_fusion.2), channel_id=1, source_target_pairs={{0,16},{8,24},{16,0},{24,8},{1,17},{9,25},{17,1},{25,9},{2,18},{10... | collective-permute-start | bytes 1769480 | tf_op jit(solution)/shard_map/ppermute | solution.py:364
Sparse Core Ops, SparseCore 0:
  10.4 54.8 all-gather.13
  66.9 22.2 all-gather.7
  90.9 50.1 all-gather.9
  142.6 49.9 all-gather.11
  291.0 42.6 reduce-scatter.7
  336.4 28.0 reduce-scatter.9
  366.9 31.9 reduce-scatter.5
  401.2 57.3 reduce-scatter.13
  460.9 53.3 reduce-scatter.11

commit v2 on v1

v2 whole, which is shorter than its diff:
```python
import jax
import jax.numpy as jnp
from jax import lax
from jax.experimental import pallas as pl
from jax.experimental.pallas import tpu as pltpu
from jax.sharding import PartitionSpec as P

F32 = jnp.float32
BF = jnp.bfloat16
HEAD = 64
PR_DEV = 128
PAIR = 2 * HEAD
SCALE = 0.125
EPS = 1e-05
NEG = -1e30
VMEM_LIMIT = 60 * 1024 * 1024
EXTRA = 16


def dot_nt(a, b):
    return lax.dot_general(a, b, (((1,), (1,)), ((), ())), preferred_element_type=F32)


def dot_nn(a, b):
    return lax.dot_general(a, b, (((1,), (0,)), ((), ())), preferred_element_type=F32)


def dot_tn(a, b):
    return lax.dot_general(a, b, (((0,), (0,)), ((), ())), preferred_element_type=F32)


def normalize(values):
    centered = values - jnp.mean(values, axis=-1, keepdims=True)
    inv = lax.rsqrt(jnp.mean(centered * centered, axis=-1, keepdims=True) + EPS)
    return centered * inv, inv


def norm_back(e, z, inv):
    return inv * (
        e - jnp.mean(e, axis=-1, keepdims=True) - z * jnp.mean(e * z, axis=-1, keepdims=True)
    )


def cost(flops, nbytes, trans=0):
    return pl.CostEstimate(flops=int(flops), bytes_accessed=int(nbytes), transcendentals=int(trans))


def fixed(shape):
    return pl.BlockSpec(shape, lambda *_: (0,) * len(shape))


def qkv_call(bundle, tokens, vecs, shard):
    ns, _, width = bundle.shape
    tok = tokens.shape[0]
    cont = tok - PR_DEV
    plen = ns * PR_DEV
    keys = plen + cont
    dsh = width // ns
    step = cont // PR_DEV
    chunks = ns // step

    def kern(sh_ref, g_ref, t_ref, vec_ref, h_ref, q_ref, k_ref, v_ref, x_ref):
        i = pl.program_id(0)
        gain, bias, bq, bv = vec_ref[0:1], vec_ref[1:2], vec_ref[2:3], vec_ref[3:4]
        wq, wk, wv = (
            g_ref[:, j * dsh : (j + 1) * dsh, :].reshape(width, width) for j in range(3)
        )

        def to_q(h):
            return ((dot_nn(h, wq) + bq).astype(BF).astype(F32) * SCALE).astype(BF)

        @pl.when(i < chunks)
        def _():
            x = g_ref[pl.ds(i * step, step), 3 * dsh : 3 * dsh + PR_DEV, :]
            x_ref[...] = x.reshape(cont, width)

        @pl.when(i == chunks)
        def _():
            x_ref[...] = t_ref[PR_DEV:, :]

        h = (normalize(x_ref[...].astype(F32))[0] * gain + bias).astype(BF)
        h_ref[...] = h
        k_ref[...] = dot_nn(h, wk).astype(BF)
        v_ref[...] = (dot_nn(h, wv) + bv).astype(BF)

        @pl.when(i == sh_ref[0] // step)
        def _():
            own = pl.multiple_of((sh_ref[0] % step) * PR_DEV, PR_DEV)
            q_ref[:PR_DEV, :] = to_q(h_ref[pl.ds(own, PR_DEV), :])

        @pl.when(i == chunks)
        def _():
            q_ref[PR_DEV:, :] = to_q(h_ref[...])

    shape = lambda r: jax.ShapeDtypeStruct((r, width), BF)
    rows = pl.BlockSpec((cont, width), lambda i: (i, 0))
    return pl.pallas_call(
        kern,
        grid=(chunks + 1,),
        in_specs=[
            pl.BlockSpec(memory_space=pltpu.SMEM),
            fixed(bundle.shape),
            fixed(tokens.shape),
            fixed(vecs.shape),
        ],
        out_specs=[rows, fixed((tok, width)), rows, rows],
        out_shape=[shape(keys), shape(tok), shape(keys), shape(keys)],
        scratch_shapes=[pltpu.VMEM((cont, width), BF)],
        compiler_params=pltpu.CompilerParams(vmem_limit_bytes=VMEM_LIMIT),
        cost_estimate=cost(2 * width * width * (2 * keys + tok), 2 * width * (6 * keys)),
        name="qkv",
    )(shard, bundle, tokens, vecs)


def attn_fwd(q, k, v, shard, rb):
    tok, width = q.shape
    keys = k.shape[0]
    cont = tok - PR_DEV
    plen = keys - cont
    npair = width // PAIR

    def kern(sh_ref, q_ref, k_ref, v_ref, o_ref, lse_ref):
        sh = sh_ref[0]
        first = lax.broadcasted_iota(jnp.int32, (1, PAIR), 1) < HEAD

        def block(r0, rows, n, offset, masked):
            outs, lses = [], []
            for h in range(2):
                mine = first if h == 0 else jnp.logical_not(first)
                qq = jnp.where(mine, q_ref[pl.ds(r0, rows), :], 0).astype(BF)
                s = dot_nt(qq, k_ref[pl.ds(0, n), :])
                tail = s[:, n - masked :]
                row = lax.broadcasted_iota(jnp.int32, tail.shape, 0)
                col = lax.broadcasted_iota(jnp.int32, tail.shape, 1)
                tail = jnp.where(col <= row + offset, tail, NEG)
                s = tail if masked == n else jnp.concatenate([s[:, : n - masked], tail], axis=1)
                top = jnp.max(s, axis=1, keepdims=True)
                p = jnp.exp(s - top)
                total = jnp.sum(p, axis=1, keepdims=True)
                outs.append(dot_nn(p.astype(BF), v_ref[pl.ds(0, n), :]) * (1.0 / total))
                lses.append(top + jnp.log(total))
            o_ref[pl.ds(r0, rows), :] = jnp.where(first, outs[0], outs[1]).astype(BF)
            turned = jnp.transpose(jnp.where(first, lses[0], lses[1]))
            lse_ref[0, 0:1, pl.ds(r0, rows)] = turned[0:1]
            lse_ref[0, 1:2, pl.ds(r0, rows)] = turned[HEAD : HEAD + 1]

        block(0, PR_DEV, plen, sh * PR_DEV, plen)
        for i in range(cont // rb):
            block(PR_DEV + i * rb, rb, plen + (i + 1) * rb, 0, rb)

    spq = pl.BlockSpec((tok, PAIR), lambda i: (0, i))
    spk = pl.BlockSpec((keys, PAIR), lambda i: (0, i))
    return pl.pallas_call(
        kern,
        grid=(npair,),
        in_specs=[pl.BlockSpec(memory_space=pltpu.SMEM), spq, spk, spk],
        out_specs=[spq, pl.BlockSpec((1, 2, tok), lambda i: (i, 0, 0))],
        out_shape=[
            jax.ShapeDtypeStruct((tok, width), BF),
            jax.ShapeDtypeStruct((npair, 2, tok), F32),
        ],
        compiler_params=pltpu.CompilerParams(vmem_limit_bytes=VMEM_LIMIT),
        cost_estimate=cost(16 * width * tok * keys, 4 * width * (tok + keys)),
        name="attn_fwd",
    )(shard, q, k, v)


def attn_bwd(q, k, v, o, do, lse, shard, rb):
    tok, width = q.shape
    keys = k.shape[0]
    cont = tok - PR_DEV
    plen = keys - cont
    npair = width // PAIR

    def kern(sh_ref, q_ref, k_ref, v_ref, o_ref, do_ref, lse_ref, dq_ref, dkv_ref, ka, va):
        sh = sh_ref[0]
        first = lax.broadcasted_iota(jnp.int32, (1, PAIR), 1) < HEAD
        ka[...] = jnp.zeros_like(ka)
        va[...] = jnp.zeros_like(va)
        hr = lax.broadcasted_iota(jnp.int32, (8, PAIR), 0)
        hc = lax.broadcasted_iota(jnp.int32, (8, PAIR), 1)
        pick = jnp.where(hc // HEAD == hr, 1.0, 0.0).astype(F32)

        def block(r0, rows, n, offset, masked):
            prod = o_ref[pl.ds(r0, rows), :].astype(F32) * do_ref[pl.ds(r0, rows), :].astype(F32)
            row_dot = lax.dot_general(
                pick,
                prod,
                (((1,), (1,)), ((), ())),
                precision=lax.Precision.HIGHEST,
                preferred_element_type=F32,
            )
            dqs = []
            for h in range(2):
                mine = first if h == 0 else jnp.logical_not(first)
                qq = jnp.where(mine, q_ref[pl.ds(r0, rows), :], 0).astype(BF)
                gg = jnp.where(mine, do_ref[pl.ds(r0, rows), :], 0).astype(BF)
                kk = k_ref[pl.ds(0, n), :]
                s = dot_nt(kk, qq)
                tail = s[n - masked :]
                col = lax.broadcasted_iota(jnp.int32, tail.shape, 0)
                row = lax.broadcasted_iota(jnp.int32, tail.shape, 1)
                tail = jnp.where(col <= row + offset, tail, NEG)
                s = tail if masked == n else jnp.concatenate([s[: n - masked], tail], axis=0)
                p = jnp.exp(s - lse_ref[0, h : h + 1, pl.ds(r0, rows)])
                dp = dot_nt(v_ref[pl.ds(0, n), :], gg)
                ds = (p * (dp - row_dot[h : h + 1, :])).astype(BF)
                va[pl.ds(0, n), :] += dot_nn(p.astype(BF), gg)
                ka[pl.ds(0, n), :] += dot_nn(ds, qq)
                dqs.append(dot_tn(ds, kk))
            dq_ref[pl.ds(r0, rows), :] = (jnp.where(first, dqs[0], dqs[1]) * SCALE).astype(BF)

        block(0, PR_DEV, plen, sh * PR_DEV, plen)
        for i in range(cont // rb):
            block(PR_DEV + i * rb, rb, plen + (i + 1) * rb, 0, rb)
        dkv_ref[0] = ka[...].astype(BF)
        dkv_ref[1] = va[...].astype(BF)

    spq = pl.BlockSpec((tok, PAIR), lambda i: (0, i))
    spk = pl.BlockSpec((keys, PAIR), lambda i: (0, i))
    return pl.pallas_call(
        kern,
        grid=(npair,),
        in_specs=[
            pl.BlockSpec(memory_space=pltpu.SMEM),
            spq,
            spk,
            spk,
            spq,
            spq,
            pl.BlockSpec((1, 2, tok), lambda i: (i, 0, 0)),
        ],
        out_specs=[spq, pl.BlockSpec((2, keys, PAIR), lambda i: (0, 0, i))],
        out_shape=[
            jax.ShapeDtypeStruct((tok, width), BF),
            jax.ShapeDtypeStruct((2, keys, width), BF),
        ],
        scratch_shapes=[pltpu.VMEM((keys, PAIR), F32), pltpu.VMEM((keys, PAIR), F32)],
        compiler_params=pltpu.CompilerParams(vmem_limit_bytes=VMEM_LIMIT),
        cost_estimate=cost(40 * width * tok * keys, 8 * width * (tok + keys)),
        name="attn_bwd",
    )(shard, q, k, v, o, do, lse)


def out_proj_call(mix, second, tokens, vecs):
    ns, _, width = second.shape
    tok = tokens.shape[0]
    dsh = width // ns

    def kern(o_ref, w_ref, t_ref, vec_ref, x_ref, h_ref):
        wo = w_ref[...].reshape(width, width)
        x1 = t_ref[...].astype(F32) + (dot_nn(o_ref[...], wo) + vec_ref[4:5])
        x_ref[...] = x1
        h_ref[...] = (normalize(x1)[0] * vec_ref[5:6] + vec_ref[6:7]).astype(BF)

    whole = lambda a: pl.BlockSpec(a.shape, lambda i: (0,) * a.ndim)
    return pl.pallas_call(
        kern,
        grid=(1,),
        in_specs=[
            whole(mix),
            pl.BlockSpec((ns, dsh, width), lambda i: (0, 1, 0)),
            whole(tokens),
            whole(vecs),
        ],
        out_specs=[pl.BlockSpec((tok, width), lambda i: (0, 0))] * 2,
        out_shape=[jax.ShapeDtypeStruct((tok, width), F32), jax.ShapeDtypeStruct((tok, width), BF)],
        compiler_params=pltpu.CompilerParams(vmem_limit_bytes=VMEM_LIMIT),
        cost_estimate=cost(2 * width * width * tok, 12 * width * tok),
        name="out_proj",
    )(mix, second, tokens, vecs)


def fc_call(h2, second, got, other, vecs, where):
    ns, _, width = second.shape
    tok = h2.shape[0]
    dsh = width // ns
    half = ns // 2
    nq = len(got) + 1

    def kern(*refs):
        wh_ref, h_ref, own_ref = refs[:3]
        got_refs = refs[3 : 2 + nq]
        other_refs = refs[2 + nq : 1 + 2 * nq]
        vec_ref, g_ref, gp_ref, w_ref = refs[1 + 2 * nq :]
        me, core = wh_ref[0], wh_ref[1]
        step = pl.program_id(0)
        rows = half * dsh

        @pl.when(step == 0)
        def _():
            w_ref[0] = own_ref[...].reshape(width, width)

        for j in range(1, nq):

            @pl.when(step == j)
            def _():
                first = pl.multiple_of(core * rows, rows)
                second_half = pl.multiple_of((1 - core) * rows, rows)
                w_ref[0, pl.ds(first, rows), :] = got_refs[j - 1][...].reshape(rows, width)
                w_ref[0, pl.ds(second_half, rows), :] = other_refs[j - 1][...].reshape(rows, width)

        c = jnp.bitwise_xor(me, step)
        f = dot_nn(h_ref[...], w_ref[0]) + vec_ref[pl.ds(8 + c, 1), :]
        square = f * f
        t = jnp.tanh(0.7978845608028654 * f * (1.0 + 0.044715 * square))
        up = 0.5 * (1.0 + t)
        g_ref[0] = (f * up).astype(BF)
        slope = 0.5 * f * (1.0 - t * t) * (0.7978845608028654 + 0.1070322243 * square)
        gp_ref[0] = (up + slope).astype(BF)

    pick = lambda j, wh: (jnp.bitwise_xor(wh[0], j), 0, 0)
    return pl.pallas_call(
        kern,
        grid_spec=pltpu.PrefetchScalarGridSpec(
            num_scalar_prefetch=1,
            grid=(nq,),
            in_specs=[fixed(h2.shape), fixed((ns, dsh, width))]
            + [fixed(a.shape) for a in got]
            + [fixed(a.shape) for a in other]
            + [fixed(vecs.shape)],
            out_specs=[
                pl.BlockSpec((1, tok, width), pick),
                pl.BlockSpec((1, tok, width), pick),
                pl.BlockSpec((1, width, width), pick),
            ],
        ),
        out_shape=[
            jax.ShapeDtypeStruct((nq, tok, width), BF),
            jax.ShapeDtypeStruct((nq, tok, width), BF),
            jax.ShapeDtypeStruct((nq, width, width), BF),
        ],
        compiler_params=pltpu.CompilerParams(vmem_limit_bytes=VMEM_LIMIT),
        cost_estimate=cost(2 * nq * width * width * tok, 4 * nq * width * (tok + width)),
        name="fc",
    )(where, h2, second, *got, *other, vecs)


def proj_call(g, w_proj, x1, teacher, cotangent, weight, vecs):
    nq, tok, width = g.shape

    def kern(g_ref, w_ref, x_ref, te_ref, co_ref, wt_ref, vec_ref, y_ref, dy_ref, dm_ref, gw_ref, pb_ref, acc, keep):
        i = pl.program_id(0)

        @pl.when(i == 0)
        def _():
            acc[...] = x_ref[...] + vec_ref[7:8]

        @pl.when(i < nq)
        def _():
            keep[i] = g_ref[0]
            acc[...] += dot_nn(g_ref[0], w_ref[...])

        @pl.when(i == nq - 1)
        def _():
            y = acc[...]
            y_ref[...] = y.astype(BF)
            dy = co_ref[...].astype(F32) + wt_ref[...] * (y - te_ref[...].astype(F32))
            dy_ref[...] = dy
            dm = dy.astype(BF)
            dm_ref[...] = dm
            pb_ref[0:1, :] = jnp.sum(dm.astype(F32), axis=0, keepdims=True)
            pb_ref[1:8, :] = jnp.zeros((7, width), F32)

        @pl.when(i >= nq)
        def _():
            gw_ref[...] = dot_tn(keep[i - nq], dm_ref[...]).astype(BF)

    last = nq - 1
    return pl.pallas_call(
        kern,
        grid=(2 * nq,),
        in_specs=[
            pl.BlockSpec((1, tok, width), lambda i: (jnp.minimum(i, last), 0, 0)),
            pl.BlockSpec((width, width), lambda i: (jnp.minimum(i, last), 0)),
        ]
        + [fixed(a.shape) for a in (x1, teacher, cotangent, weight, vecs)],
        out_specs=[
            fixed((tok, width)),
            fixed((tok, width)),
            fixed((tok, width)),
            pl.BlockSpec((width, width), lambda i: (jnp.maximum(i - nq, 0), 0)),
            fixed((8, width)),
        ],
        out_shape=[
            jax.ShapeDtypeStruct((tok, width), BF),
            jax.ShapeDtypeStruct((tok, width), F32),
            jax.ShapeDtypeStruct((tok, width), BF),
            jax.ShapeDtypeStruct((nq * width, width), BF),
            jax.ShapeDtypeStruct((8, width), F32),
        ],
        scratch_shapes=[pltpu.VMEM((tok, width), F32), pltpu.VMEM((nq, tok, width), BF)],
        compiler_params=pltpu.CompilerParams(vmem_limit_bytes=VMEM_LIMIT),
        cost_estimate=cost(4 * nq * width * width * tok, 2 * nq * width * (tok + 2 * width)),
        name="proj",
    )(g, w_proj, x1, teacher, cotangent, weight, vecs)


def mid_call(dm, dy, w_proj, gp, h2, w_fc, x1, mix, second, vecs, core):
    nq, tok, width = gp.shape
    ns = second.shape[0]
    dsh = width // ns
    nz = ns // 2

    def kern(*refs):
        (co_ref, dm_ref, dy_ref, wp_ref, gp_ref, h_ref, wf_ref, x_ref, o_ref, wo_ref, vec_ref) = refs[:11]
        (fm_ref, ft_ref, om_ref, ot_ref, dx_ref, do_ref, sm_ref, fb_ref, ht, dh2) = refs[11:]
        j = pl.program_id(0)
        total = lambda m: jnp.sum(m, axis=0, keepdims=True)

        def split(gw, mine, theirs):
            gw = gw.astype(BF).reshape(nz, 2, dsh, width)
            for c in range(2):

                @pl.when(co_ref[0] == c)
                def _():
                    mine[...] = gw[:, c]
                    theirs[...] = gw[:, 1 - c]

        @pl.when(j == 0)
        def _():
            ht[...] = jnp.transpose(h_ref[...])
            dh2[...] = jnp.zeros_like(dh2)

        @pl.when(j < nq)
        def _():
            dg = dot_nt(dm_ref[...], wp_ref[...])
            df = (dg * gp_ref[0].astype(F32)).astype(BF)
            fb_ref[pl.ds(j, 1), :] = total(df.astype(F32))
            split(dot_nn(ht[...], df), fm_ref.at[0], ft_ref.at[0])
            dh2[...] += dot_nt(df, wf_ref[0])

        @pl.when(j == nq)
        def _():
            z, inv = normalize(x_ref[...])
            grad = dh2[...]
            sm_ref[0:1, :] = total(grad * z)
            sm_ref[1:2, :] = total(grad)
            dx = dy_ref[...] + norm_back(grad * vec_ref[5:6], z, inv)
            dx_ref[...] = dx
            da = dx.astype(BF)
            sm_ref[2:3, :] = total(da.astype(F32))
            do_ref[...] = dot_nt(da, wo_ref[...].reshape(width, width)).astype(BF)
            split(dot_tn(o_ref[...], da), om_ref, ot_ref)

    last = nq - 1
    pick = lambda j: (jnp.minimum(j, last), 0, 0)
    out = pl.BlockSpec((1, nz, dsh, width), lambda j: (jnp.minimum(j, last), 0, 0, 0))
    return pl.pallas_call(
        kern,
        grid=(nq + 1,),
        in_specs=[
            pl.BlockSpec(memory_space=pltpu.SMEM),
            fixed(dm.shape),
            fixed(dy.shape),
            pl.BlockSpec((width, width), lambda j: (jnp.minimum(j, last), 0)),
            pl.BlockSpec((1, tok, width), pick),
            fixed(h2.shape),
            pl.BlockSpec((1, width, width), pick),
            fixed(x1.shape),
            fixed(mix.shape),
            pl.BlockSpec((ns, dsh, width), lambda j: (0, 1, 0)),
            fixed(vecs.shape),
        ],
        out_specs=[
            out,
            out,
            fixed((nz, dsh, width)),
            fixed((nz, dsh, width)),
            fixed((tok, width)),
            fixed((tok, width)),
            fixed((8, width)),
            fixed((nq, width)),
        ],
        out_shape=[
            jax.ShapeDtypeStruct((nq, nz, dsh, width), BF),
            jax.ShapeDtypeStruct((nq, nz, dsh, width), BF),
            jax.ShapeDtypeStruct((nz, dsh, width), BF),
            jax.ShapeDtypeStruct((nz, dsh, width), BF),
            jax.ShapeDtypeStruct((tok, width), F32),
            jax.ShapeDtypeStruct((tok, width), BF),
            jax.ShapeDtypeStruct((8, width), F32),
            jax.ShapeDtypeStruct((nq, width), F32),
        ],
        scratch_shapes=[pltpu.VMEM((width, tok), BF), pltpu.VMEM((tok, width), F32)],
        compiler_params=pltpu.CompilerParams(vmem_limit_bytes=VMEM_LIMIT),
        cost_estimate=cost(
            2 * width * width * tok * (3 * nq + 2), 2 * width * (nq * (tok + 4 * width) + 8 * tok)
        ),
        name="mid",
    )(core, dm, dy, w_proj, gp, h2, w_fc, x1, mix, second, vecs)


def grads_call(h1, dq, dkv, shard, ns):
    keys, width = h1.shape
    tok = dq.shape[0]
    plen = ns * PR_DEV
    dsh = width // ns

    def kern(sh_ref, h_ref, dq_ref, d_ref, o_ref, ht):
        j = pl.program_id(0)

        @pl.when(j == 0)
        def _():
            ht[...] = jnp.transpose(h_ref[...])

        @pl.when(j < 2)
        def _():
            o_ref[...] = dot_nn(ht[...], d_ref[0]).astype(BF).reshape(ns, dsh, width)

        @pl.when(j == 2)
        def _():
            own = pl.ds(pl.multiple_of(sh_ref[0] * PR_DEV, PR_DEV), PR_DEV)
            gq = dot_nn(ht[:, plen:], dq_ref[PR_DEV:, :]) + dot_tn(h_ref[own, :], dq_ref[:PR_DEV, :])
            o_ref[...] = gq.astype(BF).reshape(ns, dsh, width)

    return pl.pallas_call(
        kern,
        grid=(3,),
        in_specs=[
            pl.BlockSpec(memory_space=pltpu.SMEM),
            fixed(h1.shape),
            fixed(dq.shape),
            pl.BlockSpec((1, keys, width), lambda j: (jnp.minimum(j, 1), 0, 0)),
        ],
        out_specs=pl.BlockSpec((ns, dsh, width), lambda j: (0, (j + 1) % 3, 0)),
        out_shape=jax.ShapeDtypeStruct((ns, 3 * dsh, width), BF),
        scratch_shapes=[pltpu.VMEM((width, keys), BF)],
        compiler_params=pltpu.CompilerParams(vmem_limit_bytes=VMEM_LIMIT),
        cost_estimate=cost(2 * width * width * (2 * keys + tok), 2 * width * 5 * keys),
        name="grads",
    )(shard, h1, dq, dkv)


def dh1_call(bundle, tokens, vecs, dq, dkv, dx1, sums, fc_sums, last, shard):
    ns, _, width = bundle.shape
    tok = tokens.shape[0]
    cont = tok - PR_DEV
    plen = ns * PR_DEV
    dsh = width // ns
    nq = fc_sums.shape[0]
    base = 3 * dsh
    step = cont // PR_DEV
    chunks = ns // step

    def kern(*refs):
        (sh_ref, g_ref, t_ref, vec_ref, dq_ref, dk_ref, dv_ref, dx_ref) = refs[:8]
        (s2_ref, fb_ref, s3_ref, o_ref, ig_ref, sm) = refs[8:]
        i = pl.program_id(0)
        wq, wk, wv = (
            g_ref[:, j * dsh : (j + 1) * dsh, :].reshape(width, width) for j in range(3)
        )
        total = lambda m: jnp.sum(m, axis=0, keepdims=True)

        @pl.when(i == 0)
        def _():
            sm[...] = jnp.zeros_like(sm)

        def add(dh, z):
            sm[0:1, :] += total(dh * z)
            sm[1:2, :] += total(dh)

        dv = dv_ref[0]
        sm[3:4, :] += total(dv.astype(F32))
        dh = dot_nt(dk_ref[0], wk) + dot_nt(dv, wv)

        @pl.when(i < chunks)
        def _():
            x = g_ref[pl.ds(i * step, step), base : base + PR_DEV, :]
            z, _ = normalize(x.reshape(cont, width).astype(F32))
            add(dh, z)
            o_ref[pl.ds(i * step, step), EXTRA:, :] = dh.astype(BF).reshape(step, PR_DEV, width)

        @pl.when(i == sh_ref[0] // step)
        def _():
            own = pl.ds(pl.multiple_of((sh_ref[0] % step) * PR_DEV, PR_DEV), PR_DEV)
            z, _ = normalize(t_ref[:PR_DEV, :].astype(F32))
            part = dot_nt(dq_ref[:PR_DEV, :], wq)
            add(part, z)
            both = dot_nt(dk_ref[0, own, :], wk) + dot_nt(dv_ref[0, own, :], wv)
            o_ref[sh_ref[0], EXTRA:, :] = (both + part).astype(BF)

        @pl.when(i == chunks)
        def _():
            z, inv = normalize(t_ref[PR_DEV:, :].astype(F32))
            full = dh + dot_nt(dq_ref[PR_DEV:, :], wq)
            add(full, z)
            ig_ref[PR_DEV:, :] = dx_ref[PR_DEV:, :] + norm_back(full * vec_ref[0:1], z, inv)
            ig_ref[:PR_DEV, :] = dx_ref[:PR_DEV, :]
            sm[2:3, :] = total(dq_ref[...].astype(F32))
            sm[4:5, :] = s2_ref[2:3, :]
            sm[5:7, :] = s2_ref[0:2, :]
            sm[7:8, :] = s3_ref[0:1, :]
            sm[8 : 8 + nq, :] = fb_ref[...]
            small = sm[...].astype(BF)
            for b in range(ns):
                o_ref[b, :EXTRA, :] = small

    chunk = lambda k: pl.BlockSpec((1, cont, width), lambda i: (k, i, 0))
    out = (ns, EXTRA + PR_DEV, width)
    return pl.pallas_call(
        kern,
        grid=(chunks + 1,),
        in_specs=[
            pl.BlockSpec(memory_space=pltpu.SMEM),
            fixed(bundle.shape),
            fixed(tokens.shape),
            fixed(vecs.shape),
            fixed(dq.shape),
            chunk(0),
            chunk(1),
        ]
        + [fixed(a.shape) for a in (dx1, sums, fc_sums, last)],
        out_specs=[fixed(out), fixed((tok, width))],
        out_shape=[jax.ShapeDtypeStruct(out, BF), jax.ShapeDtypeStruct((tok, width), F32)],
        scratch_shapes=[pltpu.VMEM((EXTRA, width), F32)],
        compiler_params=pltpu.CompilerParams(vmem_limit_bytes=VMEM_LIMIT),
        cost_estimate=cost(
            2 * width * width * (2 * (plen + cont) + tok), 2 * width * (5 * plen + 10 * cont)
        ),
        name="dh1",
    )(shard, bundle, tokens, vecs, dq, dkv, dkv, dx1, sums, fc_sums, last)


def finish_call(grad, summed, tokens, vecs):
    tok, width = grad.shape

    def kern(g_ref, s_ref, t_ref, vec_ref, o_ref):
        z, inv = normalize(t_ref[...].astype(F32))
        e = s_ref[...].astype(F32) * vec_ref[0:1]
        o_ref[...] = g_ref[...] + norm_back(e, z, inv)

    block = pl.BlockSpec((PR_DEV, width), lambda i: (0, 0))
    return pl.pallas_call(
        kern,
        grid=(1,),
        in_specs=[block, block, block, pl.BlockSpec(vecs.shape, lambda i: (0, 0))],
        out_specs=block,
        out_shape=jax.ShapeDtypeStruct((tok, width), F32),
        input_output_aliases={0: 0},
        cost_estimate=cost(20 * PR_DEV * width, 12 * PR_DEV * width),
        name="finish",
    )(grad, summed, tokens, vecs)


def over(axis, values, bit):
    n = lax.axis_size(axis)
    return lax.ppermute(values, axis, [(i, i ^ bit) for i in range(n)])


def rep_sum(values):
    n = lax.axis_size("rep")
    bits = [1 << b for b in range(n.bit_length() - 1)]
    cut = values.shape[0] // 2
    halves = [values[:cut], values[cut:]]
    for i in range(len(bits)):
        steps = (bits[i], bits[-1 - i])
        got = [over("rep", v, b) for v, b in zip(halves, steps)]
        halves = [(v.astype(F32) + g.astype(F32)).astype(v.dtype) for v, g in zip(halves, got)]
    return jnp.concatenate(halves)


def local(
    tokens,
    ln1_gain,
    ln1_bias,
    w_qkv,
    qv_bias,
    w_out,
    out_bias,
    ln2_gain,
    ln2_bias,
    w_fc,
    fc_bias,
    w_proj,
    proj_bias,
    teacher,
    cotangent,
    valid_mask,
):
    ns = lax.axis_size("shard")
    nr = lax.axis_size("rep")
    me = lax.axis_index("shard").astype(jnp.int32)
    shard = me.reshape(1)
    tok, width = tokens.shape
    nq = min(nr, w_fc.shape[1] // width)
    group = lax.axis_index("rep").astype(jnp.int32) % nq
    dsh = width // ns
    rb = 256

    bundle = lax.all_gather(
        jnp.concatenate(
            [w_qkv[:, :width], w_qkv[:, width : 2 * width], w_qkv[:, 2 * width :], tokens[:PR_DEV]]
        ),
        "shard",
    )
    fc_own = lax.dynamic_slice_in_dim(w_fc, group * width, width, 1)
    second = lax.all_gather(jnp.concatenate([fc_own, w_out]), "shard")
    full_proj = lax.all_gather(w_proj, "shard", axis=0, tiled=True)

    mask_f = valid_mask.astype(F32)
    counts = jnp.sum(mask_f.reshape(-1, PR_DEV), axis=1).astype(BF)
    parts = [ln1_gain, ln1_bias, qv_bias, out_bias, ln2_gain, ln2_bias, proj_bias, fc_bias]
    offs = [0]
    for p in parts:
        offs.append(offs[-1] + p.shape[0])
    packed = jnp.concatenate(parts + [counts])
    packed = jnp.pad(packed, (0, (-packed.shape[0]) % 128))
    params = lax.all_gather(packed.reshape(1, -1), "shard", axis=0, tiled=True).astype(F32)
    vecs = jnp.concatenate(
        [params[:, offs[i] : offs[i + 1]].reshape(-1, width) for i in range(8)]
        + [jnp.zeros((16 - 8 - nq, width), F32)]
    )
    count = jnp.sum(params[:, offs[8] : offs[8] + counts.shape[0]])
    token_total = rep_sum(jnp.full((16, 128), count, F32))[0, 0]
    factor = tok * nr * ns / token_total
    weight = (factor * mask_f).reshape(tok, 1)

    h1, q, k, v = qkv_call(bundle, tokens, vecs, shard)
    mix, lse = attn_fwd(q, k, v, shard, rb)
    x1, h2 = out_proj_call(mix, second, tokens, vecs)

    core = me % 2
    piece = lax.dynamic_slice_in_dim(second, core * (ns // 2), ns // 2, 0)[:, :dsh]
    got = [over("rep", piece, j) for j in range(1, nq)]
    other = [over("shard", g, 1) for g in got]
    g, gp, full_fc = fc_call(h2, second, got, other, vecs, jnp.stack([group, core]))
    out, dy, dm, grad_proj, last = proj_call(g, full_proj, x1, teacher, cotangent, weight, vecs)
    own_proj = lax.psum_scatter(grad_proj, "shard", scatter_dimension=0, tiled=True)
    fc_mine, fc_theirs, out_mine, out_theirs, dx1, do, sums, fc_sums = mid_call(
        dm, dy, full_proj, gp, h2, full_fc, x1, mix, second, vecs, core.reshape(1)
    )
    dq, dkv = attn_bwd(q, k, v, mix, do, lse, shard, rb)

    plus = lambda *terms: sum(t.astype(F32) for t in terms).astype(BF)
    nz = ns // 2
    fc_half = plus(fc_mine, over("shard", fc_theirs, 1))
    out_half = plus(out_mine, over("shard", out_theirs, 1))
    out_half = jnp.swapaxes(out_half.reshape(nz, nq, dsh // nq, width), 0, 1)
    pair = jnp.concatenate([fc_half, out_half], axis=2)

    dq, dkv, own_proj, pair = lax.optimization_barrier((dq, dkv, own_proj, pair))
    grads = grads_call(h1, dq, dkv, shard, ns)
    own_qkv = lax.psum_scatter(grads.reshape(-1, width), "shard", scatter_dimension=0, tiled=True)
    dq, dkv, grads = lax.optimization_barrier((dq, dkv, grads))
    last_part, ig = dh1_call(bundle, tokens, vecs, dq, dkv, dx1, sums, fc_sums, last, shard)
    last_part, own_qkv = lax.optimization_barrier((last_part, own_qkv))
    own = lax.psum_scatter(last_part.reshape(-1, width), "shard", scatter_dimension=0, tiled=True)
    input_grad = finish_call(ig, own[EXTRA:], tokens, vecs)

    pick = lambda a, n: lax.dynamic_index_in_dim(a, n, 0, keepdims=False)
    quarter = plus(
        pick(pair, group),
        *[over("rep", pick(pair, jnp.bitwise_xor(group, b)), b) for b in range(1, nq)],
    )
    z = me // 2
    final = plus(
        pick(quarter, z),
        *[over("shard", pick(quarter, jnp.bitwise_xor(z, b)), 2 * b) for b in range(1, nz)],
    )
    bit = nq
    while bit < nr:
        final = plus(final, over("rep", final, bit))
        bit *= 2
    relative = jnp.stack([final] + [over("rep", final, b) for b in range(1, nq)])
    natural = [pick(relative, jnp.bitwise_xor(group, b)) for b in range(nq)]
    sum_fc = jnp.concatenate([n[:dsh] for n in natural], axis=1).astype(F32)
    sum_out = jnp.concatenate([n[dsh:] for n in natural], axis=0).astype(F32)

    sum_proj = rep_sum(own_proj).astype(F32)
    sum_qkv = rep_sum(own_qkv).astype(F32)
    small = rep_sum(own[:EXTRA]).astype(F32)

    def take(first, rows):
        n = rows * dsh
        return lax.dynamic_slice_in_dim(small[first : first + rows].reshape(-1), me * n, n)

    return (
        out,
        input_grad,
        take(0, 1),
        take(1, 1),
        jnp.concatenate([sum_qkv[j * dsh : (j + 1) * dsh] for j in range(3)], axis=1),
        take(2, 2),
        sum_out,
        take(4, 1),
        take(5, 1),
        take(6, 1),
        sum_fc,
        take(8, nq),
        sum_proj,
        take(7, 1),
    )


def solution(mesh):
    rows = P(("rep", "shard"), None)
    mat = P("shard", None)
    vec = P("shard")
    return jax.shard_map(
        local,
        mesh=mesh,
        in_specs=(
            rows,
            vec,
            vec,
            mat,
            vec,
            mat,
            vec,
            vec,
            vec,
            mat,
            vec,
            mat,
            vec,
            rows,
            rows,
            P(("rep", "shard")),
        ),
        out_specs=(rows, rows, vec, vec, mat, vec, mat, vec, vec, vec, mat, vec, mat, vec),
        check_vma=False,
    )
```

time: 562 us -> 369 us (0.66)
  waiting for transfers between devices: 327 us -> 123 us
  matrix products: 66 us -> 0 us
  Pallas kernels: 90.3 us -> 151 us
  starting transfers between devices: 15.5 us -> 32.2 us
    reduce_scatter x4 -> x2, waiting for transfers between devices: 155 us -> 0.04 us  [the longest x1 0.02 us: local(): lax.psum_scatter(grad_proj, 'shard', scatter_dimension=0, tiled=True)]
    dot_general x9 -> x0, matrix products: 66 us -> none  [the longest x3 22.6 us: dot_nt(): lax.dot_general(a, b, (((1,), (1,)), ((), ())), preferred_element_type=F32)]
    pallas_call x3 -> x7, Pallas kernels: 32.9 us -> 94.3 us  [the longest x1 24.6 us: mid_call(): pl.pallas_call(kern, grid=(nq + 1,), in_specs=[pl.BlockSpec(memory_space=...]
    all_gather x1, waiting for transfers between devices: 43.6 us -> 0.01 us  [local(): full_proj = lax.all_gather(w_proj, 'shard', axis=0, tiled=True)]
    ppermute x10 -> x31, waiting for transfers between devices: 38.5 us -> 69.6 us  [over(): return lax.ppermute(values, axis, [(i, i ^ bit) for i in range(n)])]
    all_gather x2 -> x1, waiting for transfers between devices: 39.7 us -> 13.8 us  [local(): second = lax.all_gather(jnp.concatenate([fc_own, w_out]), 'shard')]
    ppermute x10 -> x31, starting transfers between devices: 14.9 us -> 32 us  [over(): return lax.ppermute(values, axis, [(i, i ^ bit) for i in range(n)])]
    all_gather x1, waiting for transfers between devices: 29.1 us -> 22 us  [local(): lax.all_gather(jnp.concatenate([w_qkv[:, :width], w_qkv[:, width:2 * widt...]
  transfers between devices with their start and end apart: 19 -> 37, of which waited for: 15 -> 19; matrix products, arithmetic and copies ran while one was open for 8% -> 6% of each run, Pallas kernels for 6% -> 35%
where the time goes in v2:
time: 369 us; the launch traced here: 365 us
  Pallas kernels  151 us (41%)
  waiting for transfers between devices  123 us (33%)
  starting transfers between devices  32.2 us (9%)
  between operations  15.9 us (4%)
  other arithmetic  15.2 us (4%)
  local copies, waits for them, and re-layouts  15.1 us (4%)
  blocking collectives  12.4 us (3%)
    ppermute x31, waiting for transfers between devices, over(): return lax.ppermute(values, axis, [(i, i ^ bit) for i in range(n)])  69.6 us
    pallas_call x1, Pallas kernels, attn_bwd(): pl.pallas_call(kern, grid=(npair,), in_specs=[pl.BlockSpec(memory_space=p...  32.4 us
    ppermute x31, starting transfers between devices, over(): return lax.ppermute(values, axis, [(i, i ^ bit) for i in range(n)])  32 us
    pallas_call x1, Pallas kernels, mid_call(): pl.pallas_call(kern, grid=(nq + 1,), in_specs=[pl.BlockSpec(memory_space=...  24.6 us
    pallas_call x1, Pallas kernels, attn_fwd(): pl.pallas_call(kern, grid=(npair,), in_specs=[pl.BlockSpec(memory_space=p...  22.5 us
    all_gather x1, waiting for transfers between devices, local(): lax.all_gather(jnp.concatenate([w_qkv[:, :width], w_qkv[:, width:2 * widt...  22 us
    reduce_scatter x1, waiting for transfers between devices, local(): lax.psum_scatter(grads.reshape(-1, width), 'shard', scatter_dimension=0,...  17 us
    pallas_call x1, Pallas kernels, proj_call(): pl.pallas_call(kern, grid=(2 * nq,), in_specs=[pl.BlockSpec((1, tok, widt...  15.5 us
  transfers between devices with their start and end apart: 37, of which 19 were waited for; matrix products, arithmetic and copies ran while one was open for 6% of the time, Pallas kernels for 35%

profile of v2, /device:TPU:16, one launch (start us, length us, event | category | flops | bytes accessed | tf_op | source)
XLA Modules:
  0.0 365.5 jit_solution(186698454895268841)
XLA Ops:
  8.3 1.6 pad_maximum_fusion.4
  13.2 12.4 %all-gather.3 = bf16[8,1,1280]{2,1,0:T(2,128)(2,1)S(1)} all-gather(bf16[1,1,1280]{2,1,0:T(2,128)(2,1)S(1)} %reshape.129), channel_id=3, replica_groups=mesh['rep'=4,'shard'=8] {'shard'}, dimensions={0}, use_global_device_ids=true | all-gather | bytes 23040 | tf_op jit(solution)/shard_map/all_gather | solution.py:709
  26.9 1.5 collective-permute-start.6
  28.4 13.8 %all-gather.12.cloned.1.call-done = bf16[1536,768]{1,0:T(8,128)(2,1)} async-done(((bf16[192,768]{1,0:T(8,128)(2,1)}), bf16[1536,768]{1,0:T(8,128)(2,1)}) %all-gather.12.cloned.1.call-update) | async-done | bytes 2359312 | tf_op jit(solution)/shard_map/all_gather | solution.py:698
  43.3 1.5 collective-permute-start
  44.8 1.5 collective-permute-start.1
  47.5 1.5 collective-permute-start.7
  50.3 1.3 concatenate.35.vec_ref.refs_9_.refs_10_.refs_3_
  51.5 21.2 %collective-permute-done.7 = f32[8,128]{1,0:T(8,128)S(1)} collective-permute-done((f32[8,128]{1,0:T(8,128)S(1)}, f32[8,128]{1,0:T(8,128)S(1)}, u32[]{:S(2)}, u32[]{:S(2)}) %collective-permute-start.7) | collective-permute-done | bytes 4128 | tf_op jit(solution)/shard_map/ppermute | solution.py:648
  76.1 22.0 %all-gather.10.cloned.1.call-done = bf16[3328,768]{1,0:T(8,128)(2,1)} async-done(((bf16[416,768]{1,0:T(8,128)(2,1)}), bf16[3328,768]{1,0:T(8,128)(2,1)}) %all-gather.10.cloned.1.call-update) | async-done | bytes 5111824 | tf_op jit(solution)/shard_map/all_gather | solution.py:691
  98.1 11.9 %qkv.1 = (bf16[1536,768]{1,0:T(8,128)(2,1)}, bf16[640,768]{1,0:T(8,128)(2,1)}, bf16[1536,768]{1,0:T(8,128)(2,1)}, bf16[1536,768]{1,0:T(8,128)(2,1)}) custom-call(s32[1]{0:T(128)} %bitcast.2.sh_ref.refs_0_, bf16[8,416,768]{2,1,0:T(8,128)(2,1)} %bitcast.67, bf16[640,768]{1,0:T(8,128)(2,1)} %t_ref.5, f32[16,768]{1,0:T(8,128)} %concatenate.35.vec_ref.refs_9_.refs_10_.refs_3_), custom_call_target="tpu_custom_call" | custom-call | flops 4378853376 | bytes 14155776 | tf_op jit(solution)/shard_map/qkv/pallas_call | solution.py:97
  110.0 22.5 %attn_fwd.1 = (bf16[640,768]{1,0:T(8,128)(2,1)}, f32[6,2,640]{2,1,0:T(2,128)}) custom-call(s32[1]{0:T(128)} %bitcast.2.sh_ref.refs_0_, bf16[640,768]{1,0:T(8,128)(2,1)} %get-tuple-element.50.q_ref, bf16[1536,768]{1,0:T(8,128)(2,1)} %get-tuple-element.51.k_ref, bf16[1536,768]{1,0:T(8,128)(2,1)} %get-tuple-element.52.v_ref), custom_call_target="tpu_custom_call" | custom-call | flops 12079595520 | bytes 6684672 | tf_op jit(solution)/shard_map/attn_fwd/pallas_call | solution.py:153
  132.6 4.5 %out_proj.1 = (f32[640,768]{1,0:T(8,128)}, bf16[640,768]{1,0:T(8,128)(2,1)}) custom-call(bf16[640,768]{1,0:T(8,128)(2,1)} %get-tuple-element.53.o_ref.refs_8_, bf16[8,192,768]{2,1,0:T(8,128)(2,1)} %bitcast.70, bf16[640,768]{1,0:T(8,128)(2,1)} %t_ref.5, f32[16,768]{1,0:T(8,128)} %concatenate.35.vec_ref.refs_9_.refs_10_.refs_3_), custom_call_target="tpu_custom_call" | custom-call | flops 754974720 | bytes 5898240 | tf_op jit(solution)/shard_map/out_proj/pallas_call | solution.py:257
  138.1 12.6 %fc.1 = (bf16[4,640,768]{2,1,0:T(8,128)(2,1)}, bf16[4,640,768]{2,1,0:T(8,128)(2,1)}, bf16[4,768,768]{2,1,0:T(8,128)(2,1)}) custom-call(s32[2]{0:T(128)} %pad_add_fusion.refs_0_, bf16[640,768]{1,0:T(8,128)(2,1)} %get-tuple-element.54.refs_1_.refs_5_, bf16[8,192,768]{2,1,0:T(8,128)(2,1)} %bitcast.71, bf16[4,96,768]{2,1,0:T(8,128)(2,1)} %copy-done.16, ...), custom_call_target="tpu_custom_call" | custom-call | flops 3019898880 | bytes 17301504 | tf_op jit(solution)/shard_map/fc/pallas_call | solution.py:313
  150.7 15.5 %proj.1 = (bf16[640,768]{1,0:T(8,128)(2,1)}, f32[640,768]{1,0:T(8,128)}, bf16[640,768]{1,0:T(8,128)(2,1)}, bf16[3072,768]{1,0:T(8,128)(2,1)}, f32[8,768]{1,0:T(8,128)}) custom-call(bf16[4,640,768]{2,1,0:T(8,128)(2,1)} %get-tuple-element.55.g_ref, bf16[3072,768]{1,0:T(8,128)(2,1)} %all-gather.8.cloned.1.call-done.w_ref.refs_3_, ...), custom_call_target="tpu_custom_call" | custom-call | flops 6039797760 | bytes 13369344 | tf_op jit(solution)/shard_map/proj/pallas_call | solution.py:370
  166.3 24.6 %mid.1 = (bf16[4,4,96,768]{3,2,1,0:T(8,128)(2,1)}, bf16[4,4,96,768]{3,2,1,0:T(8,128)(2,1)}, bf16[4,96,768]{2,1,0:T(8,128)(2,1)}, bf16[4,96,768]{2,1,0:T(8,128)(2...) custom-call(s32[1]{0:T(128)} %bitcast.1.refs_0_, ...), custom_call_target="tpu_custom_call" | custom-call | flops 10569646080 | bytes 30670848 | tf_op jit(solution)/shard_map/mid/pallas_call | solution.py:449
  191.6 32.4 %attn_bwd.1 = (bf16[640,768]{1,0:T(8,128)(2,1)}, bf16[2,1536,768]{2,1,0:T(8,128)(2,1)}) custom-call(s32[1]{0:T(128)} %bitcast.2.sh_ref.refs_0_, bf16[640,768]{1,0:T(8,128)(2,1)} %get-tuple-element.50.q_ref, bf16[1536,768]{1,0:T(8,128)(2,1)} %get-tuple-element.51.k_ref, bf16[1536,768]{1,0:T(8,128)(2,1)} %get-tuple-element.52.v_ref, ...), custom_call_target="tpu_custom_call" | custom-call | flops 30198988800 | bytes 13369344 | tf_op jit(solution)/shard_map/attn_bwd/pallas_call | solution.py:221
  224.2 1.4 copy-done.2
  226.5 9.6 %grads.1 = bf16[8,288,768]{2,1,0:T(8,128)(2,1)} custom-call(s32[1]{0:T(128)} %bitcast.2.sh_ref.refs_0_, bf16[1536,768]{1,0:T(8,128)(2,1)} %get-tuple-element.73.h_ref, bf16[640,768]{1,0:T(8,128)(2,1)} %get-tuple-element.74.dq_ref.refs_4_, bf16[2,1536,768]{2,1,0:T(8,128)(2,1)} %get-tuple-element.75.d_ref.refs_5_.refs_6_), custom_call_target="tpu_custom_call" | custom-call | flops 4378853376 | bytes 11796480 | tf_op jit(solution)/shard_map/grads/pallas_call | solution.py:517
  236.2 1.4 dynamic-slice_bitcast_fusion.2
  237.7 1.4 collective-permute-start.18
  239.0 1.6 collective-permute-start.19
  242.0 1.4 collective-permute-start.27
  243.4 1.6 collective-permute-start.29
  245.0 15.5 %dh1.1 = (bf16[8,144,768]{2,1,0:T(8,128)(2,1)}, f32[640,768]{1,0:T(8,128)}) custom-call(s32[1]{0:T(128)} %bitcast.2.sh_ref.refs_0_, bf16[8,416,768]{2,1,0:T(8,128)(2,1)} %bitcast.68, bf16[640,768]{1,0:T(8,128)(2,1)} %t_ref.5, f32[16,768]{1,0:T(8,128)} %concatenate.35.vec_ref.refs_9_.refs_10_.refs_3_, bf16[640,768]{1,0:T(8,128)(2,1)} %get-tuple-element.74.dq_ref.refs_4_, ...), custom_call_target="tpu_custom_call" | custom-call | flops 4378853376 | bytes 15728640 | tf_op jit(solution)/shard_map/dh1/pallas_call | solution.py:601
  260.4 17.0 %reduce-scatter.6.cloned.1.call-done = bf16[288,768]{1,0:T(8,128)(2,1)} async-done(((bf16[2304,768]{1,0:T(8,128)(2,1)}), bf16[288,768]{1,0:T(8,128)(2,1)}) %reduce-scatter.6.cloned.1.call-update) | async-done | bytes 442384 | tf_op jit(solution)/shard_map/reduce_scatter | solution.py:744
  277.5 1.2 collective-permute-done.27
  281.0 1.6 collective-permute-start.28
  283.1 1.9 fusion.2
  285.6 1.4 collective-permute-start.22
  287.0 1.6 collective-permute-start.23
  289.1 7.5 %collective-permute-done.21 = bf16[120,768]{1,0:T(8,128)(2,1)S(1)} collective-permute-done((bf16[120,768]{1,0:T(8,128)(2,1)S(1)}, bf16[120,768]{1,0:T(8,128)(2,1)S(1)}, u32[]{:S(2)}, u32[]{:S(2)}) %collective-permute-start.21) | collective-permute-done | bytes 184352 | tf_op jit(solution)/shard_map/ppermute | solution.py:648
  296.6 7.0 %collective-permute-done.22 = bf16[120,768]{1,0:T(8,128)(2,1)S(1)} collective-permute-done((bf16[120,768]{1,0:T(8,128)(2,1)S(1)}, bf16[120,768]{1,0:T(8,128)(2,1)S(1)}, u32[]{:S(2)}, u32[]{:S(2)}) %collective-permute-start.22) | collective-permute-done | bytes 184352 | tf_op jit(solution)/shard_map/ppermute | solution.py:648
  303.6 11.2 %collective-permute-done.23 = bf16[120,768]{1,0:T(8,128)(2,1)S(1)} collective-permute-done((bf16[120,768]{1,0:T(8,128)(2,1)S(1)}, bf16[120,768]{1,0:T(8,128)(2,1)S(1)}, u32[]{:S(2)}, u32[]{:S(2)}) %collective-permute-start.23) | collective-permute-done | bytes 184352 | tf_op jit(solution)/shard_map/ppermute | solution.py:648
  315.9 2.5 collective-permute-start.26
  319.7 2.1 collective-permute-done.24
  321.8 2.1 collective-permute-done.25
  324.0 2.0 collective-permute-start.14
  327.6 2.5 collective-permute-done.14
  330.0 4.2 %collective-permute-done.16 = bf16[144,768]{1,0:T(8,128)(2,1)S(1)} collective-permute-done((bf16[144,768]{1,0:T(8,128)(2,1)S(1)}, bf16[144,768]{1,0:T(8,128)(2,1)S(1)}, u32[]{:S(2)}, u32[]{:S(2)}) %collective-permute-start.16) | collective-permute-done | bytes 221216 | tf_op jit(solution)/shard_map/ppermute | solution.py:648
  335.2 1.8 collective-permute-start.17
  337.0 3.4 collective-permute-done.15
  342.1 1.8 collective-permute-start.10
  344.1 1.6 collective-permute-done.10
  345.8 1.8 collective-permute-done.12
  350.2 2.3 finish.1
  352.5 2.0 collective-permute-start.13
  354.5 1.7 collective-permute-done.13
  (155 shorter events, 31.1 us)
Async XLA Ops:
  7.2 4.0 %slice-start = ((bf16[640,768]{1,0:T(8,128)(2,1)}), bf16[128,768]{1,0:T(8,128)(2,1)S(1)}, s32[]{:S(2)}) async-start(bf16[640,768]{1,0:T(8,128)(2,1)} %t_ref.5), calls=%async_computation.9 | async-start | bytes 393216 | tf_op jit(solution)/shard_map/slice | solution.py:693
  7.2 35.0 %all-gather.12.cloned.1.call-start = ((), (), s32[]{:S(2)}) async-start(), calls=%async_computation.8 | async-start | bytes 2654208 | tf_op jit(solution)/shard_map/all_gather | solution.py:698
  9.9 3.1 copy-start.8
  10.0 3.1 copy-start.9
  10.0 88.1 %all-gather.10.cloned.1.call-start = ((), (), s32[]{:S(2)}) async-start(), calls=%async_computation.7 | async-start | bytes 5750784 | tf_op jit(solution)/shard_map/all_gather | solution.py:691
  12.1 138.6 %all-gather.8.cloned.1.call-start = ((), (), s32[]{:S(2)}) async-start(), calls=%async_computation.3 | async-start | bytes 5308416 | tf_op jit(solution)/shard_map/all_gather | solution.py:699
  12.8 213.7 %reduce-scatter.4.cloned.1.call-start = ((), (), s32[]{:S(2)}) async-start(), calls=%async_computation.4 | async-start | bytes 5308416 | tf_op jit(solution)/shard_map/reduce_scatter | solution.py:729
  26.9 19.9 %collective-permute-start.6 = (f32[8,128]{1,0:T(8,128)S(1)}, f32[8,128]{1,0:T(8,128)S(1)}, u32[]{:S(2)}, u32[]{:S(2)}) collective-permute-start(f32[8,128]{1,0:T(8,128)S(1)} %slice.168), channel_id=1, source_target_pairs={{0,8},{8,0},{16,24},{24,16},{1,9},{9,1},{17,25},{25,17},{2,10},{10... | collective-permute-start | bytes 12296 | tf_op jit(solution)/shard_map/ppermute | solution.py:648
  43.3 32.2 %collective-permute-start = (bf16[4,96,768]{2,1,0:T(8,128)(2,1)S(1)}, bf16[4,96,768]{2,1,0:T(8,128)(2,1)S(1)}, u32[]{:S(2)}, u32[]{:S(2)}) collective-permute-start(bf16[4,96,768]{2,1,0:T(8,128)(2,1)S(1)} %constant_dynamic-slice_fusion.12), channel_id=1, source_target_pairs={{0,8},{8,0},{16,24},{24,16},{1,9},{9,1},{17,25},{25,17},{2,10},{10... | collective-permute-start | bytes 1769480 | tf_op jit(solution)/shard_map/ppermute | solution.py:648
  44.8 30.7 %collective-permute-start.1 = (bf16[4,96,768]{2,1,0:T(8,128)(2,1)S(1)}, bf16[4,96,768]{2,1,0:T(8,128)(2,1)S(1)}, u32[]{:S(2)}, u32[]{:S(2)}) collective-permute-start(bf16[4,96,768]{2,1,0:T(8,128)(2,1)S(1)} %constant_dynamic-slice_fusion.12), channel_id=1, source_target_pairs={{0,16},{8,24},{16,0},{24,8},{1,17},{9,25},{17,1},{25,9},{2,18},{10... | collective-permute-start | bytes 1769480 | tf_op jit(solution)/shard_map/ppermute | solution.py:648
  46.3 29.7 %collective-permute-start.2 = (bf16[4,96,768]{2,1,0:T(8,128)(2,1)S(1)}, bf16[4,96,768]{2,1,0:T(8,128)(2,1)S(1)}, u32[]{:S(2)}, u32[]{:S(2)}) collective-permute-start(bf16[4,96,768]{2,1,0:T(8,128)(2,1)S(1)} %constant_dynamic-slice_fusion.12), channel_id=1, source_target_pairs={{0,24},{8,16},{16,8},{24,0},{1,25},{9,17},{17,9},{25,1},{2,26},{10... | collective-permute-start | bytes 1769480 | tf_op jit(solution)/shard_map/ppermute | solution.py:648
  47.5 25.2 %collective-permute-start.7 = (f32[8,128]{1,0:T(8,128)S(1)}, f32[8,128]{1,0:T(8,128)S(1)}, u32[]{:S(2)}, u32[]{:S(2)}) collective-permute-start(f32[8,128]{1,0:T(8,128)S(1)} %broadcast_add_fusion), channel_id=1, source_target_pairs={{0,16},{8,24},{16,0},{24,8},{1,17},{9,25},{17,1},{25,9},{2,18},{10... | collective-permute-start | bytes 12296 | tf_op jit(solution)/shard_map/ppermute | solution.py:648
  75.5 34.5 %copy-start.16 = (bf16[4,96,768]{2,1,0:T(8,128)(2,1)}, bf16[4,96,768]{2,1,0:T(8,128)(2,1)S(1)}, u32[]{:S(2)}) copy-start(bf16[4,96,768]{2,1,0:T(8,128)(2,1)S(1)} %collective-permute-done.refs_3_) | copy-start | bytes 1769476
  75.5 61.6 %collective-permute-start.3 = (bf16[4,96,768]{2,1,0:T(8,128)(2,1)S(1)}, bf16[4,96,768]{2,1,0:T(8,128)(2,1)S(1)}, u32[]{:S(2)}, u32[]{:S(2)}) collective-permute-start(bf16[4,96,768]{2,1,0:T(8,128)(2,1)S(1)} %collective-permute-done.refs_3_), channel_id=1, source_target_pairs={{0,1},{1,0},{2,3},{3,2},{4,5},{5,4},{6,7},{7,6},{8,9},{9,8},{10,11... | collective-permute-start | bytes 1769480 | tf_op jit(solution)/shard_map/ppermute | solution.py:648
  75.5 34.5 %copy-start.17 = (bf16[4,96,768]{2,1,0:T(8,128)(2,1)}, bf16[4,96,768]{2,1,0:T(8,128)(2,1)S(1)}, u32[]{:S(2)}) copy-start(bf16[4,96,768]{2,1,0:T(8,128)(2,1)S(1)} %collective-permute-done.1.refs_4_) | copy-start | bytes 1769476
  75.5 61.6 %collective-permute-start.4 = (bf16[4,96,768]{2,1,0:T(8,128)(2,1)S(1)}, bf16[4,96,768]{2,1,0:T(8,128)(2,1)}, u32[]{:S(2)}, u32[]{:S(2)}) collective-permute-start(bf16[4,96,768]{2,1,0:T(8,128)(2,1)S(1)} %collective-permute-done.1.refs_4_), channel_id=1, source_target_pairs={{0,1},{1,0},{2,3},{3,2},{4,5},{5,4},{6,7},{7,6},{8,9},{9,8},{10,11... | collective-permute-start | bytes 1769480 | tf_op jit(solution)/shard_map/ppermute | solution.py:648
  76.0 34.0 %copy-start.18 = (bf16[4,96,768]{2,1,0:T(8,128)(2,1)}, bf16[4,96,768]{2,1,0:T(8,128)(2,1)S(1)}, u32[]{:S(2)}) copy-start(bf16[4,96,768]{2,1,0:T(8,128)(2,1)S(1)} %collective-permute-done.2.refs_5_) | copy-start | bytes 1769476
  76.0 61.1 %collective-permute-start.5 = (bf16[4,96,768]{2,1,0:T(8,128)(2,1)S(1)}, bf16[4,96,768]{2,1,0:T(8,128)(2,1)S(1)}, u32[]{:S(2)}, u32[]{:S(2)}) collective-permute-start(bf16[4,96,768]{2,1,0:T(8,128)(2,1)S(1)} %collective-permute-done.2.refs_5_), channel_id=1, source_target_pairs={{0,1},{1,0},{2,3},{3,2},{4,5},{5,4},{6,7},{7,6},{8,9},{9,8},{10,11... | collective-permute-start | bytes 1769480 | tf_op jit(solution)/shard_map/ppermute | solution.py:648
  166.3 111.1 %reduce-scatter.6.cloned.1.call-start = ((), (), s32[]{:S(2)}) async-start(), calls=%async_computation.5 | async-start | bytes 3981312 | tf_op jit(solution)/shard_map/reduce_scatter | solution.py:744
  191.0 33.2 %collective-permute-start.8 = (bf16[4,4,96,768]{3,2,1,0:T(8,128)(2,1)}, bf16[4,4,96,768]{3,2,1,0:T(8,128)(2,1)S(1)}, u32[]{:S(2)}, u32[]{:S(2)}) collective-permute-start(bf16[4,4,96,768]{3,2,1,0:T(8,128)(2,1)} %get-tuple-element.68), channel_id=1, source_target_pairs={{0,1},{1,0},{2,3},{3,2},{4,5},{5,4},{6,7},{7,6},{8,9},{9,8},{10,11... | collective-permute-start | bytes 7077896 | tf_op jit(solution)/shard_map/ppermute | solution.py:648
  191.2 32.7 %collective-permute-start.9 = (bf16[4,96,768]{2,1,0:T(8,128)(2,1)}, bf16[4,96,768]{2,1,0:T(8,128)(2,1)S(1)}, u32[]{:S(2)}, u32[]{:S(2)}) collective-permute-start(bf16[4,96,768]{2,1,0:T(8,128)(2,1)} %get-tuple-element.70), channel_id=1, source_target_pairs={{0,1},{1,0},{2,3},{3,2},{4,5},{5,4},{6,7},{7,6},{8,9},{9,8},{10,11... | collective-permute-start | bytes 1769480 | tf_op jit(solution)/shard_map/ppermute | solution.py:648
  191.6 32.4 %copy-start.5 = (bf16[4,96,768]{2,1,0:T(8,128)(2,1)S(1)}, bf16[4,96,768]{2,1,0:T(8,128)(2,1)}, u32[]{:S(2)}) copy-start(bf16[4,96,768]{2,1,0:T(8,128)(2,1)} %get-tuple-element.69) | copy-start | bytes 1769476
  236.2 105.1 %reduce-scatter.8.cloned.1.call-start = ((), (), s32[]{:S(2)}) async-start(), calls=%async_computation.6 | async-start | bytes 1990656 | tf_op jit(solution)/shard_map/reduce_scatter | solution.py:748
  236.2 4.9 %copy-start.3 = (bf16[384,768]{1,0:T(8,128)(2,1)S(1)}, bf16[384,768]{1,0:T(8,128)(2,1)}, u32[]{:S(2)}) copy-start(bf16[384,768]{1,0:T(8,128)(2,1)} %reduce-scatter.4.cloned.1.call-done) | copy-start | bytes 1769476
  237.7 45.5 %collective-permute-start.18 = (bf16[4,120,768]{2,1,0:T(8,128)(2,1)}, bf16[4,120,768]{2,1,0:T(8,128)(2,1)}, u32[]{:S(2)}, u32[]{:S(2)}) collective-permute-start(bf16[4,120,768]{2,1,0:T(8,128)(2,1)} %get-tuple-element.86), channel_id=1, source_target_pairs={{0,8},{8,0},{16,24},{24,16},{1,9},{9,1},{17,25},{25,17},{2,10},{10... | collective-permute-start | bytes 2211848 | tf_op jit(solution)/shard_map/ppermute | solution.py:648
  239.0 44.1 %collective-permute-start.19 = (bf16[4,120,768]{2,1,0:T(8,128)(2,1)}, bf16[4,120,768]{2,1,0:T(8,128)(2,1)}, u32[]{:S(2)}, u32[]{:S(2)}) collective-permute-start(bf16[4,120,768]{2,1,0:T(8,128)(2,1)} %get-tuple-element.88), channel_id=1, source_target_pairs={{0,16},{8,24},{16,0},{24,8},{1,17},{9,25},{17,1},{25,9},{2,18},{10... | collective-permute-start | bytes 2211848 | tf_op jit(solution)/shard_map/ppermute | solution.py:648
  240.6 42.5 %collective-permute-start.20 = (bf16[4,120,768]{2,1,0:T(8,128)(2,1)}, bf16[4,120,768]{2,1,0:T(8,128)(2,1)}, u32[]{:S(2)}, u32[]{:S(2)}) collective-permute-start(bf16[4,120,768]{2,1,0:T(8,128)(2,1)} %get-tuple-element.87), channel_id=1, source_target_pairs={{0,24},{8,16},{16,8},{24,0},{1,25},{9,17},{17,9},{25,1},{2,26},{10... | collective-permute-start | bytes 2211848 | tf_op jit(solution)/shard_map/ppermute | solution.py:648
  242.0 36.7 %collective-permute-start.27 = (bf16[192,768]{1,0:T(8,128)(2,1)}, bf16[192,768]{1,0:T(8,128)(2,1)}, u32[]{:S(2)}, u32[]{:S(2)}) collective-permute-start(bf16[192,768]{1,0:T(8,128)(2,1)} %get-tuple-element.105), channel_id=1, source_target_pairs={{0,8},{8,0},{16,24},{24,16},{1,9},{9,1},{17,25},{25,17},{2,10},{10... | collective-permute-start | bytes 884744 | tf_op jit(solution)/shard_map/ppermute | solution.py:648
  243.4 36.4 %collective-permute-start.29 = (bf16[192,768]{1,0:T(8,128)(2,1)}, bf16[192,768]{1,0:T(8,128)(2,1)}, u32[]{:S(2)}, u32[]{:S(2)}) collective-permute-start(bf16[192,768]{1,0:T(8,128)(2,1)} %get-tuple-element.106), channel_id=1, source_target_pairs={{0,16},{8,24},{16,0},{24,8},{1,17},{9,25},{17,1},{25,9},{2,18},{10... | collective-permute-start | bytes 884744 | tf_op jit(solution)/shard_map/ppermute | solution.py:648
  281.0 8.0 %collective-permute-start.28 = (bf16[192,768]{1,0:T(8,128)(2,1)S(1)}, bf16[192,768]{1,0:T(8,128)(2,1)S(1)}, u32[]{:S(2)}, u32[]{:S(2)}) collective-permute-start(bf16[192,768]{1,0:T(8,128)(2,1)S(1)} %get-tuple-element.103), channel_id=1, source_target_pairs={{0,16},{8,24},{16,0},{24,8},{1,17},{9,25},{17,1},{25,9},{2,18},{10... | collective-permute-start | bytes 884744 | tf_op jit(solution)/shard_map/ppermute | solution.py:648
  282.6 35.9 %collective-permute-start.30 = (bf16[192,768]{1,0:T(8,128)(2,1)S(1)}, bf16[192,768]{1,0:T(8,128)(2,1)S(1)}, u32[]{:S(2)}, u32[]{:S(2)}) collective-permute-start(bf16[192,768]{1,0:T(8,128)(2,1)S(1)} %get-tuple-element.104), channel_id=1, source_target_pairs={{0,8},{8,0},{16,24},{24,16},{1,9},{9,1},{17,25},{25,17},{2,10},{10... | collective-permute-start | bytes 884744 | tf_op jit(solution)/shard_map/ppermute | solution.py:648
  285.1 11.5 %collective-permute-start.21 = (bf16[120,768]{1,0:T(8,128)(2,1)S(1)}, bf16[120,768]{1,0:T(8,128)(2,1)S(1)}, u32[]{:S(2)}, u32[]{:S(2)}) collective-permute-start(bf16[120,768]{1,0:T(8,128)(2,1)S(1)} %get-tuple-element.100), channel_id=1, source_target_pairs={{0,2},{1,3},{2,0},{3,1},{4,6},{5,7},{6,4},{7,5},{8,10},{9,11},{10,... | collective-permute-start | bytes 552968 | tf_op jit(solution)/shard_map/ppermute | solution.py:648
  285.6 18.0 %collective-permute-start.22 = (bf16[120,768]{1,0:T(8,128)(2,1)S(1)}, bf16[120,768]{1,0:T(8,128)(2,1)S(1)}, u32[]{:S(2)}, u32[]{:S(2)}) collective-permute-start(bf16[120,768]{1,0:T(8,128)(2,1)S(1)} %get-tuple-element.102), channel_id=1, source_target_pairs={{0,4},{1,5},{2,6},{3,7},{4,0},{5,1},{6,2},{7,3},{8,12},{9,13},{10,... | collective-permute-start | bytes 552968 | tf_op jit(solution)/shard_map/ppermute | solution.py:648
  287.0 27.8 %collective-permute-start.23 = (bf16[120,768]{1,0:T(8,128)(2,1)S(1)}, bf16[120,768]{1,0:T(8,128)(2,1)S(1)}, u32[]{:S(2)}, u32[]{:S(2)}) collective-permute-start(bf16[120,768]{1,0:T(8,128)(2,1)S(1)} %get-tuple-element.101), channel_id=1, source_target_pairs={{0,6},{1,7},{2,4},{3,5},{4,2},{5,3},{6,0},{7,1},{8,14},{9,15},{10,... | collective-permute-start | bytes 552968 | tf_op jit(solution)/shard_map/ppermute | solution.py:648
  314.9 6.8 %collective-permute-start.24 = (bf16[120,768]{1,0:T(8,128)(2,1)S(1)}, bf16[120,768]{1,0:T(8,128)(2,1)S(1)}, u32[]{:S(2)}, u32[]{:S(2)}) collective-permute-start(bf16[120,768]{1,0:T(8,128)(2,1)S(1)} %fusion.5), channel_id=1, source_target_pairs={{0,8},{8,0},{16,24},{24,16},{1,9},{9,1},{17,25},{25,17},{2,10},{10... | collective-permute-start | bytes 552968 | tf_op jit(solution)/shard_map/ppermute | solution.py:648
  315.9 7.9 %collective-permute-start.25 = (bf16[120,768]{1,0:T(8,128)(2,1)S(1)}, bf16[120,768]{1,0:T(8,128)(2,1)S(1)}, u32[]{:S(2)}, u32[]{:S(2)}) collective-permute-start(bf16[120,768]{1,0:T(8,128)(2,1)S(1)} %fusion.5), channel_id=1, source_target_pairs={{0,16},{8,24},{16,0},{24,8},{1,17},{9,25},{17,1},{25,9},{2,18},{10... | collective-permute-start | bytes 552968 | tf_op jit(solution)/shard_map/ppermute | solution.py:648
  315.9 7.9 %collective-permute-start.26 = (bf16[120,768]{1,0:T(8,128)(2,1)S(1)}, bf16[120,768]{1,0:T(8,128)(2,1)S(1)}, u32[]{:S(2)}, u32[]{:S(2)}) collective-permute-start(bf16[120,768]{1,0:T(8,128)(2,1)S(1)} %fusion.5), channel_id=1, source_target_pairs={{0,24},{8,16},{16,8},{24,0},{1,25},{9,17},{17,9},{25,1},{2,26},{10... | collective-permute-start | bytes 552968 | tf_op jit(solution)/shard_map/ppermute | solution.py:648
  318.6 5.4 %copy-start.4 = (bf16[288,768]{1,0:T(8,128)(2,1)S(1)}, bf16[288,768]{1,0:T(8,128)(2,1)}, u32[]{:S(2)}) copy-start(bf16[288,768]{1,0:T(8,128)(2,1)} %reduce-scatter.6.cloned.1.call-done) | copy-start | bytes 1327108
  324.0 6.0 %collective-permute-start.14 = (bf16[144,768]{1,0:T(8,128)(2,1)S(1)}, bf16[144,768]{1,0:T(8,128)(2,1)S(1)}, u32[]{:S(2)}, u32[]{:S(2)}) collective-permute-start(bf16[144,768]{1,0:T(8,128)(2,1)S(1)} %get-tuple-element.109), channel_id=1, source_target_pairs={{0,8},{8,0},{16,24},{24,16},{1,9},{9,1},{17,25},{25,17},{2,10},{10... | collective-permute-start | bytes 663560 | tf_op jit(solution)/shard_map/ppermute | solution.py:648
  326.1 8.2 %collective-permute-start.16 = (bf16[144,768]{1,0:T(8,128)(2,1)S(1)}, bf16[144,768]{1,0:T(8,128)(2,1)S(1)}, u32[]{:S(2)}, u32[]{:S(2)}) collective-permute-start(bf16[144,768]{1,0:T(8,128)(2,1)S(1)} %get-tuple-element.110), channel_id=1, source_target_pairs={{0,16},{8,24},{16,0},{24,8},{1,17},{9,25},{17,1},{25,9},{2,18},{10... | collective-permute-start | bytes 663560 | tf_op jit(solution)/shard_map/ppermute | solution.py:648
  334.3 6.0 %collective-permute-start.15 = (bf16[144,768]{1,0:T(8,128)(2,1)S(1)}, bf16[144,768]{1,0:T(8,128)(2,1)S(1)}, u32[]{:S(2)}, u32[]{:S(2)}) collective-permute-start(bf16[144,768]{1,0:T(8,128)(2,1)S(1)} %get-tuple-element.107), channel_id=1, source_target_pairs={{0,16},{8,24},{16,0},{24,8},{1,17},{9,25},{17,1},{25,9},{2,18},{10... | collective-permute-start | bytes 663560 | tf_op jit(solution)/shard_map/ppermute | solution.py:648
  335.2 5.9 %collective-permute-start.17 = (bf16[144,768]{1,0:T(8,128)(2,1)S(1)}, bf16[144,768]{1,0:T(8,128)(2,1)S(1)}, u32[]{:S(2)}, u32[]{:S(2)}) collective-permute-start(bf16[144,768]{1,0:T(8,128)(2,1)S(1)} %get-tuple-element.108), channel_id=1, source_target_pairs={{0,8},{8,0},{16,24},{24,16},{1,9},{9,1},{17,25},{25,17},{2,10},{10... | collective-permute-start | bytes 663560 | tf_op jit(solution)/shard_map/ppermute | solution.py:648
  341.3 8.3 %copy-start.6 = (bf16[144,768]{1,0:T(8,128)(2,1)S(1)}, bf16[144,768]{1,0:T(8,128)(2,1)}, u32[]{:S(2)}) copy-start(bf16[144,768]{1,0:T(8,128)(2,1)} %reduce-scatter.8.cloned.1.call-done) | copy-start | bytes 663556
  342.1 3.7 %collective-permute-start.10 = (bf16[8,768]{1,0:T(8,128)(2,1)S(1)}, bf16[8,768]{1,0:T(8,128)(2,1)S(1)}, u32[]{:S(2)}, u32[]{:S(2)}) collective-permute-start(bf16[8,768]{1,0:T(8,128)(2,1)S(1)} %get-tuple-element.116), channel_id=1, source_target_pairs={{0,8},{8,0},{16,24},{24,16},{1,9},{9,1},{17,25},{25,17},{2,10},{10... | collective-permute-start | bytes 36872 | tf_op jit(solution)/shard_map/ppermute | solution.py:648
  343.9 3.7 %collective-permute-start.12 = (bf16[8,768]{1,0:T(8,128)(2,1)S(1)}, bf16[8,768]{1,0:T(8,128)(2,1)S(1)}, u32[]{:S(2)}, u32[]{:S(2)}) collective-permute-start(bf16[8,768]{1,0:T(8,128)(2,1)S(1)} %get-tuple-element.117), channel_id=1, source_target_pairs={{0,16},{8,24},{16,0},{24,8},{1,17},{9,25},{17,1},{25,9},{2,18},{10... | collective-permute-start | bytes 36872 | tf_op jit(solution)/shard_map/ppermute | solution.py:648
  348.3 6.2 %collective-permute-start.11 = (bf16[8,768]{1,0:T(8,128)(2,1)S(1)}, bf16[8,768]{1,0:T(8,128)(2,1)S(1)}, u32[]{:S(2)}, u32[]{:S(2)}) collective-permute-start(bf16[8,768]{1,0:T(8,128)(2,1)S(1)} %get-tuple-element.114), channel_id=1, source_target_pairs={{0,16},{8,24},{16,0},{24,8},{1,17},{9,25},{17,1},{25,9},{2,18},{10... | collective-permute-start | bytes 36872 | tf_op jit(solution)/shard_map/ppermute | solution.py:648
  350.2 7.9 %copy-start.1 = (bf16[96,3072]{1,0:T(8,128)(2,1)S(1)}, bf16[96,3072]{1,0:T(8,128)(2,1)}, u32[]{:S(2)}) copy-start(bf16[96,3072]{1,0:T(8,128)(2,1)} %param.25) | copy-start | bytes 1769476
  352.5 3.7 %collective-permute-start.13 = (bf16[8,768]{1,0:T(8,128)(2,1)S(1)}, bf16[8,768]{1,0:T(8,128)(2,1)S(1)}, u32[]{:S(2)}, u32[]{:S(2)}) collective-permute-start(bf16[8,768]{1,0:T(8,128)(2,1)S(1)} %get-tuple-element.115), channel_id=1, source_target_pairs={{0,8},{8,0},{16,24},{24,16},{1,9},{9,1},{17,25},{25,17},{2,10},{10... | collective-permute-start | bytes 36872 | tf_op jit(solution)/shard_map/ppermute | solution.py:648
  (11 other events, 25.7 us)
Sparse Core Ops, SparseCore 0:
  10.2 31.9 all-gather.11
  44.4 53.7 all-gather.9
  99.8 49.9 all-gather.7
  166.4 52.4 reduce-scatter.3
  236.3 41.0 reduce-scatter.5
  279.6 45.0 reduce-scatter.7

commit v3 on v2

--- a/solution.py
+++ b/solution.py
@@ -56,56 +56,39 @@
     plen = ns * PR_DEV
     keys = plen + cont
     dsh = width // ns
-    step = cont // PR_DEV
-    chunks = ns // step
-
-    def kern(sh_ref, g_ref, t_ref, vec_ref, h_ref, q_ref, k_ref, v_ref, x_ref):
-        i = pl.program_id(0)
+
+    def kern(sh_ref, g_ref, t_ref, vec_ref, h_ref, q_ref, k_ref, v_ref):
         gain, bias, bq, bv = vec_ref[0:1], vec_ref[1:2], vec_ref[2:3], vec_ref[3:4]
         wq, wk, wv = (
             g_ref[:, j * dsh : (j + 1) * dsh, :].reshape(width, width) for j in range(3)
         )
+        step = 4
+
+        def chunk(x, r0):
+            h = (normalize(x.astype(F32))[0] * gain + bias).astype(BF)
+            rows = pl.ds(r0, h.shape[0])
+            h_ref[rows, :] = h
+            k_ref[rows, :] = dot_nn(h, wk).astype(BF)
+            v_ref[rows, :] = (dot_nn(h, wv) + bv).astype(BF)
 
         def to_q(h):
             return ((dot_nn(h, wq) + bq).astype(BF).astype(F32) * SCALE).astype(BF)
 
-        @pl.when(i < chunks)
-        def _():
-            x = g_ref[pl.ds(i * step, step), 3 * dsh : 3 * dsh + PR_DEV, :]
-            x_ref[...] = x.reshape(cont, width)
-
-        @pl.when(i == chunks)
-        def _():
-            x_ref[...] = t_ref[PR_DEV:, :]
-
-        h = (normalize(x_ref[...].astype(F32))[0] * gain + bias).astype(BF)
-        h_ref[...] = h
-        k_ref[...] = dot_nn(h, wk).astype(BF)
-        v_ref[...] = (dot_nn(h, wv) + bv).astype(BF)
-
-        @pl.when(i == sh_ref[0] // step)
-        def _():
-            own = pl.multiple_of((sh_ref[0] % step) * PR_DEV, PR_DEV)
-            q_ref[:PR_DEV, :] = to_q(h_ref[pl.ds(own, PR_DEV), :])
-
-        @pl.when(i == chunks)
-        def _():
-            q_ref[PR_DEV:, :] = to_q(h_ref[...])
+        for b in range(0, ns, step):
+            x = g_ref[b : b + step, 3 * dsh : 3 * dsh + PR_DEV, :]
+            chunk(x.reshape(x.shape[0] * PR_DEV, width), b * PR_DEV)
+        chunk(t_ref[PR_DEV:, :], plen)
+        own = pl.multiple_of(sh_ref[0] * PR_DEV, PR_DEV)
+        q_ref[:PR_DEV, :] = to_q(h_ref[pl.ds(own, PR_DEV), :])
+        q_ref[PR_DEV:, :] = to_q(h_ref[plen:, :])
 
     shape = lambda r: jax.ShapeDtypeStruct((r, width), BF)
-    rows = pl.BlockSpec((cont, width), lambda i: (i, 0))
-    return pl.pallas_call(
-        kern,
-        grid=(chunks + 1,),
-        in_specs=[
-            pl.BlockSpec(memory_space=pltpu.SMEM),
-            fixed(bundle.shape),
-            fixed(tokens.shape),
-            fixed(vecs.shape),
-        ],
-        out_specs=[rows, fixed((tok, width)), rows, rows],
+    vm = pl.BlockSpec(memory_space=pltpu.VMEM)
+    return pl.pallas_call(
+        kern,
+        in_specs=[pl.BlockSpec(memory_space=pltpu.SMEM), vm, vm, vm],
+        out_specs=[vm] * 4,
         out_shape=[shape(keys), shape(tok), shape(keys), shape(keys)],
-        scratch_shapes=[pltpu.VMEM((cont, width), BF)],
         compiler_params=pltpu.CompilerParams(vmem_limit_bytes=VMEM_LIMIT),
         cost_estimate=cost(2 * width * width * (2 * keys + tok), 2 * width * (6 * keys)),
         name="qkv",
@@ -648,16 +631,19 @@
     return lax.ppermute(values, axis, [(i, i ^ bit) for i in range(n)])
 
 
-def rep_sum(values):
+def halves_sum(halves, step):
+    bits = [1 << b for b in range(lax.axis_size("rep").bit_length() - 1)]
+    got = [over("rep", v, b) for v, b in zip(halves, (bits[step], bits[-1 - step]))]
+    return [(v.astype(F32) + g.astype(F32)).astype(v.dtype) for v, g in zip(halves, got)]
+
+
+def rep_sum_small(values):
     n = lax.axis_size("rep")
-    bits = [1 << b for b in range(n.bit_length() - 1)]
-    cut = values.shape[0] // 2
-    halves = [values[:cut], values[cut:]]
-    for i in range(len(bits)):
-        steps = (bits[i], bits[-1 - i])
-        got = [over("rep", v, b) for v, b in zip(halves, steps)]
-        halves = [(v.astype(F32) + g.astype(F32)).astype(v.dtype) for v, g in zip(halves, got)]
-    return jnp.concatenate(halves)
+    terms = [values] + [over("rep", values, b) for b in range(1, n)]
+    terms = [t.astype(F32) for t in terms]
+    while len(terms) > 1:
+        terms = [terms[i] + terms[i + 1] for i in range(0, len(terms), 2)]
+    return terms[0]
 
 
 def local(
@@ -712,7 +698,7 @@
         + [jnp.zeros((16 - 8 - nq, width), F32)]
     )
     count = jnp.sum(params[:, offs[8] : offs[8] + counts.shape[0]])
-    token_total = rep_sum(jnp.full((16, 128), count, F32))[0, 0]
+    token_total = rep_sum_small(jnp.full((8, 128), count, F32))[0, 0]
     factor = tok * nr * ns / token_total
     weight = (factor * mask_f).reshape(tok, 1)
 
@@ -739,20 +725,23 @@
     out_half = jnp.swapaxes(out_half.reshape(nz, nq, dsh // nq, width), 0, 1)
     pair = jnp.concatenate([fc_half, out_half], axis=2)
 
+    pick = lambda a, n: lax.dynamic_index_in_dim(a, n, 0, keepdims=False)
+
     dq, dkv, own_proj, pair = lax.optimization_barrier((dq, dkv, own_proj, pair))
     grads = grads_call(h1, dq, dkv, shard, ns)
     own_qkv = lax.psum_scatter(grads.reshape(-1, width), "shard", scatter_dimension=0, tiled=True)
     dq, dkv, grads = lax.optimization_barrier((dq, dkv, grads))
     last_part, ig = dh1_call(bundle, tokens, vecs, dq, dkv, dx1, sums, fc_sums, last, shard)
-    last_part, own_qkv = lax.optimization_barrier((last_part, own_qkv))
-    own = lax.psum_scatter(last_part.reshape(-1, width), "shard", scatter_dimension=0, tiled=True)
-    input_grad = finish_call(ig, own[EXTRA:], tokens, vecs)
-
-    pick = lambda a, n: lax.dynamic_index_in_dim(a, n, 0, keepdims=False)
     quarter = plus(
         pick(pair, group),
         *[over("rep", pick(pair, jnp.bitwise_xor(group, b)), b) for b in range(1, nq)],
     )
+    last_part, own_qkv, quarter, own_proj = lax.optimization_barrier(
+        (last_part, own_qkv, quarter, own_proj)
+    )
+    own = lax.psum_scatter(last_part.reshape(-1, width), "shard", scatter_dimension=0, tiled=True)
+    input_grad = finish_call(ig, own[EXTRA:], tokens, vecs)
+
     z = me // 2
     final = plus(
         pick(quarter, z),
@@ -762,14 +751,20 @@
     while bit < nr:
         final = plus(final, over("rep", final, bit))
         bit *= 2
+    both = jnp.concatenate([own_qkv, own_proj])
+    cut = both.shape[0] // 2
+    both = halves_sum([both[:cut], both[cut:]], 0)
+    final, *both = lax.optimization_barrier((final, *both))
+    for step in range(1, nr.bit_length() - 1):
+        both = halves_sum(both, step)
+    both = jnp.concatenate(both).astype(F32)
+    sum_qkv, sum_proj = both[: 3 * dsh], both[3 * dsh :]
     relative = jnp.stack([final] + [over("rep", final, b) for b in range(1, nq)])
     natural = [pick(relative, jnp.bitwise_xor(group, b)) for b in range(nq)]
     sum_fc = jnp.concatenate([n[:dsh] for n in natural], axis=1).astype(F32)
     sum_out = jnp.concatenate([n[dsh:] for n in natural], axis=0).astype(F32)
 
-    sum_proj = rep_sum(own_proj).astype(F32)
-    sum_qkv = rep_sum(own_qkv).astype(F32)
-    small = rep_sum(own[:EXTRA]).astype(F32)
+    small = rep_sum_small(own[:EXTRA])
 
     def take(first, rows):
         n = rows * dsh

time: 369 us -> 357 us (0.967)
  waiting for transfers between devices: 123 us -> 111 us
    reduce_scatter x1, waiting for transfers between devices: 17 us -> 1.04 us  [local(): lax.psum_scatter(grads.reshape(-1, width), 'shard', scatter_dimension=0,...]
    ppermute x31 -> x27, waiting for transfers between devices: 69.6 us -> 74.5 us  [over(): return lax.ppermute(values, axis, [(i, i ^ bit) for i in range(n)])]
    ppermute x31 -> x27, starting transfers between devices: 32 us -> 28.9 us  [over(): return lax.ppermute(values, axis, [(i, i ^ bit) for i in range(n)])]
  transfers between devices with their start and end apart: 37 -> 33, of which waited for: 19 -> 13; matrix products, arithmetic and copies ran while one was open for 6% -> 6% of each run, Pallas kernels for 35% -> 36%
where the time goes in v3:
time: 357 us; the launch traced here: 351 us
  Pallas kernels  150 us (42%)
  waiting for transfers between devices  111 us (31%)
  starting transfers between devices  29.2 us (8%)
  local copies, waits for them, and re-layouts  17 us (5%)
  between operations  15.8 us (4%)
  other arithmetic  15.2 us (4%)
  blocking collectives  12.4 us (3%)
    ppermute x27, waiting for transfers between devices, over(): return lax.ppermute(values, axis, [(i, i ^ bit) for i in range(n)])  74.5 us
    pallas_call x1, Pallas kernels, attn_bwd(): pl.pallas_call(kern, grid=(npair,), in_specs=[pl.BlockSpec(memory_space=p...  32.3 us
    ppermute x27, starting transfers between devices, over(): return lax.ppermute(values, axis, [(i, i ^ bit) for i in range(n)])  28.9 us
    pallas_call x1, Pallas kernels, mid_call(): pl.pallas_call(kern, grid=(nq + 1,), in_specs=[pl.BlockSpec(memory_space=...  24.6 us
    pallas_call x1, Pallas kernels, attn_fwd(): pl.pallas_call(kern, grid=(npair,), in_specs=[pl.BlockSpec(memory_space=p...  22.9 us
    all_gather x1, waiting for transfers between devices, local(): lax.all_gather(jnp.concatenate([w_qkv[:, :width], w_qkv[:, width:2 * widt...  22.2 us
    pallas_call x1, Pallas kernels, dh1_call(): pl.pallas_call(kern, grid=(chunks + 1,), in_specs=[pl.BlockSpec(memory_sp...  15.7 us
    pallas_call x1, Pallas kernels, proj_call(): pl.pallas_call(kern, grid=(2 * nq,), in_specs=[pl.BlockSpec((1, tok, widt...  15.5 us
  transfers between devices with their start and end apart: 33, of which 13 were waited for; matrix products, arithmetic and copies ran while one was open for 6% of the time, Pallas kernels for 36%

profile of v3, /device:TPU:16, one launch (start us, length us, event | category | flops | bytes accessed | tf_op | source)
XLA Modules:
  0.0 351.0 jit_solution(12845575298306324393)
XLA Ops:
  8.3 1.6 pad_maximum_fusion.6
  10.1 1.1 fusion.14
  13.2 12.4 %all-gather.3 = bf16[8,1,1280]{2,1,0:T(2,128)(2,1)S(1)} all-gather(bf16[1,1,1280]{2,1,0:T(2,128)(2,1)S(1)} %reshape.129), channel_id=3, replica_groups=mesh['rep'=4,'shard'=8] {'shard'}, dimensions={0}, use_global_device_ids=true | all-gather | bytes 23040 | tf_op jit(solution)/shard_map/all_gather | solution.py:695
  26.9 1.5 collective-permute-start.6
  28.4 1.5 collective-permute-start.7
  29.9 12.3 %all-gather.12.cloned.1.call-done = bf16[1536,768]{1,0:T(8,128)(2,1)} async-done(((bf16[192,768]{1,0:T(8,128)(2,1)}), bf16[1536,768]{1,0:T(8,128)(2,1)}) %all-gather.12.cloned.1.call-update) | async-done | bytes 2359312 | tf_op jit(solution)/shard_map/all_gather | solution.py:684
  42.2 1.1 constant_dynamic-slice_fusion.6
  43.3 1.5 collective-permute-start
  44.8 1.5 collective-permute-start.1
  46.9 2.4 collective-permute-start.8
  50.5 1.3 concatenate.32.vec_ref.refs_9_.refs_10_.refs_3_
  51.8 20.7 %collective-permute-done.8 = f32[8,128]{1,0:T(8,128)S(1)} collective-permute-done((f32[8,128]{1,0:T(8,128)S(1)}, f32[8,128]{1,0:T(8,128)S(1)}, u32[]{:S(2)}, u32[]{:S(2)}) %collective-permute-start.8) | collective-permute-done | bytes 4128 | tf_op jit(solution)/shard_map/ppermute | solution.py:631
  75.9 22.2 %all-gather.10.cloned.1.call-done = bf16[3328,768]{1,0:T(8,128)(2,1)} async-done(((bf16[416,768]{1,0:T(8,128)(2,1)}), bf16[3328,768]{1,0:T(8,128)(2,1)}) %all-gather.10.cloned.1.call-update) | async-done | bytes 5111824 | tf_op jit(solution)/shard_map/all_gather | solution.py:677
  98.1 9.9 %qkv.1 = (bf16[1536,768]{1,0:T(8,128)(2,1)}, bf16[640,768]{1,0:T(8,128)(2,1)}, bf16[1536,768]{1,0:T(8,128)(2,1)}, bf16[1536,768]{1,0:T(8,128)(2,1)}) custom-call(s32[1]{0:T(128)} %bitcast.2.sh_ref.refs_0_, bf16[8,416,768]{2,1,0:T(8,128)(2,1)} %bitcast.67, bf16[640,768]{1,0:T(8,128)(2,1)} %t_ref.5, f32[16,768]{1,0:T(8,128)} %concatenate.32.vec_ref.refs_9_.refs_10_.refs_3_), custom_call_target="tpu_custom_call" | custom-call | flops 4378853376 | bytes 14155776 | tf_op jit(solution)/shard_map/qkv/pallas_call | solution.py:87
  108.0 22.9 %attn_fwd.1 = (bf16[640,768]{1,0:T(8,128)(2,1)}, f32[6,2,640]{2,1,0:T(2,128)}) custom-call(s32[1]{0:T(128)} %bitcast.2.sh_ref.refs_0_, bf16[640,768]{1,0:T(8,128)(2,1)} %get-tuple-element.55.q_ref, bf16[1536,768]{1,0:T(8,128)(2,1)} %get-tuple-element.56.k_ref, bf16[1536,768]{1,0:T(8,128)(2,1)} %get-tuple-element.57.v_ref), custom_call_target="tpu_custom_call" | custom-call | flops 12079595520 | bytes 6684672 | tf_op jit(solution)/shard_map/attn_fwd/pallas_call | solution.py:136
  130.9 4.5 %out_proj.1 = (f32[640,768]{1,0:T(8,128)}, bf16[640,768]{1,0:T(8,128)(2,1)}) custom-call(bf16[640,768]{1,0:T(8,128)(2,1)} %get-tuple-element.58.o_ref.refs_8_, bf16[8,192,768]{2,1,0:T(8,128)(2,1)} %bitcast.70, bf16[640,768]{1,0:T(8,128)(2,1)} %t_ref.5, f32[16,768]{1,0:T(8,128)} %concatenate.32.vec_ref.refs_9_.refs_10_.refs_3_), custom_call_target="tpu_custom_call" | custom-call | flops 754974720 | bytes 5898240 | tf_op jit(solution)/shard_map/out_proj/pallas_call | solution.py:240
  136.5 12.6 %fc.1 = (bf16[4,640,768]{2,1,0:T(8,128)(2,1)}, bf16[4,640,768]{2,1,0:T(8,128)(2,1)}, bf16[4,768,768]{2,1,0:T(8,128)(2,1)}) custom-call(s32[2]{0:T(128)} %pad_add_fusion.refs_0_, bf16[640,768]{1,0:T(8,128)(2,1)} %get-tuple-element.59.refs_1_.refs_5_, bf16[8,192,768]{2,1,0:T(8,128)(2,1)} %bitcast.71, bf16[4,96,768]{2,1,0:T(8,128)(2,1)} %copy-done.17, ...), custom_call_target="tpu_custom_call" | custom-call | flops 3019898880 | bytes 17301504 | tf_op jit(solution)/shard_map/fc/pallas_call | solution.py:296
  149.7 15.5 %proj.1 = (bf16[640,768]{1,0:T(8,128)(2,1)}, f32[640,768]{1,0:T(8,128)}, bf16[640,768]{1,0:T(8,128)(2,1)}, bf16[3072,768]{1,0:T(8,128)(2,1)}, f32[8,768]{1,0:T(8,128)}) custom-call(bf16[4,640,768]{2,1,0:T(8,128)(2,1)} %get-tuple-element.60.g_ref, bf16[3072,768]{1,0:T(8,128)(2,1)} %all-gather.8.cloned.1.call-done.w_ref.refs_3_, ...), custom_call_target="tpu_custom_call" | custom-call | flops 6039797760 | bytes 13369344 | tf_op jit(solution)/shard_map/proj/pallas_call | solution.py:353
  165.3 24.6 %mid.1 = (bf16[4,4,96,768]{3,2,1,0:T(8,128)(2,1)}, bf16[4,4,96,768]{3,2,1,0:T(8,128)(2,1)}, bf16[4,96,768]{2,1,0:T(8,128)(2,1)}, bf16[4,96,768]{2,1,0:T(8,128)(2...) custom-call(s32[1]{0:T(128)} %bitcast.1.refs_0_, ...), custom_call_target="tpu_custom_call" | custom-call | flops 10569646080 | bytes 30670848 | tf_op jit(solution)/shard_map/mid/pallas_call | solution.py:432
  190.5 32.3 %attn_bwd.1 = (bf16[640,768]{1,0:T(8,128)(2,1)}, bf16[2,1536,768]{2,1,0:T(8,128)(2,1)}) custom-call(s32[1]{0:T(128)} %bitcast.2.sh_ref.refs_0_, bf16[640,768]{1,0:T(8,128)(2,1)} %get-tuple-element.55.q_ref, bf16[1536,768]{1,0:T(8,128)(2,1)} %get-tuple-element.56.k_ref, bf16[1536,768]{1,0:T(8,128)(2,1)} %get-tuple-element.57.v_ref, ...), custom_call_target="tpu_custom_call" | custom-call | flops 30198988800 | bytes 13369344 | tf_op jit(solution)/shard_map/attn_bwd/pallas_call | solution.py:204
  223.1 1.4 copy-done.4
  225.5 9.6 %grads.1 = bf16[8,288,768]{2,1,0:T(8,128)(2,1)} custom-call(s32[1]{0:T(128)} %bitcast.2.sh_ref.refs_0_, bf16[1536,768]{1,0:T(8,128)(2,1)} %get-tuple-element.78.h_ref, bf16[640,768]{1,0:T(8,128)(2,1)} %get-tuple-element.79.dq_ref.refs_4_, bf16[2,1536,768]{2,1,0:T(8,128)(2,1)} %get-tuple-element.80.d_ref.refs_5_.refs_6_), custom_call_target="tpu_custom_call" | custom-call | flops 4378853376 | bytes 11796480 | tf_op jit(solution)/shard_map/grads/pallas_call | solution.py:500
  235.1 1.4 dynamic-slice_bitcast_fusion.2
  236.5 1.5 collective-permute-start.11
  238.0 1.5 collective-permute-start.12
  240.0 15.7 %dh1.1 = (bf16[8,144,768]{2,1,0:T(8,128)(2,1)}, f32[640,768]{1,0:T(8,128)}) custom-call(s32[1]{0:T(128)} %bitcast.2.sh_ref.refs_0_, bf16[8,416,768]{2,1,0:T(8,128)(2,1)} %bitcast.68, bf16[640,768]{1,0:T(8,128)(2,1)} %t_ref.5, f32[16,768]{1,0:T(8,128)} %concatenate.32.vec_ref.refs_9_.refs_10_.refs_3_, bf16[640,768]{1,0:T(8,128)(2,1)} %get-tuple-element.79.dq_ref.refs_4_, ...), custom_call_target="tpu_custom_call" | custom-call | flops 4378853376 | bytes 15728640 | tf_op jit(solution)/shard_map/dh1/pallas_call | solution.py:584
  256.2 16.2 %collective-permute-done.12 = bf16[4,120,768]{2,1,0:T(8,128)(2,1)} collective-permute-done((bf16[4,120,768]{2,1,0:T(8,128)(2,1)}, bf16[4,120,768]{2,1,0:T(8,128)(2,1)}, u32[]{:S(2)}, u32[]{:S(2)}) %collective-permute-start.12) | collective-permute-done | bytes 737312 | tf_op jit(solution)/shard_map/ppermute | solution.py:631
  272.4 2.8 fusion.2
  275.2 1.0 reduce-scatter.6.cloned.1.call-done
  277.3 1.5 collective-permute-start.21
  278.9 1.6 collective-permute-start.17
  280.5 1.8 collective-permute-start.18
  282.7 1.5 collective-permute-start.20
  284.2 6.3 %collective-permute-done.17 = bf16[120,768]{1,0:T(8,128)(2,1)S(1)} collective-permute-done((bf16[120,768]{1,0:T(8,128)(2,1)S(1)}, bf16[120,768]{1,0:T(8,128)(2,1)S(1)}, u32[]{:S(2)}, u32[]{:S(2)}) %collective-permute-start.17) | collective-permute-done | bytes 184352 | tf_op jit(solution)/shard_map/ppermute | solution.py:631
  290.5 6.6 %collective-permute-done.18 = bf16[120,768]{1,0:T(8,128)(2,1)S(1)} collective-permute-done((bf16[120,768]{1,0:T(8,128)(2,1)S(1)}, bf16[120,768]{1,0:T(8,128)(2,1)S(1)}, u32[]{:S(2)}, u32[]{:S(2)}) %collective-permute-start.18) | collective-permute-done | bytes 184352 | tf_op jit(solution)/shard_map/ppermute | solution.py:631
  297.1 10.7 %collective-permute-done.19 = bf16[120,768]{1,0:T(8,128)(2,1)S(1)} collective-permute-done((bf16[120,768]{1,0:T(8,128)(2,1)S(1)}, bf16[120,768]{1,0:T(8,128)(2,1)S(1)}, u32[]{:S(2)}, u32[]{:S(2)}) %collective-permute-start.19) | collective-permute-done | bytes 184352 | tf_op jit(solution)/shard_map/ppermute | solution.py:631
  307.9 1.2 add_convert_fusion.4
  309.1 1.2 add_convert_fusion.5
  310.2 1.6 collective-permute-start.24
  311.8 2.0 collective-permute-start.26
  313.8 1.5 collective-permute-start.23
  315.3 2.5 collective-permute-done.24
  317.8 3.8 %collective-permute-done.25 = bf16[120,768]{1,0:T(8,128)(2,1)S(1)} collective-permute-done((bf16[120,768]{1,0:T(8,128)(2,1)S(1)}, bf16[120,768]{1,0:T(8,128)(2,1)S(1)}, u32[]{:S(2)}, u32[]{:S(2)}) %collective-permute-start.25) | collective-permute-done | bytes 184352 | tf_op jit(solution)/shard_map/ppermute | solution.py:631
  322.6 1.1 maximum_convert_fusion
  323.7 7.1 %collective-permute-done.22 = bf16[336,768]{1,0:T(8,128)(2,1)S(1)} collective-permute-done((bf16[336,768]{1,0:T(8,128)(2,1)S(1)}, bf16[336,768]{1,0:T(8,128)(2,1)S(1)}, u32[]{:S(2)}, u32[]{:S(2)}) %collective-permute-start.22) | collective-permute-done | bytes 516128 | tf_op jit(solution)/shard_map/ppermute | solution.py:631
  334.2 2.3 collective-permute-start.16
  336.4 1.1 fusion.3
  338.2 2.3 finish.1
  (145 shorter events, 23.1 us)
Async XLA Ops:
  7.2 4.0 %slice-start = ((bf16[640,768]{1,0:T(8,128)(2,1)}), bf16[128,768]{1,0:T(8,128)(2,1)S(1)}, s32[]{:S(2)}) async-start(bf16[640,768]{1,0:T(8,128)(2,1)} %t_ref.5), calls=%async_computation.9 | async-start | bytes 393216 | tf_op jit(solution)/shard_map/slice | solution.py:679
  7.2 35.0 %all-gather.12.cloned.1.call-start = ((), (), s32[]{:S(2)}) async-start(), calls=%async_computation.8 | async-start | bytes 2654208 | tf_op jit(solution)/shard_map/all_gather | solution.py:684
  9.9 3.1 copy-start.9
  10.0 3.1 copy-start.10
  10.0 3.0 copy-start.11
  10.0 3.0 copy-start.12
  10.0 3.0 copy-start.13
  10.0 3.0 copy-start.14
  10.0 3.0 copy-start.15
  10.0 88.1 %all-gather.10.cloned.1.call-start = ((), (), s32[]{:S(2)}) async-start(), calls=%async_computation.7 | async-start | bytes 5750784 | tf_op jit(solution)/shard_map/all_gather | solution.py:677
  12.1 137.7 %all-gather.8.cloned.1.call-start = ((), (), s32[]{:S(2)}) async-start(), calls=%async_computation.3 | async-start | bytes 5308416 | tf_op jit(solution)/shard_map/all_gather | solution.py:685
  12.8 212.6 %reduce-scatter.4.cloned.1.call-start = ((), (), s32[]{:S(2)}) async-start(), calls=%async_computation.4 | async-start | bytes 5308416 | tf_op jit(solution)/shard_map/reduce_scatter | solution.py:715
  26.9 20.0 %collective-permute-start.6 = (f32[8,128]{1,0:T(8,128)S(1)}, f32[8,128]{1,0:T(8,128)S(1)}, u32[]{:S(2)}, u32[]{:S(2)}) collective-permute-start(f32[8,128]{1,0:T(8,128)S(1)} %broadcast_in_dim.7), channel_id=1, source_target_pairs={{0,8},{8,0},{16,24},{24,16},{1,9},{9,1},{17,25},{25,17},{2,10},{10... | collective-permute-start | bytes 12296 | tf_op jit(solution)/shard_map/ppermute | solution.py:631
  28.4 23.5 %collective-permute-start.7 = (f32[8,128]{1,0:T(8,128)S(1)}, f32[8,128]{1,0:T(8,128)S(1)}, u32[]{:S(2)}, u32[]{:S(2)}) collective-permute-start(f32[8,128]{1,0:T(8,128)S(1)} %broadcast_in_dim.7), channel_id=1, source_target_pairs={{0,16},{8,24},{16,0},{24,8},{1,17},{9,25},{17,1},{25,9},{2,18},{10... | collective-permute-start | bytes 12296 | tf_op jit(solution)/shard_map/ppermute | solution.py:631
  43.3 32.0 %collective-permute-start = (bf16[4,96,768]{2,1,0:T(8,128)(2,1)S(1)}, bf16[4,96,768]{2,1,0:T(8,128)(2,1)S(1)}, u32[]{:S(2)}, u32[]{:S(2)}) collective-permute-start(bf16[4,96,768]{2,1,0:T(8,128)(2,1)S(1)} %constant_dynamic-slice_fusion.6), channel_id=1, source_target_pairs={{0,8},{8,0},{16,24},{24,16},{1,9},{9,1},{17,25},{25,17},{2,10},{10... | collective-permute-start | bytes 1769480 | tf_op jit(solution)/shard_map/ppermute | solution.py:631
  44.8 30.5 %collective-permute-start.1 = (bf16[4,96,768]{2,1,0:T(8,128)(2,1)S(1)}, bf16[4,96,768]{2,1,0:T(8,128)(2,1)S(1)}, u32[]{:S(2)}, u32[]{:S(2)}) collective-permute-start(bf16[4,96,768]{2,1,0:T(8,128)(2,1)S(1)} %constant_dynamic-slice_fusion.6), channel_id=1, source_target_pairs={{0,16},{8,24},{16,0},{24,8},{1,17},{9,25},{17,1},{25,9},{2,18},{10... | collective-permute-start | bytes 1769480 | tf_op jit(solution)/shard_map/ppermute | solution.py:631
  46.3 29.5 %collective-permute-start.2 = (bf16[4,96,768]{2,1,0:T(8,128)(2,1)S(1)}, bf16[4,96,768]{2,1,0:T(8,128)(2,1)S(1)}, u32[]{:S(2)}, u32[]{:S(2)}) collective-permute-start(bf16[4,96,768]{2,1,0:T(8,128)(2,1)S(1)} %constant_dynamic-slice_fusion.6), channel_id=1, source_target_pairs={{0,24},{8,16},{16,8},{24,0},{1,25},{9,17},{17,9},{25,1},{2,26},{10... | collective-permute-start | bytes 1769480 | tf_op jit(solution)/shard_map/ppermute | solution.py:631
  46.9 25.6 %collective-permute-start.8 = (f32[8,128]{1,0:T(8,128)S(1)}, f32[8,128]{1,0:T(8,128)S(1)}, u32[]{:S(2)}, u32[]{:S(2)}) collective-permute-start(f32[8,128]{1,0:T(8,128)S(1)} %broadcast_in_dim.7), channel_id=1, source_target_pairs={{0,24},{8,16},{16,8},{24,0},{1,25},{9,17},{17,9},{25,1},{2,26},{10... | collective-permute-start | bytes 12296 | tf_op jit(solution)/shard_map/ppermute | solution.py:631
  75.3 32.7 %copy-start.17 = (bf16[4,96,768]{2,1,0:T(8,128)(2,1)}, bf16[4,96,768]{2,1,0:T(8,128)(2,1)S(1)}, u32[]{:S(2)}) copy-start(bf16[4,96,768]{2,1,0:T(8,128)(2,1)S(1)} %collective-permute-done.refs_3_) | copy-start | bytes 1769476
  75.3 60.2 %collective-permute-start.3 = (bf16[4,96,768]{2,1,0:T(8,128)(2,1)S(1)}, bf16[4,96,768]{2,1,0:T(8,128)(2,1)S(1)}, u32[]{:S(2)}, u32[]{:S(2)}) collective-permute-start(bf16[4,96,768]{2,1,0:T(8,128)(2,1)S(1)} %collective-permute-done.refs_3_), channel_id=1, source_target_pairs={{0,1},{1,0},{2,3},{3,2},{4,5},{5,4},{6,7},{7,6},{8,9},{9,8},{10,11... | collective-permute-start | bytes 1769480 | tf_op jit(solution)/shard_map/ppermute | solution.py:631
  75.3 32.7 %copy-start.18 = (bf16[4,96,768]{2,1,0:T(8,128)(2,1)}, bf16[4,96,768]{2,1,0:T(8,128)(2,1)S(1)}, u32[]{:S(2)}) copy-start(bf16[4,96,768]{2,1,0:T(8,128)(2,1)S(1)} %collective-permute-done.1.refs_4_) | copy-start | bytes 1769476
  75.3 60.1 %collective-permute-start.4 = (bf16[4,96,768]{2,1,0:T(8,128)(2,1)S(1)}, bf16[4,96,768]{2,1,0:T(8,128)(2,1)}, u32[]{:S(2)}, u32[]{:S(2)}) collective-permute-start(bf16[4,96,768]{2,1,0:T(8,128)(2,1)S(1)} %collective-permute-done.1.refs_4_), channel_id=1, source_target_pairs={{0,1},{1,0},{2,3},{3,2},{4,5},{5,4},{6,7},{7,6},{8,9},{9,8},{10,11... | collective-permute-start | bytes 1769480 | tf_op jit(solution)/shard_map/ppermute | solution.py:631
  75.8 32.2 %copy-start.19 = (bf16[4,96,768]{2,1,0:T(8,128)(2,1)}, bf16[4,96,768]{2,1,0:T(8,128)(2,1)S(1)}, u32[]{:S(2)}) copy-start(bf16[4,96,768]{2,1,0:T(8,128)(2,1)S(1)} %collective-permute-done.2.refs_5_) | copy-start | bytes 1769476
  75.8 59.7 %collective-permute-start.5 = (bf16[4,96,768]{2,1,0:T(8,128)(2,1)S(1)}, bf16[4,96,768]{2,1,0:T(8,128)(2,1)S(1)}, u32[]{:S(2)}, u32[]{:S(2)}) collective-permute-start(bf16[4,96,768]{2,1,0:T(8,128)(2,1)S(1)} %collective-permute-done.2.refs_5_), channel_id=1, source_target_pairs={{0,1},{1,0},{2,3},{3,2},{4,5},{5,4},{6,7},{7,6},{8,9},{9,8},{10,11... | collective-permute-start | bytes 1769480 | tf_op jit(solution)/shard_map/ppermute | solution.py:631
  165.3 111.0 %reduce-scatter.6.cloned.1.call-start = ((), (), s32[]{:S(2)}) async-start(), calls=%async_computation.5 | async-start | bytes 3981312 | tf_op jit(solution)/shard_map/reduce_scatter | solution.py:732
  189.9 33.2 %collective-permute-start.9 = (bf16[4,4,96,768]{3,2,1,0:T(8,128)(2,1)}, bf16[4,4,96,768]{3,2,1,0:T(8,128)(2,1)S(1)}, u32[]{:S(2)}, u32[]{:S(2)}) collective-permute-start(bf16[4,4,96,768]{3,2,1,0:T(8,128)(2,1)} %get-tuple-element.73), channel_id=1, source_target_pairs={{0,1},{1,0},{2,3},{3,2},{4,5},{5,4},{6,7},{7,6},{8,9},{9,8},{10,11... | collective-permute-start | bytes 7077896 | tf_op jit(solution)/shard_map/ppermute | solution.py:631
  190.2 32.7 %collective-permute-start.10 = (bf16[4,96,768]{2,1,0:T(8,128)(2,1)}, bf16[4,96,768]{2,1,0:T(8,128)(2,1)S(1)}, u32[]{:S(2)}, u32[]{:S(2)}) collective-permute-start(bf16[4,96,768]{2,1,0:T(8,128)(2,1)} %get-tuple-element.75), channel_id=1, source_target_pairs={{0,1},{1,0},{2,3},{3,2},{4,5},{5,4},{6,7},{7,6},{8,9},{9,8},{10,11... | collective-permute-start | bytes 1769480 | tf_op jit(solution)/shard_map/ppermute | solution.py:631
  190.5 32.4 %copy-start.5 = (bf16[4,96,768]{2,1,0:T(8,128)(2,1)S(1)}, bf16[4,96,768]{2,1,0:T(8,128)(2,1)}, u32[]{:S(2)}) copy-start(bf16[4,96,768]{2,1,0:T(8,128)(2,1)} %get-tuple-element.74) | copy-start | bytes 1769476
  235.0 97.1 %reduce-scatter.8.cloned.1.call-start = ((), (), s32[]{:S(2)}) async-start(), calls=%async_computation.6 | async-start | bytes 1990656 | tf_op jit(solution)/shard_map/reduce_scatter | solution.py:742
  236.5 19.7 %collective-permute-start.11 = (bf16[4,120,768]{2,1,0:T(8,128)(2,1)}, bf16[4,120,768]{2,1,0:T(8,128)(2,1)}, u32[]{:S(2)}, u32[]{:S(2)}) collective-permute-start(bf16[4,120,768]{2,1,0:T(8,128)(2,1)} %get-tuple-element.96), channel_id=1, source_target_pairs={{0,8},{8,0},{16,24},{24,16},{1,9},{9,1},{17,25},{25,17},{2,10},{10... | collective-permute-start | bytes 2211848 | tf_op jit(solution)/shard_map/ppermute | solution.py:631
  238.0 34.4 %collective-permute-start.12 = (bf16[4,120,768]{2,1,0:T(8,128)(2,1)}, bf16[4,120,768]{2,1,0:T(8,128)(2,1)}, u32[]{:S(2)}, u32[]{:S(2)}) collective-permute-start(bf16[4,120,768]{2,1,0:T(8,128)(2,1)} %get-tuple-element.98), channel_id=1, source_target_pairs={{0,16},{8,24},{16,0},{24,8},{1,17},{9,25},{17,1},{25,9},{2,18},{10... | collective-permute-start | bytes 2211848 | tf_op jit(solution)/shard_map/ppermute | solution.py:631
  239.5 33.0 %collective-permute-start.13 = (bf16[4,120,768]{2,1,0:T(8,128)(2,1)}, bf16[4,120,768]{2,1,0:T(8,128)(2,1)}, u32[]{:S(2)}, u32[]{:S(2)}) collective-permute-start(bf16[4,120,768]{2,1,0:T(8,128)(2,1)} %get-tuple-element.97), channel_id=1, source_target_pairs={{0,24},{8,16},{16,8},{24,0},{1,25},{9,17},{17,9},{25,1},{2,26},{10... | collective-permute-start | bytes 2211848 | tf_op jit(solution)/shard_map/ppermute | solution.py:631
  255.7 20.6 %copy-start.2 = (bf16[384,768]{1,0:T(8,128)(2,1)S(1)}, bf16[384,768]{1,0:T(8,128)(2,1)}, u32[]{:S(2)}) copy-start(bf16[384,768]{1,0:T(8,128)(2,1)} %reduce-scatter.4.cloned.1.call-done) | copy-start | bytes 1769476
  277.3 30.5 %collective-permute-start.21 = (bf16[336,768]{1,0:T(8,128)(2,1)S(1)}, bf16[336,768]{1,0:T(8,128)(2,1)}, u32[]{:S(2)}, u32[]{:S(2)}) collective-permute-start(bf16[336,768]{1,0:T(8,128)(2,1)S(1)} %get-tuple-element.113), channel_id=1, source_target_pairs={{0,16},{8,24},{16,0},{24,8},{1,17},{9,25},{17,1},{25,9},{2,18},{10... | collective-permute-start | bytes 1548296 | tf_op jit(solution)/shard_map/ppermute | solution.py:631
  278.9 11.6 %collective-permute-start.17 = (bf16[120,768]{1,0:T(8,128)(2,1)S(1)}, bf16[120,768]{1,0:T(8,128)(2,1)S(1)}, u32[]{:S(2)}, u32[]{:S(2)}) collective-permute-start(bf16[120,768]{1,0:T(8,128)(2,1)S(1)} %get-tuple-element.110), channel_id=1, source_target_pairs={{0,2},{1,3},{2,0},{3,1},{4,6},{5,7},{6,4},{7,5},{8,10},{9,11},{10,... | collective-permute-start | bytes 552968 | tf_op jit(solution)/shard_map/ppermute | solution.py:631
  280.5 16.6 %collective-permute-start.18 = (bf16[120,768]{1,0:T(8,128)(2,1)S(1)}, bf16[120,768]{1,0:T(8,128)(2,1)S(1)}, u32[]{:S(2)}, u32[]{:S(2)}) collective-permute-start(bf16[120,768]{1,0:T(8,128)(2,1)S(1)} %get-tuple-element.112), channel_id=1, source_target_pairs={{0,4},{1,5},{2,6},{3,7},{4,0},{5,1},{6,2},{7,3},{8,12},{9,13},{10,... | collective-permute-start | bytes 552968 | tf_op jit(solution)/shard_map/ppermute | solution.py:631
  282.3 25.5 %collective-permute-start.19 = (bf16[120,768]{1,0:T(8,128)(2,1)S(1)}, bf16[120,768]{1,0:T(8,128)(2,1)S(1)}, u32[]{:S(2)}, u32[]{:S(2)}) collective-permute-start(bf16[120,768]{1,0:T(8,128)(2,1)S(1)} %get-tuple-element.111), channel_id=1, source_target_pairs={{0,6},{1,7},{2,4},{3,5},{4,2},{5,3},{6,0},{7,1},{8,14},{9,15},{10,... | collective-permute-start | bytes 552968 | tf_op jit(solution)/shard_map/ppermute | solution.py:631
  282.7 26.3 %collective-permute-start.20 = (bf16[336,768]{1,0:T(8,128)(2,1)S(1)}, bf16[336,768]{1,0:T(8,128)(2,1)}, u32[]{:S(2)}, u32[]{:S(2)}) collective-permute-start(bf16[336,768]{1,0:T(8,128)(2,1)S(1)} %get-tuple-element.114), channel_id=1, source_target_pairs={{0,8},{8,0},{16,24},{24,16},{1,9},{9,1},{17,25},{25,17},{2,10},{10... | collective-permute-start | bytes 1548296 | tf_op jit(solution)/shard_map/ppermute | solution.py:631
  310.2 7.6 %collective-permute-start.24 = (bf16[120,768]{1,0:T(8,128)(2,1)S(1)}, bf16[120,768]{1,0:T(8,128)(2,1)S(1)}, u32[]{:S(2)}, u32[]{:S(2)}) collective-permute-start(bf16[120,768]{1,0:T(8,128)(2,1)S(1)} %fusion.6), channel_id=1, source_target_pairs={{0,8},{8,0},{16,24},{24,16},{1,9},{9,1},{17,25},{25,17},{2,10},{10... | collective-permute-start | bytes 552968 | tf_op jit(solution)/shard_map/ppermute | solution.py:631
  311.8 9.8 %collective-permute-start.25 = (bf16[120,768]{1,0:T(8,128)(2,1)S(1)}, bf16[120,768]{1,0:T(8,128)(2,1)S(1)}, u32[]{:S(2)}, u32[]{:S(2)}) collective-permute-start(bf16[120,768]{1,0:T(8,128)(2,1)S(1)} %fusion.6), channel_id=1, source_target_pairs={{0,16},{8,24},{16,0},{24,8},{1,17},{9,25},{17,1},{25,9},{2,18},{10... | collective-permute-start | bytes 552968 | tf_op jit(solution)/shard_map/ppermute | solution.py:631
  311.8 9.8 %collective-permute-start.26 = (bf16[120,768]{1,0:T(8,128)(2,1)S(1)}, bf16[120,768]{1,0:T(8,128)(2,1)S(1)}, u32[]{:S(2)}, u32[]{:S(2)}) collective-permute-start(bf16[120,768]{1,0:T(8,128)(2,1)S(1)} %fusion.6), channel_id=1, source_target_pairs={{0,24},{8,16},{16,8},{24,0},{1,25},{9,17},{17,9},{25,1},{2,26},{10... | collective-permute-start | bytes 552968 | tf_op jit(solution)/shard_map/ppermute | solution.py:631
  313.8 17.0 %collective-permute-start.22 = (bf16[336,768]{1,0:T(8,128)(2,1)S(1)}, bf16[336,768]{1,0:T(8,128)(2,1)S(1)}, u32[]{:S(2)}, u32[]{:S(2)}) collective-permute-start(bf16[336,768]{1,0:T(8,128)(2,1)S(1)} %add_convert_fusion.5), channel_id=1, source_target_pairs={{0,16},{8,24},{16,0},{24,8},{1,17},{9,25},{17,1},{25,9},{2,18},{10... | collective-permute-start | bytes 1548296 | tf_op jit(solution)/shard_map/ppermute | solution.py:631
  313.8 17.1 %collective-permute-start.23 = (bf16[336,768]{1,0:T(8,128)(2,1)S(1)}, bf16[336,768]{1,0:T(8,128)(2,1)S(1)}, u32[]{:S(2)}, u32[]{:S(2)}) collective-permute-start(bf16[336,768]{1,0:T(8,128)(2,1)S(1)} %add_convert_fusion.4), channel_id=1, source_target_pairs={{0,8},{8,0},{16,24},{24,16},{1,9},{9,1},{17,25},{25,17},{2,10},{10... | collective-permute-start | bytes 1548296 | tf_op jit(solution)/shard_map/ppermute | solution.py:631
  332.1 5.4 %copy-start.7 = (bf16[144,768]{1,0:T(8,128)(2,1)S(1)}, bf16[144,768]{1,0:T(8,128)(2,1)}, u32[]{:S(2)}) copy-start(bf16[144,768]{1,0:T(8,128)(2,1)} %reduce-scatter.8.cloned.1.call-done) | copy-start | bytes 663556
  332.9 7.6 %collective-permute-start.14 = (bf16[16,768]{1,0:T(8,128)(2,1)S(1)}, bf16[16,768]{1,0:T(8,128)(2,1)S(1)}, u32[]{:S(2)}, u32[]{:S(2)}) collective-permute-start(bf16[16,768]{1,0:T(8,128)(2,1)S(1)} %slice.202), channel_id=1, source_target_pairs={{0,8},{8,0},{16,24},{24,16},{1,9},{9,1},{17,25},{25,17},{2,10},{10... | collective-permute-start | bytes 73736 | tf_op jit(solution)/shard_map/ppermute | solution.py:631
  333.5 7.0 %collective-permute-start.15 = (bf16[16,768]{1,0:T(8,128)(2,1)S(1)}, bf16[16,768]{1,0:T(8,128)(2,1)S(1)}, u32[]{:S(2)}, u32[]{:S(2)}) collective-permute-start(bf16[16,768]{1,0:T(8,128)(2,1)S(1)} %slice.202), channel_id=1, source_target_pairs={{0,16},{8,24},{16,0},{24,8},{1,17},{9,25},{17,1},{25,9},{2,18},{10... | collective-permute-start | bytes 73736 | tf_op jit(solution)/shard_map/ppermute | solution.py:631
  334.2 6.3 %collective-permute-start.16 = (bf16[16,768]{1,0:T(8,128)(2,1)S(1)}, bf16[16,768]{1,0:T(8,128)(2,1)S(1)}, u32[]{:S(2)}, u32[]{:S(2)}) collective-permute-start(bf16[16,768]{1,0:T(8,128)(2,1)S(1)} %slice.202), channel_id=1, source_target_pairs={{0,24},{8,16},{16,8},{24,0},{1,25},{9,17},{17,9},{25,1},{2,26},{10... | collective-permute-start | bytes 73736 | tf_op jit(solution)/shard_map/ppermute | solution.py:631
  338.2 5.4 %copy-start.1 = (bf16[96,3072]{1,0:T(8,128)(2,1)S(1)}, bf16[96,3072]{1,0:T(8,128)(2,1)}, u32[]{:S(2)}) copy-start(bf16[96,3072]{1,0:T(8,128)(2,1)} %param.25) | copy-start | bytes 1769476
  (8 other events, 14.2 us)
Sparse Core Ops, SparseCore 0:
  10.2 31.9 all-gather.11
  44.4 53.6 all-gather.9
  99.7 49.9 all-gather.7
  165.4 52.4 reduce-scatter.3
  235.2 41.0 reduce-scatter.5
  278.4 42.2 reduce-scatter.7
